TPU v7x, 32 devices: a whole 2x2x4 slice. The times are simulated.
32 devices in a mesh: group: 4 (over y, x), dp: 8 (over z, core).
Axes of the slice: x: 2, y: 2, z: 4, core: 2. Of those that a mesh axis runs over, the one named last changes fastest.
Arguments:
- tokens: bfloat16 [128, 320, 1024], P(('group', 'dp')), may hold values from -16 to 16
- keep: int32 [128, 256], P(('group', 'dp')), may hold values from 0 to 1, as said below
- cotangent: bfloat16 [128, 320, 1024], P(('group', 'dp')), may hold values from -6 to 6
- master_matrices: float32 [1024, 8192], P('group'), may hold values from -0.5 to 0.5
- master_down: float32 [4096, 1024], P('group'), may hold values from -0.09375 to 0.09375
- master_vectors: float32 [12, 1024], P(None, 'group'), may hold values from -1 to 2
- first_matrices: float32 [1024, 8192], P('group'), may hold values from -274.230852 to 274.230852
- first_down: float32 [4096, 1024], P('group'), may hold values from -228.52571 to 228.52571
- first_vectors: float32 [12, 1024], P(None, 'group'), may hold values from -457.05142 to 457.05142
- second_matrices: float32 [1024, 8192], P('group'), may hold values from 146.88 to 18800.64
- second_down: float32 [4096, 1024], P('group'), may hold values from 1632 to 13056
- second_vectors: float32 [12, 1024], P(None, 'group'), may hold values from 6528 to 52224
Outputs:
- block_output: bfloat16 [128, 320, 1024], P(('group', 'dp'))
- input_grad: float32 [128, 320, 1024], P(('group', 'dp'))
- new_matrices: float32 [1024, 8192], P('group')
- new_down: float32 [4096, 1024], P('group')
- new_vectors: float32 [12, 1024], P(None, 'group')
- new_first_matrices: float32 [1024, 8192], P('group')
- new_first_down: float32 [4096, 1024], P('group')
- new_first_vectors: float32 [12, 1024], P(None, 'group')
- new_second_matrices: float32 [1024, 8192], P('group')
- new_second_down: float32 [4096, 1024], P('group')
- new_second_vectors: float32 [12, 1024], P(None, 'group')
- copy_matrices: bfloat16 [1024, 8192], P('group')
- copy_down: bfloat16 [4096, 1024], P('group')
- copy_vectors: bfloat16 [12, 1024], P(None, 'group')
- branch_rms: float32 [3], replicated
Inputs may be any that keep to these rules, and one draw needn't show every extreme that they name: `keep`: each row keeps between 0 and 77 of its image tokens; some row keeps none and some keeps exactly 77.
All inputs are finite; a program needn't handle non-finite values.
Results may differ from a plain program's by a relative error of at most 0.009.
The roundings to bfloat16 on the way count: a program that leaves them out, or rounds other values in their place, can miss the bound.
Values may be sent and summed in bfloat16 or wider, within the bound.
A program may use at most 384 MiB of HBM per device.

v0:
```python
import math

import jax
import jax.numpy as jnp
from jax import lax
from jax.sharding import PartitionSpec as P

HEADS = 16
HEAD = 64
STEP = 7


norm_epsilon = 1e-06
beta_first = 0.5
beta_second = 0.5
adam_epsilon = 1e-08
rate_matrix = 0.05
rate_vector = 0.3
weight_decay = 0.05
root_half = 0.7071067811865476
inverse_root_two_pi = 0.3989422804014327


def layer_stats(values):
    centre = jnp.mean(values, axis=-1, keepdims=True)
    centred = values - centre
    variance = jnp.mean(centred * centred, axis=-1, keepdims=True)
    inverse = lax.rsqrt(variance + norm_epsilon)
    return (centred * inverse, inverse)


def norm_back(grad_normed, normal, inverse, gain):
    scaled = grad_normed * gain
    mean_one = jnp.mean(scaled, axis=-1, keepdims=True)
    mean_two = jnp.mean(scaled * normal, axis=-1, keepdims=True)
    return inverse * (scaled - mean_one - normal * mean_two)


def gelu_value(values):
    return 0.5 * values * (1.0 + lax.erf(values * root_half))


def gelu_slope(values):
    cumulative = 0.5 * (1.0 + lax.erf(values * root_half))
    return cumulative + values * jnp.exp(-0.5 * values * values) * inverse_root_two_pi


def adam_step(master, first, second, grad, rate, decay):
    first_new = beta_first * first + (1.0 - beta_first) * grad
    second_new = beta_second * second + (1.0 - beta_second) * grad * grad
    fix_first = 1.0 - beta_first**STEP
    fix_second = 1.0 - beta_second**STEP
    update = first_new / fix_first / (jnp.sqrt(second_new / fix_second) + adam_epsilon)
    return (master - rate * (update + decay * master), first_new, second_new)


def local(
    tokens,
    keep,
    cotangent,
    master_matrices,
    master_down,
    master_vectors,
    first_matrices,
    first_down,
    first_vectors,
    second_matrices,
    second_down,
    second_vectors,
):
    seq_count, length, features = tokens.shape
    row_count = seq_count * length
    image_len = keep.shape[1]
    head_shape = (seq_count, length, HEADS, HEAD)
    attn_cols = 4 * features
    score_scale = 1.0 / math.sqrt(HEAD)
    slots = jnp.concatenate(
        [jnp.ones((seq_count, length - image_len), jnp.float32), keep.astype(jnp.float32)], axis=1
    )
    slot_mask = slots.reshape(row_count, 1)
    key_valid = slots[:, None, None, :] > 0.5
    low_matrices = master_matrices.astype(jnp.bfloat16)
    attn_parts, vector_low = (
        lax.all_gather(low_matrices[:, :attn_cols], "group", axis=0, tiled=True),
        lax.all_gather(master_vectors.astype(jnp.bfloat16), "group", axis=1, tiled=True),
    )
    up_weight, down_weight = (
        lax.all_gather(low_matrices[:, attn_cols:], "group", axis=0, tiled=True),
        lax.all_gather(master_down.astype(jnp.bfloat16), "group", axis=0, tiled=True),
    )
    vector_rows = vector_low.astype(jnp.float32)
    w_qkv = attn_parts[:, : 3 * features]
    w_out = attn_parts[:, 3 * features :]
    inputs = tokens.astype(jnp.float32).reshape(row_count, features)
    normal_one, inverse_one = layer_stats(inputs)
    normed_one = (normal_one * vector_rows[0] + vector_rows[1]).astype(jnp.bfloat16)
    qkv_all = jnp.dot(normed_one, w_qkv, preferred_element_type=jnp.float32)
    query_heads = (qkv_all[:, :features] + vector_rows[2]).astype(jnp.bfloat16).reshape(head_shape)
    key_heads = qkv_all[:, features : 2 * features].astype(jnp.bfloat16).reshape(head_shape)
    value_heads = (
        (qkv_all[:, 2 * features :] + vector_rows[3]).astype(jnp.bfloat16).reshape(head_shape)
    )

    def scores_of(query_part, key_part):
        raw = (
            jnp.einsum("sqhd,skhd->shqk", query_part, key_part, preferred_element_type=jnp.float32)
            * score_scale
        )
        return jnp.where(key_valid, raw, -1e30)

    scores = scores_of(query_heads, key_heads)
    row_max = jnp.max(scores, axis=-1, keepdims=True)
    exponent = jnp.exp(scores - row_max)
    row_total = jnp.sum(exponent, axis=-1, keepdims=True)
    log_total = row_max + jnp.log(row_total)
    probs_low = (exponent / row_total).astype(jnp.bfloat16)
    attended = jnp.einsum(
        "shqk,skhd->sqhd", probs_low, value_heads, preferred_element_type=jnp.float32
    )
    attended = attended.reshape(row_count, features).astype(jnp.bfloat16)
    branch = jnp.dot(attended, w_out, preferred_element_type=jnp.float32) + vector_rows[4]
    resid = inputs + branch
    normal_two, inverse_two = layer_stats(resid)
    normed_two = (normal_two * vector_rows[5] + vector_rows[6]).astype(jnp.bfloat16)
    up_value = jnp.dot(normed_two, up_weight, preferred_element_type=jnp.float32) + vector_rows[
        8:12
    ].reshape(-1)
    activated = gelu_value(up_value).astype(jnp.bfloat16)
    mlp_out = jnp.dot(activated, down_weight, preferred_element_type=jnp.float32) + vector_rows[7]
    block_output = (
        ((resid + mlp_out) * slot_mask).reshape(seq_count, length, features).astype(jnp.bfloat16)
    )
    local_squares = jnp.stack(
        [
            jnp.sum(inputs * inputs * slot_mask),
            jnp.sum(branch * branch * slot_mask),
            jnp.sum(mlp_out * mlp_out * slot_mask),
        ]
    )
    square_sums, count_kept = lax.psum((local_squares, jnp.sum(slots)), ("group", "dp"))
    branch_rms = jnp.sqrt(square_sums / (count_kept * features))
    grad_out = cotangent.astype(jnp.float32).reshape(row_count, features) * slot_mask
    grad_mlp = grad_out.astype(jnp.bfloat16)
    grad_down_bias = jnp.sum(grad_mlp.astype(jnp.float32), axis=0)
    grad_down = jnp.einsum("nf,nd->fd", activated, grad_mlp, preferred_element_type=jnp.float32)
    grad_active = jnp.einsum("nd,fd->nf", grad_mlp, down_weight, preferred_element_type=jnp.float32)
    grad_upper = (grad_active * gelu_slope(up_value)).astype(jnp.bfloat16)
    grad_up_bias = jnp.sum(grad_upper.astype(jnp.float32), axis=0)
    grad_up = jnp.einsum("nd,nf->df", normed_two, grad_upper, preferred_element_type=jnp.float32)
    grad_normed_two = jnp.einsum(
        "nf,df->nd", grad_upper, up_weight, preferred_element_type=jnp.float32
    )
    grad_gain_two = jnp.sum(grad_normed_two * normal_two, axis=0)
    grad_shift_two = jnp.sum(grad_normed_two, axis=0)
    grad_resid = grad_out + norm_back(grad_normed_two, normal_two, inverse_two, vector_rows[5])
    part_up, part_down = (
        lax.psum_scatter(grad_up, "group", scatter_dimension=0, tiled=True),
        lax.psum_scatter(grad_down, "group", scatter_dimension=0, tiled=True),
    )
    grad_branch = grad_resid.astype(jnp.bfloat16)
    grad_out_bias = jnp.sum(grad_branch.astype(jnp.float32), axis=0)
    grad_wout = jnp.einsum("nd,ne->de", attended, grad_branch, preferred_element_type=jnp.float32)
    grad_attended = jnp.einsum("ne,de->nd", grad_branch, w_out, preferred_element_type=jnp.float32)
    grad_attended = grad_attended.astype(jnp.bfloat16).reshape(head_shape)
    recomputed = jnp.exp(scores_of(query_heads, key_heads) - log_total)
    grad_value = jnp.einsum(
        "shqk,sqhd->skhd", probs_low, grad_attended, preferred_element_type=jnp.float32
    ).astype(jnp.bfloat16)
    grad_probs = jnp.einsum(
        "sqhd,skhd->shqk", grad_attended, value_heads, preferred_element_type=jnp.float32
    )
    inner_sum = jnp.sum(recomputed * grad_probs, axis=-1, keepdims=True)
    grad_scores = (recomputed * (grad_probs - inner_sum)).astype(jnp.bfloat16)
    grad_query = (
        jnp.einsum("shqk,skhd->sqhd", grad_scores, key_heads, preferred_element_type=jnp.float32)
        * score_scale
    ).astype(jnp.bfloat16)
    grad_key = (
        jnp.einsum("shqk,sqhd->skhd", grad_scores, query_heads, preferred_element_type=jnp.float32)
        * score_scale
    ).astype(jnp.bfloat16)
    grad_qkv = jnp.concatenate(
        [
            grad_query.reshape(row_count, features),
            grad_key.reshape(row_count, features),
            grad_value.reshape(row_count, features),
        ],
        axis=1,
    )
    grad_query_bias = jnp.sum(grad_query.reshape(row_count, features).astype(jnp.float32), axis=0)
    grad_value_bias = jnp.sum(grad_value.reshape(row_count, features).astype(jnp.float32), axis=0)
    grad_wqkv = jnp.einsum("nd,ne->de", normed_one, grad_qkv, preferred_element_type=jnp.float32)
    grad_normed_one = jnp.einsum("ne,de->nd", grad_qkv, w_qkv, preferred_element_type=jnp.float32)
    grad_gain_one = jnp.sum(grad_normed_one * normal_one, axis=0)
    grad_shift_one = jnp.sum(grad_normed_one, axis=0)
    input_grad = (
        grad_resid + norm_back(grad_normed_one, normal_one, inverse_one, vector_rows[0])
    ).reshape(seq_count, length, features)
    vector_grads = jnp.concatenate(
        [
            jnp.stack(
                [
                    grad_gain_one,
                    grad_shift_one,
                    grad_query_bias,
                    grad_value_bias,
                    grad_out_bias,
                    grad_gain_two,
                    grad_shift_two,
                    grad_down_bias,
                ]
            ),
            grad_up_bias.reshape(4, features),
        ],
        axis=0,
    )
    attn_grads = jnp.concatenate([grad_wqkv, grad_wout], axis=1)
    part_attn, part_vectors = (
        lax.psum_scatter(attn_grads, "group", scatter_dimension=0, tiled=True),
        lax.psum_scatter(vector_grads, "group", scatter_dimension=1, tiled=True),
    )
    part_attn, part_up, part_down, part_vectors = lax.psum(
        (part_attn, part_up, part_down, part_vectors), "dp"
    )
    grad_matrices = jnp.concatenate([part_attn, part_up], axis=1)
    new_matrices, new_first_matrices, new_second_matrices = adam_step(
        master_matrices, first_matrices, second_matrices, grad_matrices, rate_matrix, weight_decay
    )
    new_down, new_first_down, new_second_down = adam_step(
        master_down, first_down, second_down, part_down, rate_matrix, weight_decay
    )
    new_vectors, new_first_vectors, new_second_vectors = adam_step(
        master_vectors, first_vectors, second_vectors, part_vectors, rate_vector, 0.0
    )
    return (
        block_output,
        input_grad,
        new_matrices,
        new_down,
        new_vectors,
        new_first_matrices,
        new_first_down,
        new_first_vectors,
        new_second_matrices,
        new_second_down,
        new_second_vectors,
        new_matrices.astype(jnp.bfloat16),
        new_down.astype(jnp.bfloat16),
        new_vectors.astype(jnp.bfloat16),
        branch_rms,
    )


def solution(mesh):
    placed = (
        P(("group", "dp"), None, None),
        P(("group", "dp"), None),
        P(("group", "dp"), None, None),
        P("group", None),
        P("group", None),
        P(None, "group"),
        P("group", None),
        P("group", None),
        P(None, "group"),
        P("group", None),
        P("group", None),
        P(None, "group"),
    )
    return jax.shard_map(
        local,
        mesh=mesh,
        in_specs=placed,
        out_specs=(
            P(("group", "dp"), None, None),
            P(("group", "dp"), None, None),
            P("group", None),
            P("group", None),
            P(None, "group"),
            P("group", None),
            P("group", None),
            P(None, "group"),
            P("group", None),
            P("group", None),
            P(None, "group"),
            P("group", None),
            P("group", None),
            P(None, "group"),
            P(),
        ),
        check_vma=False,
    )
```

profile of v0, /device:TPU:0, one launch (start us, length us, event | category | flops | bytes accessed | tf_op | source)
XLA Modules:
  0.0 1124.5 jit_solution(2824634297581670505)
XLA Ops:
  19.1 4.4 fusion.18
  24.5 10.3 all_gather.12
  41.5 62.6 %all-gather.4.cloned.1.call-done = bf16[1024,4096]{1,0:T(8,128)(2,1)} async-done(((bf16[256,4096]{1,0:T(8,128)(2,1)}), bf16[1024,4096]{1,0:T(8,128)(2,1)}) %all-gather.4.cloned.1.call-update) | async-done | bytes 8388624 | tf_op jit(solution)/shard_map/all_gather | solution.py:84
  104.1 11.3 %fusion.11 = f32[1280,3072]{1,0:T(8,128)S(1)} fusion(bf16[1280,1024]{1,0:T(8,128)(2,1)} %fusion.25, bf16[1024,4096]{1,0:T(8,128)(2,1)} %all-gather.4.cloned.1.call-done), kind=kOutput, calls=%fused_computation.31 | convolution fusion | flops 8053063680 | bytes 24641536 | tf_op jit(solution)/shard_map/dot_general | solution.py:97
  121.4 7.7 reshape.171
  129.1 7.8 copy.43
  136.9 7.7 reshape.172
  144.7 8.1 copy.44
  152.8 16.6 %fusion.7 = (f32[4,16,320]{2,1,0:T(8,128)S(1)}, f32[4,16,320,320]{2,3,1,0:T(8,128)}) fusion(pred[4,320]{1,0:T(4,128)(4,1)S(1)} %broadcast_compare_fusion, bf16[4,320,16,64]{1,3,2,0:T(8,128)(2,1)} %copy.43, bf16[4,320,16,64]{1,3,2,0:T(8,128)(2,1)} %copy.44), kind=kOutput, calls=%fused_computation.18 | convolution fusion | flops 858501120 | bytes 31540480 | tf_op jit(solution)/shard_map/sqhd,skhd->shqk/dot_general | solution.py:106
  169.4 7.8 reshape.170
  177.1 7.8 copy.45
  185.0 14.7 %fusion = f32[4,16,320]{2,1,0:T(8,128)S(1)} fusion(f32[4,16,320,320]{2,3,1,0:T(8,128)} %get-tuple-element.67, f32[4,16,320]{2,1,0:T(8,128)S(1)} %get-tuple-element.66, pred[4,320]{1,0:T(4,128)(4,1)S(1)} %broadcast_compare_fusion), kind=kLoop, calls=%fused_computation.7 | loop fusion | flops 26193920 | bytes 26379520 | tf_op jit(solution)/shard_map/reduce_sum | solution.py:114
  199.7 5.1 copy-done
  204.8 10.4 divide_convert_fusion
  215.3 8.4 convert_bitcast_fusion.1
  228.0 6.2 convert_element_type.129
  234.2 8.2 fusion.50
  245.4 21.3 %multiply_convert_fusion.1 = (bf16[1280,4096]{1,0:T(8,128)(2,1)}, f32[1280,4096]{1,0:T(8,128)}) fusion(f32[4096]{0:T(1024)S(1)} %bitcast.112, bf16[1024,4096]{1,0:T(8,128)(2,1)} %all-gather.6.cloned.1.call-done, f32[1280,1024]{1,0:T(8,128)} %copy-done.10, f32[1024]{0:T(1024)S(1)} %bitcast.125, f32[1024]{0:T(1024)S(1)} %bitcast.116, ...), kind=kOutput, calls=%fused_computation.15 | convolution fusion | flops 10775429120 | bytes 45123584 | tf_op jit(solution)/shard_map/dot_general | solution.py:125
  266.7 17.0 %all-gather.8.cloned.1.call-done = bf16[4096,1024]{1,0:T(8,128)(2,1)} async-done(((bf16[1024,1024]{1,0:T(8,128)(2,1)}), bf16[4096,1024]{1,0:T(8,128)(2,1)}) %all-gather.8.cloned.1.call-update) | async-done | bytes 8388624 | tf_op jit(solution)/shard_map/all_gather | solution.py:89
  283.7 22.4 %convert_reduce_fusion = (f32[4096]{0:T(1024)}, bf16[1280,4096]{1,0:T(8,128)(2,1)S(1)}) fusion(f32[1280,4096]{1,0:T(8,128)} %get-tuple-element.70, f32[4096]{0:T(1024)S(1)} %bitcast.113, bf16[1280,1024]{1,0:T(8,128)(2,1)S(1)} %copy-done.17, bf16[4096,1024]{1,0:T(8,128)(2,1)} %all-gather.8.cloned.1.call-done), kind=kOutput, calls=%fused_computation.14 | convolution fusion | flops 10805571584 | bytes 42500096 | tf_op jit(solution)/shard_map/nd,fd->nf/dot_general | solution.py:146
  309.9 15.1 %fusion.42 = f32[1024,4096]{1,0:T(8,128)} fusion(bf16[1280,4096]{1,0:T(8,128)(2,1)S(1)} %get-tuple-element.80, f32[1280,1024]{1,0:T(8,128)S(1)} %copy-done.11, f32[1024]{0:T(1024)S(1)} %bitcast.126, f32[1024]{0:T(1024)S(1)} %bitcast.117, f32[1280]{0:T(1024)S(1)} %add_rsqrt_fusion, f32[1280]{0:T(1024)S(1)} %broadcast_multiply_fusion.4), kind=kOutput, calls=%fused_computation.112 | convolution fusion | flops 10743971840 | bytes 32524288 | tf_op jit(solution)/shard_map/nd,nf->df/dot_general | solution.py:149
  325.1 17.1 %fusion.54 = f32[4096,1024]{1,0:T(8,128)} fusion(bf16[1280,4096]{1,0:T(8,128)(2,1)} %get-tuple-element.69, bf16[1280,1024]{1,0:T(8,128)(2,1)S(1)} %copy-done.17), kind=kOutput, calls=%fused_computation.121 | convolution fusion | flops 10737418240 | bytes 29884416 | tf_op jit(solution)/shard_map/nf,nd->fd/dot_general | solution.py:145
  342.2 21.1 %multiply_reduce_fusion.3 = (f32[1024]{0:T(1024)}, f32[1280]{0:T(1024)S(1)}, f32[1280]{0:T(1024)S(1)}, f32[1024]{0:T(1024)}, f32[1280,1024]{1,0:T(8,128)}) fusion(f32[1280,1024]{1,0:T(8,128)} %copy-done.10, f32[1280]{0:T(1024)S(1)} %add_rsqrt_fusion, f32[1280]{0:T(1024)S(1)} %broadcast_multiply_fusion.4, f32[1024]{0:T(1024)S(1)} %bitcast.118, ...), kind=kOutput, calls=%fused_computation.64 | convolution fusion | flops 10749210624 | bytes 29392896 | tf_op jit(solution)/shard_map/nf,df->nd/dot_general | solution.py:150
  363.4 24.4 %multiply_reduce_fusion.2 = (f32[]{:T(128)}, f32[]{:T(128)}, bf16[1280,1024]{1,0:T(8,128)(2,1)}, f32[1024]{0:T(1024)}, f32[1280,1024]{1,0:T(8,128)}) fusion(f32[1280,1024]{1,0:T(8,128)} %get-tuple-element.68, f32[1280]{0:T(1024)S(1)} %copy-done.34, f32[1024]{0:T(1024)S(1)} %bitcast.121, f32[1024]{0:T(1024)S(1)} %bitcast.115, f32[1280,1024]{1,0:T(8,128)} %copy-done.10, ...), kind=kOutput, calls=%fused_computation.61 | convolution fusion | flops 10768874496 | bytes 45130760 | tf_op jit(solution)/shard_map/dot_general | solution.py:129
  387.8 6.3 convolution_convert_fusion
  394.1 4.9 reshape.173
  399.0 7.1 copy.49
  406.1 8.7 convert_reduce_fusion.1
  419.1 6.2 reshape.167
  425.3 29.7 %multiply_reduce_fusion = (f32[4,16,320]{2,1,0:T(8,128)S(1)}, f32[4,16,320,320]{2,3,1,0:T(8,128)}) fusion(f32[4,16,320,320]{2,3,1,0:T(8,128)} %get-tuple-element.67, f32[4,16,320]{2,1,0:T(8,128)S(1)} %log_add_fusion, pred[4,320]{1,0:T(4,128)(4,1)S(1)} %copy-done.24, bf16[4,320,16,64]{1,3,2,0:T(8,128)(2,1)S(1)} %copy.49, bf16[4,320,16,64]{1,3,2,0:T(8,128)(2,1)} %copy.45), kind=kOutput, calls=%fused_computation.1 | convolution fusion | flops 871608320 | bytes 57836800 | tf_op jit(solution)/shard_map/sqhd,skhd->shqk/dot_general | solution.py:169
  455.1 27.7 %multiply_convert_fusion = bf16[4,16,320,320]{2,3,1,0:T(8,128)(2,1)} fusion(f32[4,16,320,320]{2,3,1,0:T(8,128)} %get-tuple-element.73, f32[4,16,320,320]{2,3,1,0:T(8,128)} %get-tuple-element.67, f32[4,16,320]{2,1,0:T(8,128)S(1)} %get-tuple-element.72, f32[4,16,320]{2,1,0:T(8,128)S(1)} %log_add_fusion, pred[4,320]{1,0:T(4,128)(4,1)S(1)} %copy-done.24), kind=kLoop, calls=%fused_computation | loop fusion | flops 39321600 | bytes 65701120 | tf_op jit(solution)/shard_map/convert_element_type | solution.py:173
  482.7 8.3 fusion.34
  491.1 4.3 copy.56
  495.3 6.6 reshape.166
  502.0 9.1 convert_reduce_fusion.2
  529.2 10.9 fusion.53
  540.1 6.2 pad_maximum_fusion
  548.1 15.8 %fusion.30 = (f32[1024]{0:T(1024)S(1)}, f32[1280]{0:T(1024)S(1)}, f32[1280]{0:T(1024)S(1)}, f32[1024]{0:T(1024)S(1)}, f32[1280,1024]{1,0:T(8,128)}) fusion(bf16[4,320,1024]{2,1,0:T(8,128)(2,1)S(1)} %copy-done.2, f32[1280]{0:T(1024)S(1)} %copy-done.28, f32[1280]{0:T(1024)S(1)} %copy-done.26, f32[1024]{0:T(1024)S(1)} %bitcast.107, ...), kind=kOutput, calls=%fused_computation.59 | convolution fusion | flops 8066166784 | bytes 22052864 | tf_op jit(solution)/shard_map/ne,de->nd/dot_general | solution.py:193
  565.3 70.5 %reduce-scatter.9.cloned.1.call-done = f32[1024,1024]{1,0:T(8,128)} async-done(((f32[4096,1024]{1,0:T(8,128)}), f32[1024,1024]{1,0:T(8,128)}) %reduce-scatter.9.cloned.1.call-update) | async-done | bytes 4194320 | tf_op jit(solution)/shard_map/reduce_scatter | solution.py:158
  635.8 156.8 %reduce-scatter.5.cloned.1.call-done = f32[256,4096]{1,0:T(8,128)} async-done(((f32[1024,4096]{1,0:T(8,128)}), f32[256,4096]{1,0:T(8,128)}) %reduce-scatter.5.cloned.1.call-update) | async-done | bytes 4194320 | tf_op jit(solution)/shard_map/reduce_scatter | solution.py:219
  794.7 39.6 %all-reduce.1 = (f32[3]{0:T(128)S(1)}, f32[]{:T(128)}) all-reduce(f32[3]{0:T(128)S(1)} %pad_maximum_fusion.1, f32[]{:T(128)} %get-tuple-element.64), channel_id=1, replica_groups=mesh['group'=4,'dp'=8] {'group','dp'}, use_global_device_ids=true, to_apply=%region_31.32 | all-reduce | flops 4 | bytes 32 | tf_op jit(solution)/shard_map/psum | solution.py:140
  835.5 6.5 fusion.29
  842.0 29.9 %psum.45 = f32[12,256]{1,0:T(8,128)S(1)} all-reduce(f32[12,256]{1,0:T(8,128)} %reduce-scatter.11.cloned.1.call-done), channel_id=1, replica_groups=mesh['group'=4,'dp'=8] {'dp'}, use_global_device_ids=true, to_apply=%region_27.28 | all-reduce | flops 3072 | bytes 24576 | tf_op jit(solution)/shard_map/psum | solution.py:222
  872.6 205.8 %all-reduce.5.cloned.1.call-done = (f32[256,4096]{1,0:T(8,128)}, f32[256,4096]{1,0:T(8,128)}, f32[1024,1024]{1,0:T(8,128)}) async-done(((f32[256,4096]{1,0:T(8,128)}, f32[256,4096]{1,0:T(8,128)}, f32[1024,1024]{1,0:T(8,128)}), (f32[256,4096]{1,0:T(8,128)}, f32[256,4096]{1,0:T(8,128)}, f32[1024,1024]{1,0:T(8,128)})) %all-reduce.5.cloned.1.call-update) | async-done | bytes 12582928 | tf_op jit(solution)/shard_map/psum | solution.py:222
  1078.3 4.9 constant_dynamic-update-slice_fusion.4
  1083.3 5.1 constant_dynamic-update-slice_fusion.3
  1089.9 6.4 fusion.46
  1096.4 21.1 %fusion.48 = (bf16[256,8192]{1,0:T(8,128)(2,1)}, f32[256,8192]{1,0:T(8,128)}, f32[256,8192]{1,0:T(8,128)}, f32[256,8192]{1,0:T(8,128)}) fusion(f32[256,8192]{1,0:T(8,128)} %param.15, f32[256,8192]{1,0:T(8,128)} %constant_dynamic-update-slice_fusion.3, f32[256,8192]{1,0:T(8,128)} %param.18, f32[256,8192]{1,0:T(8,128)} %param.21), kind=kLoop, calls=%fused_computation.116 | loop fusion | flops 31457280 | bytes 62914560 | tf_op jit(solution)/shard_map/convert_element_type | solution.py:247
  (156 shorter events, 67.2 us)
Async XLA Ops:
  7.2 96.9 %all-gather.4.cloned.1.call-start = ((), (), s32[]{:S(2)}) async-start(), calls=%async_computation.4 | async-start | bytes 10485760 | tf_op jit(solution)/shard_map/all_gather | solution.py:84
  13.5 231.9 %all-gather.6.cloned.1.call-start = ((), (), s32[]{:S(2)}) async-start(), calls=%async_computation.5 | async-start | bytes 10485760 | tf_op jit(solution)/shard_map/all_gather | solution.py:88
  13.5 4.8 copy-start.43
  13.5 5.6 copy-start.1
  14.2 269.5 %all-gather.8.cloned.1.call-start = ((), (), s32[]{:S(2)}) async-start(), calls=%async_computation.6 | async-start | bytes 10485760 | tf_op jit(solution)/shard_map/all_gather | solution.py:89
  18.2 6.2 copy-start.29
  18.2 547.0 %reduce-scatter.7.cloned.1.call-start = ((), (), s32[]{:S(2)}) async-start(), calls=%async_computation.8 | async-start | bytes 20971520 | tf_op jit(solution)/shard_map/reduce_scatter | solution.py:157
  18.4 181.3 %copy-start.23 = (pred[4,320]{1,0:T(4,128)(4,1)}, pred[4,320]{1,0:T(4,128)(4,1)S(1)}, u32[]{:S(2)}) copy-start(pred[4,320]{1,0:T(4,128)(4,1)S(1)} %broadcast_compare_fusion) | copy-start | bytes 3844
  19.1 20.1 %copy-start.33 = (f32[1280]{0:T(1024)}, f32[1280]{0:T(1024)S(1)}, u32[]{:S(2)}) copy-start(f32[1280]{0:T(1024)S(1)} %mul.279) | copy-start | bytes 15364
  24.4 17.1 %copy-start.25 = (f32[1280]{0:T(1024)}, f32[1280]{0:T(1024)S(1)}, u32[]{:S(2)}) copy-start(f32[1280]{0:T(1024)S(1)} %div.68) | copy-start | bytes 15364
  35.4 6.1 copy-start.31
  35.5 6.0 copy-start.27
  169.4 30.3 %copy-start.18 = (f32[4,16,320]{2,1,0:T(8,128)}, f32[4,16,320]{2,1,0:T(8,128)S(1)}, u32[]{:S(2)}) copy-start(f32[4,16,320]{2,1,0:T(8,128)S(1)} %get-tuple-element.66) | copy-start | bytes 245764
  185.0 19.9 %copy-start = (f32[4,16,320,320]{2,3,1,0:T(8,128)S(1)}, f32[4,16,320,320]{2,3,1,0:T(8,128)}, u32[]{:S(2)}) copy-start(f32[4,16,320,320]{2,3,1,0:T(8,128)} %get-tuple-element.67) | copy-start | bytes 78643200
  204.8 10.5 copy-start.20
  204.8 10.5 copy-start.3
  245.4 38.3 %copy-start.17 = (bf16[1280,1024]{1,0:T(8,128)(2,1)S(1)}, bf16[1280,1024]{1,0:T(8,128)(2,1)}, u32[]{:S(2)}) copy-start(bf16[1280,1024]{1,0:T(8,128)(2,1)} %fusion.31) | copy-start | bytes 7864324
  283.7 26.2 %copy-start.11 = (f32[1280,1024]{1,0:T(8,128)S(1)}, f32[1280,1024]{1,0:T(8,128)}, u32[]{:S(2)}) copy-start(f32[1280,1024]{1,0:T(8,128)} %copy-done.10) | copy-start | bytes 15728644
  306.1 3.8 copy-start.44
  325.0 310.7 %reduce-scatter.9.cloned.1.call-start = ((), (), s32[]{:S(2)}) async-start(), calls=%async_computation.9 | async-start | bytes 20971520 | tf_op jit(solution)/shard_map/reduce_scatter | solution.py:158
  342.2 21.2 %copy-start.7 = (bf16[4,320,1024]{2,1,0:T(8,128)(2,1)S(1)}, bf16[4,320,1024]{2,1,0:T(8,128)(2,1)}, u32[]{:S(2)}) copy-start(bf16[4,320,1024]{2,1,0:T(8,128)(2,1)} %param.14) | copy-start | bytes 7864324
  342.2 21.2 %copy-start.34 = (f32[1280]{0:T(1024)S(1)}, f32[1280]{0:T(1024)}, u32[]{:S(2)}) copy-start(f32[1280]{0:T(1024)} %copy-done.33) | copy-start | bytes 15364
  342.2 21.2 %copy-start.39 = (f32[1,1024]{1,0:T(1,128)S(1)}, f32[1,1024]{1,0:T(1,128)}, u32[]{:S(2)}) copy-start(f32[1,1024]{1,0:T(1,128)} %get-tuple-element.56) | copy-start | bytes 12292
  342.2 450.4 %reduce-scatter.5.cloned.1.call-start = ((), (), s32[]{:S(2)}) async-start(), calls=%async_computation.7 | async-start | bytes 20971520 | tf_op jit(solution)/shard_map/reduce_scatter | solution.py:219
  414.8 10.5 copy-start.19
  414.8 10.5 copy-start.21
  414.8 10.5 copy-start.24
  455.1 27.7 %copy-start.5 = (bf16[4,320,16,64]{1,3,2,0:T(8,128)(2,1)S(1)}, bf16[4,320,16,64]{1,3,2,0:T(8,128)(2,1)}, u32[]{:S(2)}) copy-start(bf16[4,320,16,64]{1,3,2,0:T(8,128)(2,1)} %copy.43) | copy-start | bytes 7864324
  491.1 10.9 copy-start.4
  517.3 3.5 copy-start.8
  517.3 7.7 slice-start
  519.9 5.1 slice-start.1
  519.9 6.5 copy-start.16
  520.9 4.1 copy-start.22
  526.3 2.9 copy-start.15
  546.3 295.7 %reduce-scatter.11.cloned.1.call-start = ((), (), s32[]{:S(2)}) async-start(), calls=%async_computation.10 | async-start | bytes 81920 | tf_op jit(solution)/shard_map/reduce_scatter | solution.py:220
  548.0 15.8 %copy-start.38 = (f32[1024]{0:T(1024)S(1)}, f32[1024]{0:T(1024)}, u32[]{:S(2)}) copy-start(f32[1024]{0:T(1024)} %get-tuple-element.27) | copy-start | bytes 12292
  548.0 15.8 %copy-start.40 = (f32[1024]{0:T(1024)S(1)}, f32[1024]{0:T(1024)}, u32[]{:S(2)}) copy-start(f32[1024]{0:T(1024)} %get-tuple-element.15) | copy-start | bytes 12292
  548.0 15.8 %copy-start.41 = (f32[1024]{0:T(1024)S(1)}, f32[1024]{0:T(1024)}, u32[]{:S(2)}) copy-start(f32[1024]{0:T(1024)} %get-tuple-element.21) | copy-start | bytes 12292
  548.1 15.8 %copy-start.42 = (f32[1024]{0:T(1024)S(1)}, f32[1024]{0:T(1024)}, u32[]{:S(2)}) copy-start(f32[1024]{0:T(1024)} %get-tuple-element.52) | copy-start | bytes 12292
  565.2 513.2 %all-reduce.5.cloned.1.call-start = ((), (), s32[]{:S(2)}) async-start(), calls=%async_computation.11 | async-start | bytes 25165824 | tf_op jit(solution)/shard_map/psum | solution.py:222
  835.5 36.4 %copy-start.30 = (f32[12,256]{1,0:T(8,128)S(1)}, f32[12,256]{1,0:T(8,128)}, u32[]{:S(2)}) copy-start(f32[12,256]{1,0:T(8,128)} %param.17) | copy-start | bytes 36868
  835.5 36.4 %copy-start.35 = (f32[12,256]{1,0:T(8,128)S(1)}, f32[12,256]{1,0:T(8,128)}, u32[]{:S(2)}) copy-start(f32[12,256]{1,0:T(8,128)} %param.20) | copy-start | bytes 36868
  835.5 36.4 %copy-start.36 = (f32[12,256]{1,0:T(8,128)S(1)}, f32[12,256]{1,0:T(8,128)}, u32[]{:S(2)}) copy-start(f32[12,256]{1,0:T(8,128)} %param.23) | copy-start | bytes 36868
  1078.3 10.0 copy-start.13
  1078.3 10.0 copy-start.14
  1083.3 5.1 copy-start.6
  1083.3 6.7 copy-start.12
  (7 other events, 12.7 us)
Sparse Core Ops, SparseCore 0:
  13.6 90.4 all-gather.3
  106.5 87.5 all-gather.5
  196.0 87.6 all-gather.7
  325.2 153.7 reduce-scatter.6
  481.9 153.8 reduce-scatter.8
  638.7 153.8 reduce-scatter.4
  795.9 23.6 reduce-scatter.10
  822.3 255.9 all-reduce.4
where the time goes:
time: 1130 us; the launch traced here: 1120 us
  waiting for transfers between devices  513 us (45%)
  matrix products  258 us (23%)
  local copies, waits for them, and re-layouts  137 us (12%)
  other arithmetic  121 us (11%)
  blocking collectives  79.8 us (7%)
  between operations  15.5 us (1%)
    psum x1, waiting for transfers between devices, local(): lax.psum((part_attn, part_up, part_down, part_vectors), 'dp')  206 us
    reduce_scatter x1, waiting for transfers between devices, local(): lax.psum_scatter(attn_grads, 'group', scatter_dimension=0, tiled=True)  157 us
    reduce_scatter x1, waiting for transfers between devices, local(): lax.psum_scatter(grad_down, 'group', scatter_dimension=0, tiled=True)  70.5 us
    all_gather x1, waiting for transfers between devices, local(): lax.all_gather(low_matrices[:, :attn_cols], 'group', axis=0, tiled=True)  62.6 us
    psum x1, blocking collectives, local(): lax.psum((local_squares, jnp.sum(slots)), ('group', 'dp'))  39.6 us
    psum x1, blocking collectives, local(): lax.psum((part_attn, part_up, part_down, part_vectors), 'dp')  29.9 us
    dot_general x1, matrix products, local(): jnp.einsum('sqhd,skhd->shqk', grad_attended, value_heads, preferred_eleme...  29.7 us
    unnamed x99, local copies, waits for them, and re-layouts  28.4 us
  transfers between devices with their start and end apart: 8, of which 5 were waited for; matrix products, arithmetic and copies ran while one was open for 37% of the time, Pallas kernels for 0%

commit v1 on v0

v1 whole, which is shorter than its diff:
```python
import functools
import math

import jax
import jax.numpy as jnp
from jax import lax
from jax.experimental import pallas as pl
from jax.experimental.pallas import tpu as pltpu
from jax.sharding import PartitionSpec as P

HEAD = 64
STEP = 7
KEEP_MAX = 77

norm_epsilon = 1e-06
beta_first = 0.5
beta_second = 0.5
adam_epsilon = 1e-08
rate_matrix = 0.05
rate_vector = 0.3
weight_decay = 0.05
root_half = 0.7071067811865476
inverse_root_two_pi = 0.3989422804014327

bf16 = jnp.bfloat16
f32 = jnp.float32
BOTH = ("group", "dp")
VMEM_SPEC = pl.BlockSpec(memory_space=pltpu.VMEM)
SMEM_SPEC = pl.BlockSpec(memory_space=pltpu.SMEM)
ANY_SPEC = pl.BlockSpec(memory_space=pl.ANY)
MIB = 1 << 20


def mm(a, b):
    return jnp.dot(a, b, preferred_element_type=f32)


def mm_nt(a, b):
    return lax.dot_general(a, b, (((1,), (1,)), ((), ())), preferred_element_type=f32)


def mm_tn(a, b):
    return lax.dot_general(a, b, (((0,), (0,)), ((), ())), preferred_element_type=f32)


def sds(shape, dtype):
    return jax.ShapeDtypeStruct(shape, dtype)


def params(mib, **more):
    return pltpu.CompilerParams(vmem_limit_bytes=mib * MIB, **more)


def cost(flops, nbytes):
    return pl.CostEstimate(flops=int(flops), bytes_accessed=int(nbytes), transcendentals=0)


def layer_stats(values):
    centre = jnp.mean(values, axis=-1, keepdims=True)
    centred = values - centre
    variance = jnp.mean(centred * centred, axis=-1, keepdims=True)
    inverse = lax.rsqrt(variance + norm_epsilon)
    return centred * inverse, inverse


def norm_back(grad_normed, normal, inverse, gain):
    scaled = grad_normed * gain
    mean_one = jnp.mean(scaled, axis=-1, keepdims=True)
    mean_two = jnp.mean(scaled * normal, axis=-1, keepdims=True)
    return inverse * (scaled - mean_one - normal * mean_two)


def picker(keep_row, rows):
    image = keep_row.shape[1]
    ahead = lax.broadcasted_iota(jnp.int32, (image, image), 0)
    here = lax.broadcasted_iota(jnp.int32, (image, image), 1)
    upper = jnp.where(ahead <= here, 1.0, 0.0).astype(bf16)
    kept = keep_row.astype(f32)
    place = mm(kept.astype(bf16), upper) - 1.0
    place = jnp.where(kept > 0.5, place, -1.0)
    want = lax.broadcasted_iota(jnp.int32, (rows, image), 0).astype(f32)
    return jnp.where(place == want, 1.0, 0.0).astype(bf16)


def pack_kernel(buf, info, keep, tokens, cot, v0, v1, v2, v3, x_out, em_out, h_out, vec_out, vec):
    step = pl.program_id(0)
    part = v0.shape[1]

    @pl.when(step == 0)
    def _():
        for flip, piece in enumerate((v0, v1, v2, v3)):
            place = pl.multiple_of((info[0] ^ flip) * part, part)
            vec[0:12, pl.ds(place, part)] = piece[...].astype(f32)

    vec_out[...] = vec[...]
    rows = x_out.shape[0]
    pick = picker(keep[0], rows - buf)
    for src, dst in ((tokens, x_out), (cot, em_out)):
        dst[0:buf, :] = src[0, 0:buf, :]
        dst[buf:rows, :] = mm(pick, src[0, buf:, :]).astype(bf16)
    normal, _ = layer_stats(x_out[...].astype(f32))
    h_out[...] = (normal * vec[0:1, :] + vec[1:2, :]).astype(bf16)


def pieces_of(info, e):
    core = info[1] ^ e
    first = core + 1
    second = 3 - first
    group = info[0]
    return core, (group, group ^ first, group ^ second, group ^ 3)


def head_masks():
    lane = lax.broadcasted_iota(jnp.int32, (1, 2 * HEAD), 1)
    low = jnp.where(lane < HEAD, 1.0, 0.0)
    return low.astype(bf16), (1.0 - low).astype(bf16), low > 0.5


def two_heads(x, low, high):
    return jnp.concatenate([x * low, x * high], axis=0)


def pick_heads(both, first):
    rows = both.shape[0] // 2
    return jnp.where(first, both[:rows], both[rows:])


def pair_probs(q_pair, k_pair, count):
    raw = mm_nt(q_pair, k_pair) * (1.0 / math.sqrt(HEAD))
    col = lax.broadcasted_iota(jnp.int32, raw.shape, 1)
    raw = jnp.where(col < count, raw, -1e30)
    top = jnp.max(raw, axis=-1, keepdims=True)
    exponent = jnp.exp(raw - top)
    return exponent / jnp.sum(exponent, axis=-1, keepdims=True)


def fetch_attn(info, pieces, wbuf, sems, start, width):
    copies = []
    for e in range(2):
        _, owners = pieces_of(info, e)
        for k in range(4):
            src = pieces[4 * e + k]
            rows = src.shape[0]
            copies.append(
                pltpu.make_async_copy(
                    src.at[:, pl.ds(start, width)],
                    wbuf.at[e, pl.ds(pl.multiple_of(owners[k] * rows, rows), rows), :],
                    sems.at[e, k],
                )
            )
    for one in copies:
        one.start()
    return copies


def attend_kernel(seqs, *refs):
    info, h1, x, vec = refs[:4]
    pieces = refs[4:12]
    qkv, o, r, h2, stats, wbuf, sems = refs[12:]
    rows = h1.shape[0] // seqs
    d = h1.shape[1]
    half = d // 2
    copies = fetch_attn(info, pieces, wbuf, sems, 0, 4 * half)
    for e in range(2):
        core, _ = pieces_of(info, e)
        for one in copies[4 * e : 4 * e + 4]:
            one.wait()

        @pl.loop(0, 2)
        def _(t):
            near = pl.multiple_of(core * half + t * (half // 2), half // 2)
            for j in range(3):
                w = wbuf[e, :, pl.ds(pl.multiple_of(j * half + t * (half // 2), half // 2), half // 2)]
                got = mm(h1[...], w)
                if j != 1:
                    got = got + vec[2 + j // 2 : 3 + j // 2, pl.ds(near, half // 2)]
                qkv[:, pl.ds(pl.multiple_of(j * d + near, half // 2), half // 2)] = got.astype(bf16)

    low, high, first = head_masks()
    pairs = d // (2 * HEAD)

    @pl.loop(0, seqs * pairs)
    def _(i):
        n, j = i // pairs, i % pairs
        at = pl.ds(pl.multiple_of(n * rows, 16), rows)
        lanes = [pl.ds(pl.multiple_of(j * 2 * HEAD + m * d, 2 * HEAD), 2 * HEAD) for m in range(3)]
        q_pair = two_heads(qkv[at, lanes[0]], low, high)
        probs = pair_probs(q_pair, qkv[at, lanes[1]], info[4 + n]).astype(bf16)
        o[at, lanes[0]] = pick_heads(mm(probs, qkv[at, lanes[2]]), first).astype(bf16)

    for e in range(2):
        core, _ = pieces_of(info, e)

        @pl.loop(0, 2)
        def _(t):
            near = pl.ds(pl.multiple_of(core * half + t * (half // 2), half // 2), half // 2)
            w = wbuf[e, :, pl.ds(pl.multiple_of(3 * half + t * (half // 2), half // 2), half // 2)]
            r[:, near] = mm(o[...], w) + vec[4:5, near]

    stats[...] = jnp.zeros_like(stats)

    @pl.loop(0, seqs)
    def _(n):
        at = pl.ds(pl.multiple_of(n * rows, 16), rows)
        valid = lax.broadcasted_iota(jnp.int32, (rows, 1), 0) < info[4 + n]
        valid = jnp.where(valid, 1.0, 0.0)
        inputs = x[at, :].astype(f32)
        branch = r[at, :]
        resid = inputs + branch
        r[at, :] = resid
        normal, _ = layer_stats(resid)
        h2[at, :] = (normal * vec[5:6, :] + vec[6:7, :]).astype(bf16)
        stats[0:1, :] += jnp.sum(inputs * inputs * valid, axis=0, keepdims=True)
        stats[1:2, :] += jnp.sum(branch * branch * valid, axis=0, keepdims=True)


def feed_kernel(seqs, buf, *refs):
    info, keep, h2, em, r, vec = refs[:6]
    ups, downs = refs[6:14], refs[14:22]
    z_mine, z_yours, u_mine, u_yours, er, ea, out, sums = refs[22:30]
    wup, wdown, m_acc, t_acc, sem_up, sem_down = refs[30:]
    rows = h2.shape[0] // seqs
    d = h2.shape[1]
    strip = wup.shape[2] // 4
    tile = strip // 2
    copies = [[], []]
    for e in range(2):
        _, owners = pieces_of(info, e)
        for k in range(4):
            src = ups[4 * e + k]
            deep = src.shape[0]
            copies[e].append(
                pltpu.make_async_copy(
                    src,
                    wup.at[e, pl.ds(pl.multiple_of(owners[k] * deep, deep), deep), :],
                    sem_up.at[e, k],
                )
            )
            copies[e].append(
                pltpu.make_async_copy(downs[4 * e + k], wdown.at[e, owners[k]], sem_down.at[e, k])
            )
        for one in copies[e]:
            one.start()
    sums[...] = jnp.zeros_like(sums)
    m_acc[...] = jnp.zeros_like(m_acc)
    t_acc[...] = jnp.zeros_like(t_acc)
    for e, z_out, u_out in ((0, z_mine, u_mine), (1, z_yours, u_yours)):
        core, _ = pieces_of(info, e)
        for one in copies[e]:
            one.wait()

        @pl.loop(0, 8)
        def _(i):
            s, t = i // 2, i % 2
            near = pl.ds(pl.multiple_of(i * tile, tile), tile)
            far = (pl.ds(8 + s, 1), pl.ds(pl.multiple_of(core * strip + t * tile, tile), tile))
            w_up = wup[e, :, near]
            w_down = wdown[e, s, pl.ds(pl.multiple_of(t * tile, tile), tile), :]
            u = mm(h2[...], w_up) + vec[far]
            phi = 0.5 * (1.0 + lax.erf(u * root_half))
            z = (u * phi).astype(bf16)
            z_out[:, near] = z
            slope = phi + u * jnp.exp(-0.5 * u * u) * inverse_root_two_pi
            eu = (mm_nt(em[...], w_down) * slope).astype(bf16)
            u_out[:, near] = eu
            m_acc[...] += mm(z, w_down)
            t_acc[...] += mm_nt(eu, w_up)
            sums[far] = jnp.sum(eu.astype(f32), axis=0, keepdims=True)

    @pl.loop(0, seqs)
    def _(n):
        at = pl.ds(pl.multiple_of(n * rows, 16), rows)
        valid = lax.broadcasted_iota(jnp.int32, (rows, 1), 0) < info[4 + n]
        valid = jnp.where(valid, 1.0, 0.0)
        resid = r[at, :]
        m = m_acc[at, :] + vec[7:8, :]
        packed = ((resid + m) * valid).astype(bf16)
        out[n, 0:buf, :] = packed[0:buf]
        pick = picker(keep[n], rows - buf)
        out[n, buf:, :] = mm_tn(pick, packed[buf:]).astype(bf16)
        normal, inverse = layer_stats(resid)
        t = t_acc[at, :]
        low = em[at, :].astype(f32)
        back = low + norm_back(t, normal, inverse, vec[5:6, :])
        er[at, :] = back
        ea_low = back.astype(bf16)
        ea[at, :] = ea_low
        sums[4:5, :] += jnp.sum(ea_low.astype(f32), axis=0, keepdims=True)
        sums[5:6, :] += jnp.sum(t * normal, axis=0, keepdims=True)
        sums[6:7, :] += jnp.sum(t, axis=0, keepdims=True)
        sums[7:8, :] += jnp.sum(low, axis=0, keepdims=True)
        sums[12:13, :] += jnp.sum(m * m * valid, axis=0, keepdims=True)


def back_kernel(seqs, *refs):
    info, ea, qkv = refs[:3]
    pieces = refs[3:11]
    mine, yours, sums, wbuf, eo, sems = refs[11:]
    rows = ea.shape[0] // seqs
    d = ea.shape[1]
    half = d // 2
    copies = fetch_attn(info, pieces, wbuf, sems, 3 * half, half)
    for one in copies:
        one.wait()

    @pl.loop(0, 4)
    def _(s):
        near = pl.ds(pl.multiple_of(s * (d // 4), d // 4), d // 4)
        total = None
        for e in range(2):
            core, _ = pieces_of(info, e)
            part = ea[:, pl.ds(pl.multiple_of(core * half, half), half)]
            got = mm_nt(part, wbuf[e, near, :])
            total = got if total is None else total + got
        eo[:, near] = total.astype(bf16)

    low, high, first = head_masks()
    pairs = half // (2 * HEAD)
    scale = 1.0 / math.sqrt(HEAD)
    sums[...] = jnp.zeros_like(sums)
    for e, dst in ((0, mine), (1, yours)):
        core, _ = pieces_of(info, e)

        @pl.loop(0, seqs * pairs)
        def _(i):
            n, j = i // pairs, i % pairs
            at = pl.ds(pl.multiple_of(n * rows, 16), rows)
            far = core * half + j * 2 * HEAD
            lanes = [pl.ds(pl.multiple_of(far + m * d, 2 * HEAD), 2 * HEAD) for m in range(3)]
            k_pair = qkv[at, lanes[1]]
            q_both = two_heads(qkv[at, lanes[0]], low, high)
            probs = pair_probs(q_both, k_pair, info[4 + n])
            eo_both = two_heads(eo[at, lanes[0]], low, high)
            ep = mm_nt(eo_both, qkv[at, lanes[2]])
            inner = jnp.sum(probs * ep, axis=-1, keepdims=True)
            es = (probs * (ep - inner)).astype(bf16)
            ev = mm_tn(probs.astype(bf16), eo_both).astype(bf16)
            eq = (pick_heads(mm(es, k_pair), first) * scale).astype(bf16)
            ek = (mm_tn(es, q_both) * scale).astype(bf16)
            for m, value in enumerate((eq, ek, ev)):
                dst[at, pl.ds(pl.multiple_of(m * half + j * 2 * HEAD, 2 * HEAD), 2 * HEAD)] = value
            sums[2:3, lanes[0]] += jnp.sum(eq.astype(f32), axis=0, keepdims=True)
            sums[3:4, lanes[0]] += jnp.sum(ev.astype(f32), axis=0, keepdims=True)


def input_kernel(seqs, buf, *refs):
    info, keep, mine, yours, x, er, vec = refs[:7]
    pieces = refs[7:15]
    out, sums, wbuf, t_acc, sems = refs[15:]
    rows = x.shape[0] // seqs
    d = x.shape[1]
    half = d // 2
    copies = fetch_attn(info, pieces, wbuf, sems, 0, 3 * half)
    for one in copies:
        one.wait()

    @pl.loop(0, 4)
    def _(s):
        near = pl.ds(pl.multiple_of(s * (d // 4), d // 4), d // 4)
        t_acc[:, near] = mm_nt(mine[...], wbuf[0, near, :]) + mm_nt(yours[...], wbuf[1, near, :])

    sums[...] = jnp.zeros_like(sums)

    @pl.loop(0, seqs)
    def _(n):
        at = pl.ds(pl.multiple_of(n * rows, 16), rows)
        normal, inverse = layer_stats(x[at, :].astype(f32))
        t = t_acc[at, :]
        grad = er[at, :] + norm_back(t, normal, inverse, vec[0:1, :])
        sums[0:1, :] += jnp.sum(t * normal, axis=0, keepdims=True)
        sums[1:2, :] += jnp.sum(t, axis=0, keepdims=True)
        out[n, 0:buf, :] = grad[0:buf]
        pick = picker(keep[n], rows - buf)
        rest = grad[buf:]
        high = rest.astype(bf16)
        rest = rest - high.astype(f32)
        middle = rest.astype(bf16)
        low = (rest - middle.astype(f32)).astype(bf16)
        out[n, buf:, :] = mm_tn(pick, high) + mm_tn(pick, middle) + mm_tn(pick, low)


def grad_kernel(order, a_own, a_got, b_own, b_got, out):
    left = jnp.concatenate([a_own[...], a_got[...]], axis=0)
    right = jnp.concatenate([b_own[...], b_got[...]], axis=0)
    out[0] = mm_tn(left, right).astype(bf16)


def weight_grad(order, a_own, a_got, b_own, b_got, deep, wide, tile, b_start=0):
    rows = a_own.shape[0]
    blocks = 2
    return pl.pallas_call(
        grad_kernel,
        grid_spec=pltpu.PrefetchScalarGridSpec(
            num_scalar_prefetch=1,
            grid=(blocks, wide // tile),
            in_specs=[pl.BlockSpec((rows, deep), lambda i, j, order: (0, order[i]))] * 2
            + [pl.BlockSpec((rows, tile), lambda i, j, order: (0, order[2] * b_start + j))] * 2,
            out_specs=pl.BlockSpec((1, deep, tile), lambda i, j, order: (i, 0, j)),
        ),
        out_shape=sds((blocks, deep, wide), bf16),
        compiler_params=params(40),
        cost_estimate=cost(4 * rows * deep * wide * blocks, 4 * rows * (deep * 2 + wide)),
    )(order, a_own, a_got, b_own, b_got)


def adam_math(w, f, s, grad, rate, decay):
    first_new = beta_first * f + (1.0 - beta_first) * grad
    second_new = beta_second * s + (1.0 - beta_second) * grad * grad
    fix_first = 1.0 - beta_first**STEP
    fix_second = 1.0 - beta_second**STEP
    update = first_new / fix_first / (jnp.sqrt(second_new / fix_second) + adam_epsilon)
    return w - rate * (update + decay * w), first_new, second_new


def adam_kernel(info, w, f, s, g0, g1, g2, g3, *rest):
    w_out, f_out, s_out, low_out = rest[-4:]
    quarter = pl.program_id(0)
    for k, part in enumerate((g0, g1, g2, g3)):

        @pl.when(quarter == k)
        def _():
            new, first, second = adam_math(
                w[...], f[...], s[...], part[...].astype(f32), rate_matrix, weight_decay
            )
            w_out[...] = new
            f_out[...] = first
            s_out[...] = second
            low_out[...] = new.astype(bf16)


def adam_call(info, state, quarters, block, grid_width, place, grad_place, aliased=None):
    spec = pl.BlockSpec(block, place)
    shape = state[0].shape
    grads = [
        pl.BlockSpec(block, functools.partial(lambda k, i, j, info: grad_place(jnp.where(i == k, j, 0)), k))
        for k in range(4)
    ]
    extra = [] if aliased is None else list(aliased)
    return pl.pallas_call(
        adam_kernel,
        grid_spec=pltpu.PrefetchScalarGridSpec(
            num_scalar_prefetch=1,
            grid=(4, grid_width),
            in_specs=[spec] * 3 + grads + [ANY_SPEC] * len(extra),
            out_specs=[spec] * 4,
        ),
        out_shape=[sds(shape, f32)] * 3 + [sds(shape, bf16)],
        input_output_aliases={8 + k: k for k in range(len(extra))},
        compiler_params=params(40),
        cost_estimate=cost(20 * 4 * grid_width * block[0] * block[1], 28 * 4 * grid_width * block[0] * block[1]),
    )(info, *state, *quarters, *extra)


def cast_kernel(info, src, out):
    out[...] = src[...].astype(bf16)


def half_strips(info, matrix, start, count):
    deep = matrix.shape[0]
    strip = 512
    return pl.pallas_call(
        cast_kernel,
        grid_spec=pltpu.PrefetchScalarGridSpec(
            num_scalar_prefetch=1,
            grid=(count,),
            in_specs=[pl.BlockSpec((deep, strip), lambda j, info: (0, 2 * (start + j) + info[1]))],
            out_specs=pl.BlockSpec((deep, strip), lambda j, info: (0, j)),
        ),
        out_shape=sds((deep, strip * count), bf16),
        compiler_params=params(16),
        cost_estimate=cost(deep * strip * count, 6 * deep * strip * count),
    )(info, matrix)


def half_rows(info, matrix):
    deep, wide = matrix.shape[0] // 2, matrix.shape[1]
    return pl.pallas_call(
        cast_kernel,
        grid_spec=pltpu.PrefetchScalarGridSpec(
            num_scalar_prefetch=1,
            grid=(2,),
            in_specs=[pl.BlockSpec((deep // 2, wide), lambda j, info: (2 * info[1] + j, 0))],
            out_specs=pl.BlockSpec((deep // 2, wide), lambda j, info: (j, 0)),
        ),
        out_shape=sds((deep, wide), bf16),
        compiler_params=params(16),
        cost_estimate=cost(deep * wide, 6 * deep * wide),
    )(info, matrix)


def add_low(a, b):
    return (a.astype(f32) + b.astype(f32)).astype(bf16)


def local(groups, replicas, *args):
    tokens, keep, cot, mats, down, vectors, f_mats, f_down, f_vectors, s_mats, s_down, s_vectors = args
    seqs, length, d = tokens.shape
    image = keep.shape[1]
    buf = length - image
    rows = -(-(buf + KEEP_MAX) // 16) * 16
    total = seqs * rows
    half = d // 2
    group, replica = lax.axis_index("group"), lax.axis_index("dp")
    core, level = replica % 2, (replica // 2) % 2
    counts = buf + jnp.sum(keep, axis=1)
    info = jnp.concatenate([jnp.stack([group, core, level, 0 * core]), counts]).astype(jnp.int32)

    def permute(value, target):
        pairs = []
        for a in range(groups):
            for b in range(replicas):
                to_a, to_b = target(a, b)
                pairs.append((a * replicas + b, to_a * replicas + to_b))
        return lax.ppermute(value, BOTH, pairs)

    hop_one = lambda v: permute(v, lambda a, b: (a ^ (1 + b % 2), b))
    hop_two = lambda v: permute(v, lambda a, b: (a ^ (2 - b % 2), b))
    swap = lambda v: permute(v, lambda a, b: (a, b ^ 1))
    shift = lambda v, bit: permute(v, lambda a, b: (a, b ^ bit))

    low_vectors = vectors.astype(bf16)
    vec_parts = [low_vectors] + [
        permute(low_vectors, functools.partial(lambda flip, a, b: (a ^ flip, b), flip)) for flip in (1, 2, 3)
    ]

    def gather(own):
        one = hop_one(own)
        two = hop_two(own)
        three = hop_two(one)
        mine = [own, one, two, three]
        return mine + [swap(v) for v in mine]

    own_attn = half_strips(info, mats, 0, 4)
    own_up = half_strips(info, mats, 4, 4)
    own_down = half_rows(info, down)
    w_attn = gather(own_attn)
    own_up, own_down, _ = lax.optimization_barrier((own_up, own_down, w_attn[3]))
    w_up = gather(own_up)
    own_down, _ = lax.optimization_barrier((own_down, w_up[3]))
    w_down = gather(own_down)

    keep3 = keep.reshape(seqs, 1, image)
    x, em, h1, vec = pl.pallas_call(
        functools.partial(pack_kernel, buf),
        grid_spec=pltpu.PrefetchScalarGridSpec(
            num_scalar_prefetch=1,
            grid=(seqs,),
            in_specs=[pl.BlockSpec((1, 1, image), lambda n, info: (n, 0, 0))]
            + [pl.BlockSpec((1, length, d), lambda n, info: (n, 0, 0))] * 2
            + [pl.BlockSpec((12, vectors.shape[1]), lambda n, info: (0, 0))] * 4,
            out_specs=[pl.BlockSpec((rows, d), lambda n, info: (n, 0))] * 3
            + [pl.BlockSpec((16, d), lambda n, info: (0, 0))],
            scratch_shapes=[pltpu.VMEM((16, d), f32)],
        ),
        out_shape=[sds((total, d), bf16)] * 3 + [sds((16, d), f32)],
        compiler_params=params(40),
        cost_estimate=cost(8 * total * image * d, 10 * total * d),
    )(info, keep3, tokens, cot, *vec_parts)
    h1_got, em_got = swap(h1), swap(em)

    qkv, o, r, h2, stats = pl.pallas_call(
        functools.partial(attend_kernel, seqs),
        in_specs=[SMEM_SPEC] + [VMEM_SPEC] * 3 + [ANY_SPEC] * 8,
        out_specs=[VMEM_SPEC] * 5,
        out_shape=[
            sds((total, 3 * d), bf16),
            sds((total, d), bf16),
            sds((total, d), f32),
            sds((total, d), bf16),
            sds((8, d), f32),
        ],
        scratch_shapes=[pltpu.VMEM((2, d, 2 * d), bf16), pltpu.SemaphoreType.DMA((2, 4))],
        compiler_params=params(56),
        cost_estimate=cost(2 * total * 4 * d * d * 1.5, 20 * total * d),
    )(info, h1, x, vec, *w_attn)
    o_got, h2_got = swap(o), swap(h2)

    z_mine, z_yours, u_mine, u_yours, er, ea, block_output, sums_feed = pl.pallas_call(
        functools.partial(feed_kernel, seqs, buf),
        in_specs=[SMEM_SPEC] + [VMEM_SPEC] * 5 + [ANY_SPEC] * 16,
        out_specs=[VMEM_SPEC] * 8,
        out_shape=[sds((total, 2 * d), bf16)] * 4
        + [
            sds((total, d), f32),
            sds((total, d), bf16),
            sds((seqs, length, d), bf16),
            sds((16, d), f32),
        ],
        scratch_shapes=[
            pltpu.VMEM((2, d, 2 * d), bf16),
            pltpu.VMEM((2, 4, half, d), bf16),
            pltpu.VMEM((total, d), f32),
            pltpu.VMEM((total, d), f32),
            pltpu.SemaphoreType.DMA((2, 4)),
            pltpu.SemaphoreType.DMA((2, 4)),
        ],
        compiler_params=params(60),
        cost_estimate=cost(2 * total * 16 * d * d, 60 * total * d),
    )(info, keep3, h2, em, r, vec, *w_up, *w_down)

    z_got, u_got, ea_got = swap(z_yours), swap(u_yours), swap(ea)

    first, second = core + 1, 2 - core
    send_order = jnp.stack([group ^ first, group ^ 3, core]).astype(jnp.int32)
    keep_order = jnp.stack([group, group ^ second, core]).astype(jnp.int32)

    def reduce_blocks(make):
        sent = make(send_order)
        got = hop_one(sent)
        kept = make(keep_order)
        kept = add_low(kept, got)
        mine = add_low(kept[0], hop_two(kept[1]))
        deep = mine.shape[0] // 2
        give = lax.dynamic_slice(mine, ((1 - level) * deep, 0), (deep, mine.shape[1]))
        hold = lax.dynamic_slice(mine, (level * deep, 0), (deep, mine.shape[1]))
        hold = add_low(hold, shift(give, 2))
        bit = 4
        while bit < replicas:
            hold = add_low(hold, shift(hold, bit))
            bit *= 2
        other = shift(hold, 2)
        return hold, other, swap(hold), swap(other)

    g_down = reduce_blocks(
        lambda order: weight_grad(order, z_mine, z_got, em, em_got, half, d, half)
    )

    def up_and_out(order):
        return weight_grad(order, h2, h2_got, u_mine, u_got, d // 4, 2 * d, half)

    g_up = reduce_blocks(up_and_out)
    g_out = reduce_blocks(lambda order: weight_grad(order, o, o_got, ea, ea_got, d // 4, half, half, 1))

    e_mine, e_yours, sums_back = pl.pallas_call(
        functools.partial(back_kernel, seqs),
        in_specs=[SMEM_SPEC] + [VMEM_SPEC] * 2 + [ANY_SPEC] * 8,
        out_specs=[VMEM_SPEC] * 3,
        out_shape=[sds((total, 3 * half), bf16)] * 2 + [sds((8, d), f32)],
        scratch_shapes=[
            pltpu.VMEM((2, d, half), bf16),
            pltpu.VMEM((total, d), bf16),
            pltpu.SemaphoreType.DMA((2, 4)),
        ],
        compiler_params=params(48),
        cost_estimate=cost(2 * total * 4 * d * d, 20 * total * d),
    )(info, ea, qkv, *w_attn)
    e_got = swap(e_yours)
    g_qkv = reduce_blocks(
        lambda order: weight_grad(order, h1, h1_got, e_mine, e_got, d // 4, 3 * half, half)
    )

    input_grad, sums_in = pl.pallas_call(
        functools.partial(input_kernel, seqs, buf),
        in_specs=[SMEM_SPEC] + [VMEM_SPEC] * 6 + [ANY_SPEC] * 8,
        out_specs=[VMEM_SPEC] * 2,
        out_shape=[sds((seqs, length, d), f32), sds((8, d), f32)],
        scratch_shapes=[
            pltpu.VMEM((2, d, 3 * half), bf16),
            pltpu.VMEM((total, d), f32),
            pltpu.SemaphoreType.DMA((2, 4)),
        ],
        compiler_params=params(56),
        cost_estimate=cost(2 * total * 3 * d * d, 20 * total * d),
    )(info, keep3, e_mine, e_yours, x, er, vec, *w_attn)

    squares = jnp.stack([jnp.sum(stats[0]), jnp.sum(stats[1]), jnp.sum(sums_feed[12]), jnp.sum(counts).astype(f32)])
    small = jnp.concatenate(
        [
            sums_in[0:2],
            sums_back[2:4],
            sums_feed[4:12],
            jnp.pad(squares.reshape(1, 4), ((0, 3), (0, d - 4))),
        ]
    )
    bit = 1
    while bit < groups:
        small = small + permute(small, functools.partial(lambda flip, a, b: (a ^ flip, b), bit))
        bit *= 2
    bit = 1
    while bit < replicas:
        small = small + shift(small, bit)
        bit *= 2
    branch_rms = jnp.sqrt(small[12, 0:3] / (small[12, 3] * d))
    part = vectors.shape[1]
    grad_vectors = lax.dynamic_slice(small, (0, group * part), (12, part))

    def core_of(k, info):
        return info[1] ^ (k // 2)

    def level_of(k, info):
        return info[2] ^ (k % 2)

    new_down = adam_call(
        info,
        (down, f_down, s_down),
        g_down,
        (down.shape[0] // 4, half),
        2,
        lambda i, j, info: (2 * core_of(i, info) + level_of(i, info), j),
        lambda j: (0, j),
    )

    def adam_mats(quarters, first_strip, strips, previous):
        return adam_call(
            info,
            (mats, f_mats, s_mats),
            quarters,
            (mats.shape[0] // 2, half),
            strips,
            lambda i, j, info: (level_of(i, info), 2 * (first_strip + j) + core_of(i, info)),
            lambda j: (0, j),
            previous,
        )

    new_mats = adam_mats(g_up, 4, 4, None)
    new_mats = adam_mats(g_out, 3, 1, new_mats)
    new_mats = adam_mats(g_qkv, 0, 3, new_mats)
    new_vectors, first_vectors, second_vectors = adam_math(
        vectors, f_vectors, s_vectors, grad_vectors, rate_vector, 0.0
    )
    return (
        block_output,
        input_grad,
        new_mats[0],
        new_down[0],
        new_vectors,
        new_mats[1],
        new_down[1],
        first_vectors,
        new_mats[2],
        new_down[2],
        second_vectors,
        new_mats[3],
        new_down[3],
        new_vectors.astype(bf16),
        branch_rms,
    )


def solution(mesh):
    rows, owned, columns = P(BOTH, None, None), P("group", None), P(None, "group")
    state = (owned, owned, columns)
    return jax.shard_map(
        functools.partial(local, mesh.shape["group"], mesh.shape["dp"]),
        mesh=mesh,
        in_specs=(rows, P(BOTH, None), rows) + state * 3,
        out_specs=(rows, rows) + state * 4 + (P(),),
        check_vma=False,
    )
```

time: 1130 us -> 565 us (0.50)
  waiting for transfers between devices: 513 us -> 225 us
  matrix products: 258 us -> 0 us
  Pallas kernels: 0 us -> 221 us
  local copies, waits for them, and re-layouts: 137 us -> 26.4 us
  other arithmetic: 121 us -> 21.3 us
  blocking collectives: 79.8 us -> 0 us
  starting transfers between devices: 0.33 us -> 66.4 us
  between operations: 15.5 us -> 2.85 us
    dot_general x18 -> x0, matrix products: 258 us -> none  [the longest x1 29.7 us: local(): jnp.einsum('sqhd,skhd->shqk', grad_attended, value_heads, preferred_eleme...]
    reduce_scatter x4 -> x0, waiting for transfers between devices: 227 us -> none  [the longest x1 157 us: local(): lax.psum_scatter(attn_grads, 'group', scatter_dimension=0, tiled=True)]
    ppermute x0 -> x65, waiting for transfers between devices: none -> 225 us  [permute(): return lax.ppermute(value, BOTH, pairs)]
    pallas_call x0 -> x20, Pallas kernels: none -> 221 us  [the longest x8 46.5 us: weight_grad(): pl.pallas_call(grad_kernel, grid_spec=pltpu.PrefetchScalarGridSpec(num_sc...]
    psum x1 -> x0, waiting for transfers between devices: 206 us -> none  [local(): lax.psum((part_attn, part_up, part_down, part_vectors), 'dp')]
    all_gather x3 -> x0, waiting for transfers between devices: 79.6 us -> none  [the longest x1 62.6 us: local(): lax.all_gather(low_matrices[:, :attn_cols], 'group', axis=0, tiled=True)]
    reshape x12 -> x1, local copies, waits for them, and re-layouts: 75.3 us -> 0.01 us  [local(): keep3 = keep.reshape(seqs, 1, image)]
    convert_element_type x13 -> x18, other arithmetic: 84.2 us -> 11.7 us  [the longest x16 11 us: add_low(): return (a.astype(f32) + b.astype(f32)).astype(bf16)]
  transfers between devices with their start and end apart: 8 -> 65, of which waited for: 5 -> 22; matrix products, arithmetic and copies ran while one was open for 37% -> 4% of each run, Pallas kernels for 0% -> 37%
where the time goes in v1:
time: 565 us; the launch traced here: 562 us
  waiting for transfers between devices  225 us (40%)
  Pallas kernels  221 us (39%)
  starting transfers between devices  66.4 us (12%)
  local copies, waits for them, and re-layouts  26.4 us (5%)
  other arithmetic  21.3 us (4%)
    ppermute x65, waiting for transfers between devices, permute(): return lax.ppermute(value, BOTH, pairs)  225 us
    ppermute x65, starting transfers between devices, permute(): return lax.ppermute(value, BOTH, pairs)  66.4 us
    pallas_call x8, Pallas kernels, weight_grad(): pl.pallas_call(grad_kernel, grid_spec=pltpu.PrefetchScalarGridSpec(num_sc...  46.5 us
    pallas_call x4, Pallas kernels, adam_call(): pl.pallas_call(adam_kernel, grid_spec=pltpu.PrefetchScalarGridSpec(num_sc...  43.6 us
    pallas_call x1, Pallas kernels, local(): pl.pallas_call(functools.partial(feed_kernel, seqs, buf), in_specs=[SMEM_...  40.3 us
    pallas_call x1, Pallas kernels, local(): pl.pallas_call(functools.partial(back_kernel, seqs), in_specs=[SMEM_SPEC]...  32.9 us
    pallas_call x1, Pallas kernels, local(): pl.pallas_call(functools.partial(attend_kernel, seqs), in_specs=[SMEM_SPE...  32.8 us
    unnamed x118, local copies, waits for them, and re-layouts  23.8 us
  transfers between devices with their start and end apart: 65, of which 22 were waited for; matrix products, arithmetic and copies ran while one was open for 4% of the time, Pallas kernels for 37%

profile of v1, /device:TPU:0, one launch (start us, length us, event | category | flops | bytes accessed | tf_op | source)
XLA Modules:
  0.0 562.2 jit_solution(5974022241236627674)
XLA Ops:
  2.2 3.4 copy-done
  6.6 3.0 collective-permute-start.3
  9.6 12.8 %collective-permute-done.3.refs_5_.refs_4_.refs_8_ = bf16[256,2048]{1,0:T(8,128)(2,1)S(1)} collective-permute-done((bf16[256,2048]{1,0:T(8,128)(2,1)S(1)}, bf16[256,2048]{1,0:T(8,128)(2,1)S(1)}, u32[]{:S(2)}, u32[]{:S(2)}) %collective-permute-start.3) | collective-permute-done | bytes 1048608 | tf_op jit(solution)/shard_map/ppermute | solution.py:514
  28.2 9.0 %collective-permute-done.5.refs_7_.refs_6_.refs_10_ = bf16[256,2048]{1,0:T(8,128)(2,1)S(1)} collective-permute-done((bf16[256,2048]{1,0:T(8,128)(2,1)S(1)}, bf16[256,2048]{1,0:T(8,128)(2,1)S(1)}, u32[]{:S(2)}, u32[]{:S(2)}) %collective-permute-start.5) | collective-permute-done | bytes 1048608 | tf_op jit(solution)/shard_map/ppermute | solution.py:514
  39.2 12.8 %collective-permute-done.10.refs_7_ = bf16[256,2048]{1,0:T(8,128)(2,1)S(1)} collective-permute-done((bf16[256,2048]{1,0:T(8,128)(2,1)S(1)}, bf16[256,2048]{1,0:T(8,128)(2,1)S(1)}, u32[]{:S(2)}, u32[]{:S(2)}) %collective-permute-start.10) | collective-permute-done | bytes 1048608 | tf_op jit(solution)/shard_map/ppermute | solution.py:514
  57.7 9.3 %collective-permute-done.12.refs_9_ = bf16[256,2048]{1,0:T(8,128)(2,1)S(1)} collective-permute-done((bf16[256,2048]{1,0:T(8,128)(2,1)S(1)}, bf16[256,2048]{1,0:T(8,128)(2,1)S(1)}, u32[]{:S(2)}, u32[]{:S(2)}) %collective-permute-start.12) | collective-permute-done | bytes 1048608 | tf_op jit(solution)/shard_map/ppermute | solution.py:514
  67.0 3.0 collective-permute-start.2
  69.9 5.1 collective-permute-start.7
  75.0 3.4 collective-permute-done.4.refs_6_.refs_5_.refs_9_
  82.6 20.4 %collective-permute-done.11.refs_8_ = bf16[256,2048]{1,0:T(8,128)(2,1)S(1)} collective-permute-done((bf16[256,2048]{1,0:T(8,128)(2,1)S(1)}, bf16[256,2048]{1,0:T(8,128)(2,1)S(1)}, u32[]{:S(2)}, u32[]{:S(2)}) %collective-permute-start.11) | collective-permute-done | bytes 1048608 | tf_op jit(solution)/shard_map/ppermute | solution.py:514
  103.1 2.6 collective-permute-start.18
  106.6 12.2 %collective-permute-done.18.refs_16_ = bf16[512,1024]{1,0:T(8,128)(2,1)} collective-permute-done((bf16[512,1024]{1,0:T(8,128)(2,1)}, bf16[512,1024]{1,0:T(8,128)(2,1)}, u32[]{:S(2)}, u32[]{:S(2)}) %collective-permute-start.18) | collective-permute-done | bytes 1048608 | tf_op jit(solution)/shard_map/ppermute | solution.py:514
  118.7 11.2 %collective-permute-done.19.refs_17_ = bf16[512,1024]{1,0:T(8,128)(2,1)} collective-permute-done((bf16[512,1024]{1,0:T(8,128)(2,1)S(1)}, bf16[512,1024]{1,0:T(8,128)(2,1)}, u32[]{:S(2)}, u32[]{:S(2)}) %collective-permute-start.19) | collective-permute-done | bytes 1048608 | tf_op jit(solution)/shard_map/ppermute | solution.py:514
  134.3 4.0 shard_map.235
  139.9 32.8 %shard_map.237 = (bf16[576,3072]{1,0:T(8,128)(2,1)}, bf16[576,1024]{1,0:T(8,128)(2,1)}, f32[576,1024]{1,0:T(8,128)}, bf16[576,1024]{1,0:T(8,128)(2,1)}, f32[8,1024]{1,0:T(8,128)}) custom-call(s32[8]{0:T(128)} %copy-done.32, bf16[576,1024]{1,0:T(8,128)(2,1)} %get-tuple-element.56.refs_1_.a_own, bf16[576,1024]{1,0:T(8,128)(2,1)} %copy-done.17, ...), custom_call_target="tpu_custom_call" | custom-call | flops 7247757312 | bytes 11796480 | tf_op jit(solution)/shard_map/pallas_call | solution.py:561
  174.9 40.3 %shard_map.240 = (bf16[576,2048]{1,0:T(8,128)(2,1)}, bf16[576,2048]{1,0:T(8,128)(2,1)}, bf16[576,2048]{1,0:T(8,128)(2,1)}, bf16[576,2048]{1,0:T(8,128)(2,1)}, f3...) custom-call(s32[8]{0:T(128)} %copy-done.32, ...), custom_call_target="tpu_custom_call" | custom-call | flops 19327352832 | bytes 35389440 | tf_op jit(solution)/shard_map/pallas_call | solution.py:578
  217.8 32.9 %shard_map.241 = (bf16[576,1536]{1,0:T(8,128)(2,1)}, bf16[576,1536]{1,0:T(8,128)(2,1)}, f32[8,1024]{1,0:T(8,128)S(1)}) custom-call(s32[8]{0:T(128)S(1)} %copy-done.33, bf16[576,1024]{1,0:T(8,128)(2,1)} %get-tuple-element.66.refs_1_.b_own, bf16[576,3072]{1,0:T(8,128)(2,1)} %get-tuple-element.67.refs_2_, bf16[256,2048]{1,0:T(8,128)(2,1)S(1)} %copy-done.14, ...), custom_call_target="tpu_custom_call" | custom-call | flops 4831838208 | bytes 11796480 | tf_op jit(solution)/shard_map/pallas_call | solution.py:634
  251.9 16.8 %shard_map.242 = (f32[4,320,1024]{2,1,0:T(8,128)}, f32[8,1024]{1,0:T(8,128)}) custom-call(s32[8]{0:T(128)} %copy-done.32, s32[4,1,256]{2,1,0:T(1,128)} %copy-done.35, bf16[576,1536]{1,0:T(8,128)(2,1)} %get-tuple-element.68.refs_2_.b_own, bf16[576,1536]{1,0:T(8,128)(2,1)} %get-tuple-element.69.refs_3_, bf16[576,1024]{1,0:T(8,128)(2,1)} %copy-done.17, ...), custom_call_target="tpu_custom_call" | custom-call | flops 3623878656 | bytes 11796480 | tf_op jit(solution)/shard_map/pallas_call | solution.py:652
  271.6 2.3 collective-permute-start.60
  273.9 2.6 collective-permute-done.60
  278.7 2.7 shard_map.246
  285.3 5.4 collective-permute-done.35
  294.2 2.7 shard_map.245
  300.6 2.2 collective-permute-done.63
  305.6 6.0 %shard_map.244 = bf16[2,256,1536]{2,1,0:T(8,128)(2,1)S(1)} custom-call(s32[3]{0:T(128)S(1)} %add_add_fusion.1.order, bf16[576,1024]{1,0:T(8,128)(2,1)} %get-tuple-element.56.refs_1_.a_own, bf16[576,1024]{1,0:T(8,128)(2,1)} %collective-permute-done.24.a_got, bf16[576,1536]{1,0:T(8,128)(2,1)S(1)} %copy-done.4, bf16[576,1536]{1,0:T(8,128)(2,1)S(1)} %collective-permute-done.25.b_got), custom_call_target="tpu_custom_call" | custom-call | flops 1811939328 | bytes 4718592 | tf_op jit(solution)/shard_map/pallas_call | solution.py:391
  315.5 8.3 %shard_map.248 = bf16[2,256,2048]{2,1,0:T(8,128)(2,1)S(1)} custom-call(s32[3]{0:T(128)S(1)} %add_add_fusion.1.order, bf16[576,1024]{1,0:T(8,128)(2,1)} %get-tuple-element.59.refs_2_.a_own, bf16[576,1024]{1,0:T(8,128)(2,1)} %collective-permute-done.42.a_got, bf16[576,2048]{1,0:T(8,128)(2,1)S(1)} %copy-done.6, bf16[576,2048]{1,0:T(8,128)(2,1)} %collective-permute-done.43.b_got), custom_call_target="tpu_custom_call" | custom-call | flops 2415919104 | bytes 5898240 | tf_op jit(solution)/shard_map/pallas_call | solution.py:391
  324.8 5.7 %shard_map.243 = bf16[2,256,1536]{2,1,0:T(8,128)(2,1)S(1)} custom-call(s32[3]{0:T(128)S(1)} %add_add_fusion.order, bf16[576,1024]{1,0:T(8,128)(2,1)} %get-tuple-element.56.refs_1_.a_own, bf16[576,1024]{1,0:T(8,128)(2,1)} %collective-permute-done.24.a_got, bf16[576,1536]{1,0:T(8,128)(2,1)S(1)} %copy-done.4, bf16[576,1536]{1,0:T(8,128)(2,1)S(1)} %collective-permute-done.25.b_got), custom_call_target="tpu_custom_call" | custom-call | flops 1811939328 | bytes 4718592 | tf_op jit(solution)/shard_map/pallas_call | solution.py:391
  330.6 2.7 collective-permute-start.64
  334.3 6.3 %shard_map.253 = bf16[2,512,1024]{2,1,0:T(8,128)(2,1)S(1)} custom-call(s32[3]{0:T(128)S(1)} %add_add_fusion.1.order, bf16[576,2048]{1,0:T(8,128)(2,1)S(1)} %copy-done.5, bf16[576,2048]{1,0:T(8,128)(2,1)} %collective-permute-done.51.a_got, bf16[576,1024]{1,0:T(8,128)(2,1)} %get-tuple-element.60.refs_3_.b_own, bf16[576,1024]{1,0:T(8,128)(2,1)} %collective-permute-done.52.b_got), custom_call_target="tpu_custom_call" | custom-call | flops 2415919104 | bytes 4718592 | tf_op jit(solution)/shard_map/pallas_call | solution.py:391
  341.7 8.3 %shard_map.247 = bf16[2,256,2048]{2,1,0:T(8,128)(2,1)S(1)} custom-call(s32[3]{0:T(128)S(1)} %add_add_fusion.order, bf16[576,1024]{1,0:T(8,128)(2,1)} %get-tuple-element.59.refs_2_.a_own, bf16[576,1024]{1,0:T(8,128)(2,1)} %collective-permute-done.42.a_got, bf16[576,2048]{1,0:T(8,128)(2,1)S(1)} %copy-done.6, bf16[576,2048]{1,0:T(8,128)(2,1)} %collective-permute-done.43.b_got), custom_call_target="tpu_custom_call" | custom-call | flops 2415919104 | bytes 5898240 | tf_op jit(solution)/shard_map/pallas_call | solution.py:391
  350.0 6.5 %shard_map.252 = bf16[2,512,1024]{2,1,0:T(8,128)(2,1)S(1)} custom-call(s32[3]{0:T(128)S(1)} %add_add_fusion.order, bf16[576,2048]{1,0:T(8,128)(2,1)S(1)} %copy-done.5, bf16[576,2048]{1,0:T(8,128)(2,1)} %collective-permute-done.51.a_got, bf16[576,1024]{1,0:T(8,128)(2,1)} %get-tuple-element.60.refs_3_.b_own, bf16[576,1024]{1,0:T(8,128)(2,1)} %collective-permute-done.52.b_got), custom_call_target="tpu_custom_call" | custom-call | flops 2415919104 | bytes 4718592 | tf_op jit(solution)/shard_map/pallas_call | solution.py:391
  360.0 2.5 add_convert_fusion.1
  363.1 31.4 %collective-permute-done.53 = bf16[2,512,1024]{2,1,0:T(8,128)(2,1)S(1)} collective-permute-done((bf16[2,512,1024]{2,1,0:T(8,128)(2,1)S(1)}, bf16[2,512,1024]{2,1,0:T(8,128)(2,1)S(1)}, u32[]{:S(2)}, u32[]{:S(2)}) %collective-permute-start.53) | collective-permute-done | bytes 2097184 | tf_op jit(solution)/shard_map/ppermute | solution.py:514
  397.3 2.8 collective-permute-start.46
  400.1 10.3 %collective-permute-done.54 = bf16[512,1024]{1,0:T(8,128)(2,1)S(1)} collective-permute-done((bf16[512,1024]{1,0:T(8,128)(2,1)S(1)}, bf16[512,1024]{1,0:T(8,128)(2,1)S(1)}, u32[]{:S(2)}, u32[]{:S(2)}) %collective-permute-start.54) | collective-permute-done | bytes 1048608 | tf_op jit(solution)/shard_map/ppermute | solution.py:514
  410.9 2.8 collective-permute-start.55
  413.9 2.7 collective-permute-start.47
  416.6 21.1 %collective-permute-done.55 = bf16[256,1024]{1,0:T(8,128)(2,1)S(1)} collective-permute-done((bf16[256,1024]{1,0:T(8,128)(2,1)S(1)}, bf16[256,1024]{1,0:T(8,128)(2,1)S(1)}, u32[]{:S(2)}, u32[]{:S(2)}) %collective-permute-start.55) | collective-permute-done | bytes 524320 | tf_op jit(solution)/shard_map/ppermute | solution.py:514
  438.8 4.5 collective-permute-done.28
  445.9 3.2 collective-permute-start.48
  449.0 26.1 %collective-permute-done.56 = bf16[256,1024]{1,0:T(8,128)(2,1)S(1)} collective-permute-done((bf16[256,1024]{1,0:T(8,128)(2,1)S(1)}, bf16[256,1024]{1,0:T(8,128)(2,1)S(1)}, u32[]{:S(2)}, u32[]{:S(2)}) %collective-permute-start.56) | collective-permute-done | bytes 524320 | tf_op jit(solution)/shard_map/ppermute | solution.py:514
  475.5 7.0 %collective-permute-done.29 = bf16[128,1536]{1,0:T(8,128)(2,1)S(1)} collective-permute-done((bf16[128,1536]{1,0:T(8,128)(2,1)S(1)}, bf16[128,1536]{1,0:T(8,128)(2,1)S(1)}, u32[]{:S(2)}, u32[]{:S(2)}) %collective-permute-start.29) | collective-permute-done | bytes 393248 | tf_op jit(solution)/shard_map/ppermute | solution.py:514
  485.9 18.9 %collective-permute-done.39.g1 = bf16[128,512]{1,0:T(8,128)(2,1)S(1)} collective-permute-done((bf16[128,512]{1,0:T(8,128)(2,1)S(1)}, bf16[128,512]{1,0:T(8,128)(2,1)S(1)}, u32[]{:S(2)}, u32[]{:S(2)}) %collective-permute-start.39) | collective-permute-done | bytes 131104 | tf_op jit(solution)/shard_map/ppermute | solution.py:514
  510.7 3.4 copy-done.1
  514.1 15.1 %shard_map.249 = (f32[256,8192]{1,0:T(8,128)}, f32[256,8192]{1,0:T(8,128)}, f32[256,8192]{1,0:T(8,128)}, bf16[256,8192]{1,0:T(8,128)(2,1)}) custom-call(s32[8]{0:T(128)S(1)} %copy-done.34, f32[256,8192]{1,0:T(8,128)S(1)} %copy-done.1, f32[256,8192]{1,0:T(8,128)} %f.6, f32[256,8192]{1,0:T(8,128)} %s.6, bf16[128,2048]{1,0:T(8,128)(2,1)S(1)} %add_convert_fusion.5.g0, ...), custom_call_target="tpu_custom_call" | custom-call | flops 20971520 | bytes 29360128 | tf_op jit(solution)/shard_map/pallas_call | solution.py:439
  531.4 5.8 %shard_map.250 = (f32[256,8192]{1,0:T(8,128)}, f32[256,8192]{1,0:T(8,128)}, f32[256,8192]{1,0:T(8,128)}, bf16[256,8192]{1,0:T(8,128)(2,1)}) custom-call(s32[8]{0:T(128)S(1)} %copy-done.34, f32[256,8192]{1,0:T(8,128)S(1)} %copy-done.1, f32[256,8192]{1,0:T(8,128)} %f.6, ...), custom_call_target="tpu_custom_call", output_to_operand_aliasing={{0}: (8, {}), {1}: (9, {}), {2}: (10, {}), {3}: (11, {})} | custom-call | flops 5242880 | bytes 7340032 | tf_op jit(solution)/shard_map/pallas_call | solution.py:439
  539.5 11.0 %shard_map.254 = (f32[1024,1024]{1,0:T(8,128)}, f32[1024,1024]{1,0:T(8,128)}, f32[1024,1024]{1,0:T(8,128)}, bf16[1024,1024]{1,0:T(8,128)(2,1)}) custom-call(s32[8]{0:T(128)S(1)} %copy-done.34, f32[1024,1024]{1,0:T(8,128)S(1)} %copy-done.3, f32[1024,1024]{1,0:T(8,128)S(1)} %copy-done.12, f32[1024,1024]{1,0:T(8,128)} %s.7, ...), custom_call_target="tpu_custom_call" | custom-call | flops 20971520 | bytes 29360128 | tf_op jit(solution)/shard_map/pallas_call | solution.py:439
  550.5 11.8 %shard_map.251 = (f32[256,8192]{1,0:T(8,128)}, f32[256,8192]{1,0:T(8,128)}, f32[256,8192]{1,0:T(8,128)}, bf16[256,8192]{1,0:T(8,128)(2,1)}) custom-call(s32[8]{0:T(128)S(1)} %copy-done.34, f32[256,8192]{1,0:T(8,128)S(1)} %bitcast.44, f32[256,8192]{1,0:T(8,128)} %f.6, ...), custom_call_target="tpu_custom_call", output_to_operand_aliasing={{0}: (8, {}), {1}: (9, {}), {2}: (10, {}), {3}: (11, {})} | custom-call | flops 15728640 | bytes 22020096 | tf_op jit(solution)/shard_map/pallas_call | solution.py:439
  (267 shorter events, 82.6 us)
Async XLA Ops:
  6.6 15.8 %collective-permute-start.3 = (bf16[256,2048]{1,0:T(8,128)(2,1)S(1)}, bf16[256,2048]{1,0:T(8,128)(2,1)S(1)}, u32[]{:S(2)}, u32[]{:S(2)}) collective-permute-start(bf16[256,2048]{1,0:T(8,128)(2,1)S(1)} %shard_map.236.refs_4_.refs_3_.refs_7_), channel_id=1, source_target_pairs={{0,8},{1,17},{2,10},{3,19},{4,12},{5,21},{6,14},{7,23},{8,0},{9,25... | collective-permute-start | bytes 3145736 | tf_op jit(solution)/shard_map/ppermute | solution.py:514
  54.1 24.3 %collective-permute-start.4 = (bf16[256,2048]{1,0:T(8,128)(2,1)S(1)}, bf16[256,2048]{1,0:T(8,128)(2,1)S(1)}, u32[]{:S(2)}, u32[]{:S(2)}) collective-permute-start(bf16[256,2048]{1,0:T(8,128)(2,1)S(1)} %shard_map.236.refs_4_.refs_3_.refs_7_), channel_id=1, source_target_pairs={{0,16},{1,9},{2,18},{3,11},{4,20},{5,13},{6,22},{7,15},{8,24},{9,1... | collective-permute-start | bytes 3145736 | tf_op jit(solution)/shard_map/ppermute | solution.py:514
  54.1 26.5 %collective-permute-start.6 = (bf16[256,2048]{1,0:T(8,128)(2,1)S(1)}, bf16[256,2048]{1,0:T(8,128)(2,1)S(1)}, u32[]{:S(2)}, u32[]{:S(2)}) collective-permute-start(bf16[256,2048]{1,0:T(8,128)(2,1)S(1)} %shard_map.236.refs_4_.refs_3_.refs_7_), channel_id=1, source_target_pairs={{0,1},{1,0},{2,3},{3,2},{4,5},{5,4},{6,7},{7,6},{8,9},{9,8},{10,11... | collective-permute-start | bytes 3145736 | tf_op jit(solution)/shard_map/ppermute | solution.py:514
  56.2 22.3 %collective-permute-start.1 = (bf16[12,256]{1,0:T(8,128)(2,1)S(1)}, bf16[12,256]{1,0:T(8,128)(2,1)S(1)}, u32[]{:S(2)}, u32[]{:S(2)}) collective-permute-start(bf16[12,256]{1,0:T(8,128)(2,1)S(1)} %convert_element_type.167.v0), channel_id=1, source_target_pairs={{0,16},{1,17},{2,18},{3,19},{4,20},{5,21},{6,22},{7,23},{8,24},{9,... | collective-permute-start | bytes 18440 | tf_op jit(solution)/shard_map/ppermute | solution.py:514
  78.4 24.6 %collective-permute-start.11 = (bf16[256,2048]{1,0:T(8,128)(2,1)S(1)}, bf16[256,2048]{1,0:T(8,128)(2,1)S(1)}, u32[]{:S(2)}, u32[]{:S(2)}) collective-permute-start(bf16[256,2048]{1,0:T(8,128)(2,1)S(1)} %shard_map.238.refs_6_), channel_id=1, source_target_pairs={{0,16},{1,9},{2,18},{3,11},{4,20},{5,13},{6,22},{7,15},{8,24},{9,1... | collective-permute-start | bytes 3145736 | tf_op jit(solution)/shard_map/ppermute | solution.py:514
  80.5 22.6 %collective-permute-start.9 = (bf16[256,2048]{1,0:T(8,128)(2,1)S(1)}, bf16[256,2048]{1,0:T(8,128)(2,1)S(1)}, u32[]{:S(2)}, u32[]{:S(2)}) collective-permute-start(bf16[256,2048]{1,0:T(8,128)(2,1)S(1)} %collective-permute-done.5.refs_7_.refs_6_.refs_10_), channel_id=1, source_target_pairs={{0,1},{1,0},{2,3},{3,2},{4,5},{5,4},{6,7},{7,6},{8,9},{9,8},{10,11... | collective-permute-start | bytes 3145736 | tf_op jit(solution)/shard_map/ppermute | solution.py:514
  80.6 25.0 %collective-permute-start.17 = (bf16[512,1024]{1,0:T(8,128)(2,1)}, bf16[512,1024]{1,0:T(8,128)(2,1)S(1)}, u32[]{:S(2)}, u32[]{:S(2)}) collective-permute-start(bf16[512,1024]{1,0:T(8,128)(2,1)} %shard_map.239.refs_14_), channel_id=1, source_target_pairs={{0,8},{1,17},{2,10},{3,19},{4,12},{5,21},{6,14},{7,23},{8,0},{9,25... | collective-permute-start | bytes 3145736 | tf_op jit(solution)/shard_map/ppermute | solution.py:514
  82.1 23.9 %collective-permute-start.13 = (bf16[256,2048]{1,0:T(8,128)(2,1)S(1)}, bf16[256,2048]{1,0:T(8,128)(2,1)S(1)}, u32[]{:S(2)}, u32[]{:S(2)}) collective-permute-start(bf16[256,2048]{1,0:T(8,128)(2,1)S(1)} %shard_map.238.refs_6_), channel_id=1, source_target_pairs={{0,1},{1,0},{2,3},{3,2},{4,5},{5,4},{6,7},{7,6},{8,9},{9,8},{10,11... | collective-permute-start | bytes 3145736 | tf_op jit(solution)/shard_map/ppermute | solution.py:514
  82.2 23.9 %collective-permute-start.14 = (bf16[256,2048]{1,0:T(8,128)(2,1)S(1)}, bf16[256,2048]{1,0:T(8,128)(2,1)S(1)}, u32[]{:S(2)}, u32[]{:S(2)}) collective-permute-start(bf16[256,2048]{1,0:T(8,128)(2,1)S(1)} %collective-permute-done.10.refs_7_), channel_id=1, source_target_pairs={{0,1},{1,0},{2,3},{3,2},{4,5},{5,4},{6,7},{7,6},{8,9},{9,8},{10,11... | collective-permute-start | bytes 3145736 | tf_op jit(solution)/shard_map/ppermute | solution.py:514
  105.6 24.3 %collective-permute-start.19 = (bf16[512,1024]{1,0:T(8,128)(2,1)S(1)}, bf16[512,1024]{1,0:T(8,128)(2,1)}, u32[]{:S(2)}, u32[]{:S(2)}) collective-permute-start(bf16[512,1024]{1,0:T(8,128)(2,1)S(1)} %collective-permute-done.17.refs_15_), channel_id=1, source_target_pairs={{0,16},{1,9},{2,18},{3,11},{4,20},{5,13},{6,22},{7,15},{8,24},{9,1... | collective-permute-start | bytes 3145736 | tf_op jit(solution)/shard_map/ppermute | solution.py:514
  106.0 68.8 %collective-permute-start.20 = (bf16[512,1024]{1,0:T(8,128)(2,1)}, bf16[512,1024]{1,0:T(8,128)(2,1)}, u32[]{:S(2)}, u32[]{:S(2)}) collective-permute-start(bf16[512,1024]{1,0:T(8,128)(2,1)} %shard_map.239.refs_14_), channel_id=1, source_target_pairs={{0,1},{1,0},{2,3},{3,2},{4,5},{5,4},{6,7},{7,6},{8,9},{9,8},{10,11... | collective-permute-start | bytes 3145736 | tf_op jit(solution)/shard_map/ppermute | solution.py:514
  106.0 68.3 %collective-permute-start.16 = (bf16[256,2048]{1,0:T(8,128)(2,1)S(1)}, bf16[256,2048]{1,0:T(8,128)(2,1)}, u32[]{:S(2)}, u32[]{:S(2)}) collective-permute-start(bf16[256,2048]{1,0:T(8,128)(2,1)S(1)} %collective-permute-done.12.refs_9_), channel_id=1, source_target_pairs={{0,1},{1,0},{2,3},{3,2},{4,5},{5,4},{6,7},{7,6},{8,9},{9,8},{10,11... | collective-permute-start | bytes 3145736 | tf_op jit(solution)/shard_map/ppermute | solution.py:514
  106.5 68.3 %collective-permute-start.21 = (bf16[512,1024]{1,0:T(8,128)(2,1)S(1)}, bf16[512,1024]{1,0:T(8,128)(2,1)}, u32[]{:S(2)}, u32[]{:S(2)}) collective-permute-start(bf16[512,1024]{1,0:T(8,128)(2,1)S(1)} %collective-permute-done.17.refs_15_), channel_id=1, source_target_pairs={{0,1},{1,0},{2,3},{3,2},{4,5},{5,4},{6,7},{7,6},{8,9},{9,8},{10,11... | collective-permute-start | bytes 3145736 | tf_op jit(solution)/shard_map/ppermute | solution.py:514
  118.7 56.1 %collective-permute-start.22 = (bf16[512,1024]{1,0:T(8,128)(2,1)}, bf16[512,1024]{1,0:T(8,128)(2,1)}, u32[]{:S(2)}, u32[]{:S(2)}) collective-permute-start(bf16[512,1024]{1,0:T(8,128)(2,1)} %collective-permute-done.18.refs_16_), channel_id=1, source_target_pairs={{0,1},{1,0},{2,3},{3,2},{4,5},{5,4},{6,7},{7,6},{8,9},{9,8},{10,11... | collective-permute-start | bytes 3145736 | tf_op jit(solution)/shard_map/ppermute | solution.py:514
  130.0 44.8 %collective-permute-start.23 = (bf16[512,1024]{1,0:T(8,128)(2,1)}, bf16[512,1024]{1,0:T(8,128)(2,1)}, u32[]{:S(2)}, u32[]{:S(2)}) collective-permute-start(bf16[512,1024]{1,0:T(8,128)(2,1)} %collective-permute-done.19.refs_17_), channel_id=1, source_target_pairs={{0,1},{1,0},{2,3},{3,2},{4,5},{5,4},{6,7},{7,6},{8,9},{9,8},{10,11... | collective-permute-start | bytes 3145736 | tf_op jit(solution)/shard_map/ppermute | solution.py:514
  174.3 102.2 %collective-permute-start.33 = (bf16[576,1024]{1,0:T(8,128)(2,1)}, bf16[576,1024]{1,0:T(8,128)(2,1)}, u32[]{:S(2)}, u32[]{:S(2)}) collective-permute-start(bf16[576,1024]{1,0:T(8,128)(2,1)} %get-tuple-element.72.a_own), channel_id=1, source_target_pairs={{0,1},{1,0},{2,3},{3,2},{4,5},{5,4},{6,7},{7,6},{8,9},{9,8},{10,11... | collective-permute-start | bytes 3538952 | tf_op jit(solution)/shard_map/ppermute | solution.py:514
  215.2 63.5 %collective-permute-start.34 = (bf16[576,1024]{1,0:T(8,128)(2,1)}, bf16[576,1024]{1,0:T(8,128)(2,1)S(1)}, u32[]{:S(2)}, u32[]{:S(2)}) collective-permute-start(bf16[576,1024]{1,0:T(8,128)(2,1)} %get-tuple-element.66.refs_1_.b_own), channel_id=1, source_target_pairs={{0,1},{1,0},{2,3},{3,2},{4,5},{5,4},{6,7},{7,6},{8,9},{9,8},{10,11... | collective-permute-start | bytes 3538952 | tf_op jit(solution)/shard_map/ppermute | solution.py:514
  250.7 52.2 %collective-permute-start.25 = (bf16[576,1536]{1,0:T(8,128)(2,1)}, bf16[576,1536]{1,0:T(8,128)(2,1)S(1)}, u32[]{:S(2)}, u32[]{:S(2)}) collective-permute-start(bf16[576,1536]{1,0:T(8,128)(2,1)} %get-tuple-element.69.refs_3_), channel_id=1, source_target_pairs={{0,1},{1,0},{2,3},{3,2},{4,5},{5,4},{6,7},{7,6},{8,9},{9,8},{10,11... | collective-permute-start | bytes 5308424 | tf_op jit(solution)/shard_map/ppermute | solution.py:514
  251.2 64.3 %collective-permute-start.43 = (bf16[576,2048]{1,0:T(8,128)(2,1)}, bf16[576,2048]{1,0:T(8,128)(2,1)}, u32[]{:S(2)}, u32[]{:S(2)}) collective-permute-start(bf16[576,2048]{1,0:T(8,128)(2,1)} %get-tuple-element.74), channel_id=1, source_target_pairs={{0,1},{1,0},{2,3},{3,2},{4,5},{5,4},{6,7},{7,6},{8,9},{9,8},{10,11... | collective-permute-start | bytes 7077896 | tf_op jit(solution)/shard_map/ppermute | solution.py:514
  276.5 21.7 %collective-permute-start.24 = (bf16[576,1024]{1,0:T(8,128)(2,1)}, bf16[576,1024]{1,0:T(8,128)(2,1)}, u32[]{:S(2)}, u32[]{:S(2)}) collective-permute-start(bf16[576,1024]{1,0:T(8,128)(2,1)} %get-tuple-element.56.refs_1_.a_own), channel_id=1, source_target_pairs={{0,1},{1,0},{2,3},{3,2},{4,5},{5,4},{6,7},{7,6},{8,9},{9,8},{10,11... | collective-permute-start | bytes 3538952 | tf_op jit(solution)/shard_map/ppermute | solution.py:514
  285.2 49.1 %collective-permute-start.51 = (bf16[576,2048]{1,0:T(8,128)(2,1)}, bf16[576,2048]{1,0:T(8,128)(2,1)}, u32[]{:S(2)}, u32[]{:S(2)}) collective-permute-start(bf16[576,2048]{1,0:T(8,128)(2,1)} %get-tuple-element.85), channel_id=1, source_target_pairs={{0,1},{1,0},{2,3},{3,2},{4,5},{5,4},{6,7},{7,6},{8,9},{9,8},{10,11... | collective-permute-start | bytes 7077896 | tf_op jit(solution)/shard_map/ppermute | solution.py:514
  290.7 23.1 %collective-permute-start.42 = (bf16[576,1024]{1,0:T(8,128)(2,1)}, bf16[576,1024]{1,0:T(8,128)(2,1)}, u32[]{:S(2)}, u32[]{:S(2)}) collective-permute-start(bf16[576,1024]{1,0:T(8,128)(2,1)} %get-tuple-element.59.refs_2_.a_own), channel_id=1, source_target_pairs={{0,1},{1,0},{2,3},{3,2},{4,5},{5,4},{6,7},{7,6},{8,9},{9,8},{10,11... | collective-permute-start | bytes 3538952 | tf_op jit(solution)/shard_map/ppermute | solution.py:514
  303.5 30.5 %collective-permute-start.52 = (bf16[576,1024]{1,0:T(8,128)(2,1)}, bf16[576,1024]{1,0:T(8,128)(2,1)}, u32[]{:S(2)}, u32[]{:S(2)}) collective-permute-start(bf16[576,1024]{1,0:T(8,128)(2,1)} %get-tuple-element.60.refs_3_.b_own), channel_id=1, source_target_pairs={{0,1},{1,0},{2,3},{3,2},{4,5},{5,4},{6,7},{7,6},{8,9},{9,8},{10,11... | collective-permute-start | bytes 3538952 | tf_op jit(solution)/shard_map/ppermute | solution.py:514
  311.7 44.8 %collective-permute-start.26 = (bf16[2,256,1536]{2,1,0:T(8,128)(2,1)S(1)}, bf16[2,256,1536]{2,1,0:T(8,128)(2,1)}, u32[]{:S(2)}, u32[]{:S(2)}) collective-permute-start(bf16[2,256,1536]{2,1,0:T(8,128)(2,1)S(1)} %shard_map.244), channel_id=1, source_target_pairs={{0,8},{1,17},{2,10},{3,19},{4,12},{5,21},{6,14},{7,23},{8,0},{9,25... | collective-permute-start | bytes 4718600 | tf_op jit(solution)/shard_map/ppermute | solution.py:514
  313.9 16.7 %collective-permute-start.37 = (bf16[128,512]{1,0:T(8,128)(2,1)S(1)}, bf16[128,512]{1,0:T(8,128)(2,1)S(1)}, u32[]{:S(2)}, u32[]{:S(2)}) collective-permute-start(bf16[128,512]{1,0:T(8,128)(2,1)S(1)} %constant_dynamic-slice_fusion.2), channel_id=1, source_target_pairs={{0,2},{1,3},{2,0},{3,1},{4,6},{5,7},{6,4},{7,5},{8,10},{9,11},{10,... | collective-permute-start | bytes 393224 | tf_op jit(solution)/shard_map/ppermute | solution.py:514
  323.8 36.1 %collective-permute-start.44 = (bf16[2,256,2048]{2,1,0:T(8,128)(2,1)S(1)}, bf16[2,256,2048]{2,1,0:T(8,128)(2,1)}, u32[]{:S(2)}, u32[]{:S(2)}) collective-permute-start(bf16[2,256,2048]{2,1,0:T(8,128)(2,1)S(1)} %shard_map.248), channel_id=1, source_target_pairs={{0,8},{1,17},{2,10},{3,19},{4,12},{5,21},{6,14},{7,23},{8,0},{9,25... | collective-permute-start | bytes 6291464 | tf_op jit(solution)/shard_map/ppermute | solution.py:514
  330.6 153.1 %collective-permute-start.64 = (f32[16,1024]{1,0:T(8,128)}, f32[16,1024]{1,0:T(8,128)S(1)}, u32[]{:S(2)}, u32[]{:S(2)}) collective-permute-start(f32[16,1024]{1,0:T(8,128)} %add.140), channel_id=1, source_target_pairs={{0,4},{1,5},{2,6},{3,7},{4,0},{5,1},{6,2},{7,3},{8,12},{9,13},{10,... | collective-permute-start | bytes 196616 | tf_op jit(solution)/shard_map/ppermute | solution.py:514
  333.9 148.7 %collective-permute-start.38 = (bf16[128,512]{1,0:T(8,128)(2,1)}, bf16[128,512]{1,0:T(8,128)(2,1)S(1)}, u32[]{:S(2)}, u32[]{:S(2)}) collective-permute-start(bf16[128,512]{1,0:T(8,128)(2,1)} %add_convert_fusion.11), channel_id=1, source_target_pairs={{0,4},{1,5},{2,6},{3,7},{4,0},{5,1},{6,2},{7,3},{8,12},{9,13},{10,... | collective-permute-start | bytes 393224 | tf_op jit(solution)/shard_map/ppermute | solution.py:514
  340.5 53.9 %collective-permute-start.53 = (bf16[2,512,1024]{2,1,0:T(8,128)(2,1)S(1)}, bf16[2,512,1024]{2,1,0:T(8,128)(2,1)S(1)}, u32[]{:S(2)}, u32[]{:S(2)}) collective-permute-start(bf16[2,512,1024]{2,1,0:T(8,128)(2,1)S(1)} %shard_map.253), channel_id=1, source_target_pairs={{0,8},{1,17},{2,10},{3,19},{4,12},{5,21},{6,14},{7,23},{8,0},{9,25... | collective-permute-start | bytes 6291464 | tf_op jit(solution)/shard_map/ppermute | solution.py:514
  358.4 38.3 %collective-permute-start.27 = (bf16[256,1536]{1,0:T(8,128)(2,1)S(1)}, bf16[256,1536]{1,0:T(8,128)(2,1)S(1)}, u32[]{:S(2)}, u32[]{:S(2)}) collective-permute-start(bf16[256,1536]{1,0:T(8,128)(2,1)S(1)} %slice_bitcast_fusion.4), channel_id=1, source_target_pairs={{0,16},{1,9},{2,18},{3,11},{4,20},{5,13},{6,22},{7,15},{8,24},{9,1... | collective-permute-start | bytes 2359304 | tf_op jit(solution)/shard_map/ppermute | solution.py:514
  362.6 34.3 %collective-permute-start.45 = (bf16[256,2048]{1,0:T(8,128)(2,1)S(1)}, bf16[256,2048]{1,0:T(8,128)(2,1)S(1)}, u32[]{:S(2)}, u32[]{:S(2)}) collective-permute-start(bf16[256,2048]{1,0:T(8,128)(2,1)S(1)} %slice_bitcast_fusion.2), channel_id=1, source_target_pairs={{0,16},{1,9},{2,18},{3,11},{4,20},{5,13},{6,22},{7,15},{8,24},{9,1... | collective-permute-start | bytes 3145736 | tf_op jit(solution)/shard_map/ppermute | solution.py:514
  397.3 16.5 %collective-permute-start.46 = (bf16[128,2048]{1,0:T(8,128)(2,1)S(1)}, bf16[128,2048]{1,0:T(8,128)(2,1)S(1)}, u32[]{:S(2)}, u32[]{:S(2)}) collective-permute-start(bf16[128,2048]{1,0:T(8,128)(2,1)S(1)} %constant_dynamic-slice_fusion.1), channel_id=1, source_target_pairs={{0,2},{1,3},{2,0},{3,1},{4,6},{5,7},{6,4},{7,5},{8,10},{9,11},{10,... | collective-permute-start | bytes 1572872 | tf_op jit(solution)/shard_map/ppermute | solution.py:514
  410.9 26.8 %collective-permute-start.55 = (bf16[256,1024]{1,0:T(8,128)(2,1)S(1)}, bf16[256,1024]{1,0:T(8,128)(2,1)S(1)}, u32[]{:S(2)}, u32[]{:S(2)}) collective-permute-start(bf16[256,1024]{1,0:T(8,128)(2,1)S(1)} %constant_dynamic-slice_fusion), channel_id=1, source_target_pairs={{0,2},{1,3},{2,0},{3,1},{4,6},{5,7},{6,4},{7,5},{8,10},{9,11},{10,... | collective-permute-start | bytes 1572872 | tf_op jit(solution)/shard_map/ppermute | solution.py:514
  413.7 29.6 %collective-permute-start.28 = (bf16[128,1536]{1,0:T(8,128)(2,1)S(1)}, bf16[128,1536]{1,0:T(8,128)(2,1)S(1)}, u32[]{:S(2)}, u32[]{:S(2)}) collective-permute-start(bf16[128,1536]{1,0:T(8,128)(2,1)S(1)} %constant_dynamic-slice_fusion.3), channel_id=1, source_target_pairs={{0,2},{1,3},{2,0},{3,1},{4,6},{5,7},{6,4},{7,5},{8,10},{9,11},{10,... | collective-permute-start | bytes 1179656 | tf_op jit(solution)/shard_map/ppermute | solution.py:514
  413.9 31.8 %collective-permute-start.47 = (bf16[128,2048]{1,0:T(8,128)(2,1)S(1)}, bf16[128,2048]{1,0:T(8,128)(2,1)S(1)}, u32[]{:S(2)}, u32[]{:S(2)}) collective-permute-start(bf16[128,2048]{1,0:T(8,128)(2,1)S(1)} %add_convert_fusion.6), channel_id=1, source_target_pairs={{0,4},{1,5},{2,6},{3,7},{4,0},{5,1},{6,2},{7,3},{8,12},{9,13},{10,... | collective-permute-start | bytes 1572872 | tf_op jit(solution)/shard_map/ppermute | solution.py:514
  437.9 37.3 %collective-permute-start.56 = (bf16[256,1024]{1,0:T(8,128)(2,1)S(1)}, bf16[256,1024]{1,0:T(8,128)(2,1)S(1)}, u32[]{:S(2)}, u32[]{:S(2)}) collective-permute-start(bf16[256,1024]{1,0:T(8,128)(2,1)S(1)} %add_convert_fusion.4), channel_id=1, source_target_pairs={{0,4},{1,5},{2,6},{3,7},{4,0},{5,1},{6,2},{7,3},{8,12},{9,13},{10,... | collective-permute-start | bytes 1572872 | tf_op jit(solution)/shard_map/ppermute | solution.py:514
  443.4 39.0 %collective-permute-start.29 = (bf16[128,1536]{1,0:T(8,128)(2,1)S(1)}, bf16[128,1536]{1,0:T(8,128)(2,1)S(1)}, u32[]{:S(2)}, u32[]{:S(2)}) collective-permute-start(bf16[128,1536]{1,0:T(8,128)(2,1)S(1)} %add_convert_fusion.9), channel_id=1, source_target_pairs={{0,4},{1,5},{2,6},{3,7},{4,0},{5,1},{6,2},{7,3},{8,12},{9,13},{10,... | collective-permute-start | bytes 1179656 | tf_op jit(solution)/shard_map/ppermute | solution.py:514
  445.9 39.8 %collective-permute-start.48 = (bf16[128,2048]{1,0:T(8,128)(2,1)S(1)}, bf16[128,2048]{1,0:T(8,128)(2,1)S(1)}, u32[]{:S(2)}, u32[]{:S(2)}) collective-permute-start(bf16[128,2048]{1,0:T(8,128)(2,1)S(1)} %add_convert_fusion.5.g0), channel_id=1, source_target_pairs={{0,2},{1,3},{2,0},{3,1},{4,6},{5,7},{6,4},{7,5},{8,10},{9,11},{10,... | collective-permute-start | bytes 1572872 | tf_op jit(solution)/shard_map/ppermute | solution.py:514
  475.4 30.9 %collective-permute-start.57 = (bf16[256,1024]{1,0:T(8,128)(2,1)S(1)}, bf16[256,1024]{1,0:T(8,128)(2,1)S(1)}, u32[]{:S(2)}, u32[]{:S(2)}) collective-permute-start(bf16[256,1024]{1,0:T(8,128)(2,1)S(1)} %add_convert_fusion.3.g0), channel_id=1, source_target_pairs={{0,2},{1,3},{2,0},{3,1},{4,6},{5,7},{6,4},{7,5},{8,10},{9,11},{10,... | collective-permute-start | bytes 1572872 | tf_op jit(solution)/shard_map/ppermute | solution.py:514
  482.5 26.2 %collective-permute-start.30 = (bf16[128,1536]{1,0:T(8,128)(2,1)S(1)}, bf16[128,1536]{1,0:T(8,128)(2,1)S(1)}, u32[]{:S(2)}, u32[]{:S(2)}) collective-permute-start(bf16[128,1536]{1,0:T(8,128)(2,1)S(1)} %add_convert_fusion.8.g0), channel_id=1, source_target_pairs={{0,2},{1,3},{2,0},{3,1},{4,6},{5,7},{6,4},{7,5},{8,10},{9,11},{10,... | collective-permute-start | bytes 1179656 | tf_op jit(solution)/shard_map/ppermute | solution.py:514
  482.6 26.4 %collective-permute-start.49 = (bf16[128,2048]{1,0:T(8,128)(2,1)S(1)}, bf16[128,2048]{1,0:T(8,128)(2,1)}, u32[]{:S(2)}, u32[]{:S(2)}) collective-permute-start(bf16[128,2048]{1,0:T(8,128)(2,1)S(1)} %add_convert_fusion.5.g0), channel_id=1, source_target_pairs={{0,1},{1,0},{2,3},{3,2},{4,5},{5,4},{6,7},{7,6},{8,9},{9,8},{10,11... | collective-permute-start | bytes 1572872 | tf_op jit(solution)/shard_map/ppermute | solution.py:514
  483.7 21.1 %collective-permute-start.39 = (bf16[128,512]{1,0:T(8,128)(2,1)S(1)}, bf16[128,512]{1,0:T(8,128)(2,1)S(1)}, u32[]{:S(2)}, u32[]{:S(2)}) collective-permute-start(bf16[128,512]{1,0:T(8,128)(2,1)S(1)} %add_convert_fusion.10.g0), channel_id=1, source_target_pairs={{0,2},{1,3},{2,0},{3,1},{4,6},{5,7},{6,4},{7,5},{8,10},{9,11},{10,... | collective-permute-start | bytes 393224 | tf_op jit(solution)/shard_map/ppermute | solution.py:514
  485.7 24.3 %collective-permute-start.50 = (bf16[128,2048]{1,0:T(8,128)(2,1)S(1)}, bf16[128,2048]{1,0:T(8,128)(2,1)}, u32[]{:S(2)}, u32[]{:S(2)}) collective-permute-start(bf16[128,2048]{1,0:T(8,128)(2,1)S(1)} %collective-permute-done.48.g1), channel_id=1, source_target_pairs={{0,1},{1,0},{2,3},{3,2},{4,5},{5,4},{6,7},{7,6},{8,9},{9,8},{10,11... | collective-permute-start | bytes 1572872 | tf_op jit(solution)/shard_map/ppermute | solution.py:514
  506.2 31.1 %collective-permute-start.58 = (bf16[256,1024]{1,0:T(8,128)(2,1)S(1)}, bf16[256,1024]{1,0:T(8,128)(2,1)}, u32[]{:S(2)}, u32[]{:S(2)}) collective-permute-start(bf16[256,1024]{1,0:T(8,128)(2,1)S(1)} %add_convert_fusion.3.g0), channel_id=1, source_target_pairs={{0,1},{1,0},{2,3},{3,2},{4,5},{5,4},{6,7},{7,6},{8,9},{9,8},{10,11... | collective-permute-start | bytes 1572872 | tf_op jit(solution)/shard_map/ppermute | solution.py:514
  506.3 30.9 %collective-permute-start.59 = (bf16[256,1024]{1,0:T(8,128)(2,1)S(1)}, bf16[256,1024]{1,0:T(8,128)(2,1)}, u32[]{:S(2)}, u32[]{:S(2)}) collective-permute-start(bf16[256,1024]{1,0:T(8,128)(2,1)S(1)} %collective-permute-done.57.g1), channel_id=1, source_target_pairs={{0,1},{1,0},{2,3},{3,2},{4,5},{5,4},{6,7},{7,6},{8,9},{9,8},{10,11... | collective-permute-start | bytes 1572872 | tf_op jit(solution)/shard_map/ppermute | solution.py:514
  508.8 41.7 %collective-permute-start.31 = (bf16[128,1536]{1,0:T(8,128)(2,1)S(1)}, bf16[128,1536]{1,0:T(8,128)(2,1)S(1)}, u32[]{:S(2)}, u32[]{:S(2)}) collective-permute-start(bf16[128,1536]{1,0:T(8,128)(2,1)S(1)} %add_convert_fusion.8.g0), channel_id=1, source_target_pairs={{0,1},{1,0},{2,3},{3,2},{4,5},{5,4},{6,7},{7,6},{8,9},{9,8},{10,11... | collective-permute-start | bytes 1179656 | tf_op jit(solution)/shard_map/ppermute | solution.py:514
  509.0 41.4 %collective-permute-start.32 = (bf16[128,1536]{1,0:T(8,128)(2,1)S(1)}, bf16[128,1536]{1,0:T(8,128)(2,1)}, u32[]{:S(2)}, u32[]{:S(2)}) collective-permute-start(bf16[128,1536]{1,0:T(8,128)(2,1)S(1)} %collective-permute-done.30.g1), channel_id=1, source_target_pairs={{0,1},{1,0},{2,3},{3,2},{4,5},{5,4},{6,7},{7,6},{8,9},{9,8},{10,11... | collective-permute-start | bytes 1179656 | tf_op jit(solution)/shard_map/ppermute | solution.py:514
  510.0 19.2 %collective-permute-start.41 = (bf16[128,512]{1,0:T(8,128)(2,1)S(1)}, bf16[128,512]{1,0:T(8,128)(2,1)S(1)}, u32[]{:S(2)}, u32[]{:S(2)}) collective-permute-start(bf16[128,512]{1,0:T(8,128)(2,1)S(1)} %collective-permute-done.39.g1), channel_id=1, source_target_pairs={{0,1},{1,0},{2,3},{3,2},{4,5},{5,4},{6,7},{7,6},{8,9},{9,8},{10,11... | collective-permute-start | bytes 393224 | tf_op jit(solution)/shard_map/ppermute | solution.py:514
  (76 other events, 1841.9 us)

commit v2 on v1

--- a/solution.py
+++ b/solution.py
@@ -82,32 +82,116 @@
     return jnp.where(place == want, 1.0, 0.0).astype(bf16)
 
 
-def pack_kernel(buf, info, keep, tokens, cot, v0, v1, v2, v3, x_out, em_out, h_out, vec_out, vec):
-    step = pl.program_id(0)
-    part = v0.shape[1]
-
-    @pl.when(step == 0)
-    def _():
-        for flip, piece in enumerate((v0, v1, v2, v3)):
-            place = pl.multiple_of((info[0] ^ flip) * part, part)
-            vec[0:12, pl.ds(place, part)] = piece[...].astype(f32)
-
-    vec_out[...] = vec[...]
-    rows = x_out.shape[0]
-    pick = picker(keep[0], rows - buf)
-    for src, dst in ((tokens, x_out), (cot, em_out)):
-        dst[0:buf, :] = src[0, 0:buf, :]
-        dst[buf:rows, :] = mm(pick, src[0, buf:, :]).astype(bf16)
-    normal, _ = layer_stats(x_out[...].astype(f32))
-    h_out[...] = (normal * vec[0:1, :] + vec[1:2, :]).astype(bf16)
-
-
-def pieces_of(info, e):
-    core = info[1] ^ e
-    first = core + 1
-    second = 3 - first
-    group = info[0]
-    return core, (group, group ^ first, group ^ second, group ^ 3)
+MESH = pl.DeviceIdType.MESH
+
+
+def flip(value, bit):
+    return value + bit - 2 * bit * ((value // bit) % 2)
+
+
+class Place:
+    def __init__(self):
+        self.group, self.replica = lax.axis_index("group"), lax.axis_index("dp")
+        self.core, self.level = self.replica % 2, (self.replica // 2) % 2
+        one, two = flip(self.group, 1), flip(self.group, 2)
+        self.first = (1 - self.core) * one + self.core * two
+        self.second = (1 - self.core) * two + self.core * one
+        self.third = flip(one, 2)
+        self.to_first = (self.first, self.replica)
+        self.to_second = (self.second, self.replica)
+        self.to_third = (self.third, self.replica)
+        self.to_core = (self.group, flip(self.replica, 1))
+
+    def to_bit(self, bit):
+        return (self.group, flip(self.replica, bit))
+
+    def meet(self, partners):
+        barrier = pltpu.get_barrier_semaphore()
+        for partner in partners:
+            pl.semaphore_signal(barrier, inc=1, device_id=partner, device_id_type=MESH)
+        pl.semaphore_wait(barrier, len(partners))
+
+
+class Gather:
+    def __init__(self, place, own, full, send, recv):
+        self.place, self.own, self.full, self.send, self.recv = place, own, full, send, recv
+        deep = own.shape[0]
+        self.deep, self.strip = deep, 5 * deep // 16
+        self.main = deep - self.strip
+        self.main_at = place.level * self.strip
+        self.strip_at = place.level * self.main
+
+    def block(self, owner, start, size):
+        at = pl.multiple_of(owner * self.deep + start, 16)
+        return self.full.at[self.place.core, pl.ds(at, size), :]
+
+    def make(self, k, owner, start, size, device):
+        view = self.block(owner, start, size)
+        return pltpu.make_async_remote_copy(
+            src_ref=view, dst_ref=view, send_sem=self.send.at[k], recv_sem=self.recv.at[k],
+            device_id=device, device_id_type=MESH,
+        )
+
+    def plan(self, k):
+        p = self.place
+        main, strip, whole = (self.main_at, self.main), (self.strip_at, self.strip), (0, self.deep)
+        return (
+            (p.group, *main, p.to_first),
+            (p.group, *main, p.to_second),
+            (p.first, *main, p.to_second),
+            (p.first, *strip, p.to_bit(2)),
+            (p.second, *strip, p.to_bit(2)),
+            (p.third, *strip, p.to_bit(2)),
+            (p.group, *whole, p.to_core),
+            (p.first, *whole, p.to_core),
+            (p.second, *whole, p.to_core),
+            (p.third, *whole, p.to_core),
+        )[k]
+
+    def start(self, *ks):
+        for k in ks:
+            owner, at, size, device = self.plan(k)
+            if k in (0, 1, 6):
+                start = pl.multiple_of(at, 16) if k < 6 else 0
+                pltpu.make_async_remote_copy(
+                    src_ref=self.own.at[pl.ds(start, size), :], dst_ref=self.block(owner, at, size),
+                    send_sem=self.send.at[k], recv_sem=self.recv.at[k], device_id=device, device_id_type=MESH,
+                ).start()
+            else:
+                self.make(k, owner, at, size, device).start()
+
+    def arrived(self, *ks):
+        for k in ks:
+            self.make(k, *self.plan(k)).wait_recv()
+
+    def sent(self, *ks):
+        for k in ks:
+            self.make(k, *self.plan(k)).wait_send()
+
+    def step_one(self):
+        self.start(0, 1, 6)
+
+    def step_two(self):
+        self.arrived(0)
+        self.start(2, 3)
+        self.arrived(1)
+        self.start(4)
+
+    def step_three(self):
+        self.arrived(2)
+        self.start(5)
+        self.arrived(3)
+        self.start(7)
+        self.arrived(4)
+        self.start(8)
+
+    def step_four(self):
+        self.arrived(5)
+        self.start(9)
+
+    def step_five(self):
+        self.arrived(6, 7, 8, 9)
+        self.sent(*range(10))
 
 
 def head_masks():
@@ -134,75 +218,152 @@
     return exponent / jnp.sum(exponent, axis=-1, keepdims=True)
 
 
-def fetch_attn(info, pieces, wbuf, sems, start, width):
-    copies = []
-    for e in range(2):
-        _, owners = pieces_of(info, e)
-        for k in range(4):
-            src = pieces[4 * e + k]
-            rows = src.shape[0]
-            copies.append(
-                pltpu.make_async_copy(
-                    src.at[:, pl.ds(start, width)],
-                    wbuf.at[e, pl.ds(pl.multiple_of(owners[k] * rows, rows), rows), :],
-                    sems.at[e, k],
-                )
-            )
-    for one in copies:
-        one.start()
-    return copies
-
-
-def attend_kernel(seqs, *refs):
-    info, h1, x, vec = refs[:4]
-    pieces = refs[4:12]
-    qkv, o, r, h2, stats, wbuf, sems = refs[12:]
+def fetch(src, buf, sem, start, width):
+    copy = pltpu.make_async_copy(src.at[:, :, pl.ds(start, width)], buf, sem)
+    copy.start()
+    return copy
+
+
+def attend_kernel(seqs, buf, *refs):
+    counts, keep, vectors, mats, down, tokens, cot = refs[:7]
+    w_attn, w_up, w_down, x, em, h1, vec, qkv, o, r, h2, stats = refs[7:19]
+    wbuf, wide, tall, low_up, low_down, rows_in, parts, send, recv, vec_send, vec_recv, loads, stores, reads = refs[19:]
     rows = h1.shape[0] // seqs
     d = h1.shape[1]
     half = d // 2
-    copies = fetch_attn(info, pieces, wbuf, sems, 0, 4 * half)
-    for e in range(2):
-        core, _ = pieces_of(info, e)
-        for one in copies[4 * e : 4 * e + 4]:
-            one.wait()
-
-        @pl.loop(0, 2)
-        def _(t):
-            near = pl.multiple_of(core * half + t * (half // 2), half // 2)
-            for j in range(3):
-                w = wbuf[e, :, pl.ds(pl.multiple_of(j * half + t * (half // 2), half // 2), half // 2)]
-                got = mm(h1[...], w)
-                if j != 1:
-                    got = got + vec[2 + j // 2 : 3 + j // 2, pl.ds(near, half // 2)]
-                qkv[:, pl.ds(pl.multiple_of(j * d + near, half // 2), half // 2)] = got.astype(bf16)
-
+    place = Place()
+    core = place.core
+    deep = mats.shape[0]
+
+    takes = []
+    for j in range(8):
+        at = pl.ds(pl.multiple_of((2 * j + core) * half, half), half)
+        takes.append(
+            pltpu.make_async_copy(mats.at[:, at], wide.at[j // 4, :, pl.ds((j % 4) * half, half)], loads.at[j])
+        )
+    takes.append(
+        pltpu.make_async_copy(down.at[pl.ds(pl.multiple_of(core * half, half), half), :], tall, loads.at[8])
+    )
+    for one in takes:
+        one.start()
+    reads_in = []
+    for n in range(seqs):
+        for k, src in enumerate((tokens, cot)):
+            reads_in.append(pltpu.make_async_copy(src.at[n], rows_in.at[k, n], reads.at[k, n]))
+    for one in reads_in:
+        one.start()
+
+    place.meet((place.to_first, place.to_second, place.to_third, place.to_core, place.to_bit(2)))
+
+    part = vectors.shape[1]
+    parts[place.group] = jnp.concatenate([vectors[...], jnp.zeros((4, part), f32)], axis=0).astype(bf16)
+    for k, partner in enumerate((place.to_first, place.to_second, place.to_third)):
+        pltpu.make_async_remote_copy(
+            src_ref=parts.at[place.group], dst_ref=parts.at[place.group],
+            send_sem=vec_send.at[k], recv_sem=vec_recv.at[k], device_id=partner, device_id_type=MESH,
+        ).start()
+
+    for one in takes[:4]:
+        one.wait()
+    own = wbuf.at[core, pl.ds(pl.multiple_of(place.group * deep, deep), deep), :]
+    own[...] = wide[0].astype(bf16)
+    attn = Gather(place, own, wbuf, send.at[0], recv.at[0])
+    attn.step_one()
+    for one in takes[4:]:
+        one.wait()
+    low_up[...] = wide[1].astype(bf16)
+    low_down[...] = tall[...].astype(bf16)
+    up = Gather(place, low_up, w_up, send.at[1], recv.at[1])
+    downs = Gather(place, low_down, w_down, send.at[2], recv.at[2])
+    keep_up = pltpu.make_async_copy(low_up, up.block(place.group, 0, deep), stores.at[0])
+    keep_down = pltpu.make_async_copy(low_down, downs.block(place.group, 0, half), stores.at[1])
+    keep_up.start()
+    keep_down.start()
+
+    for one in reads_in:
+        one.wait()
+
+    @pl.loop(0, seqs)
+    def _(n):
+        at = pl.multiple_of(n * rows, 16)
+        pick = picker(keep[n], rows - buf)
+        for k, dst in ((0, x), (1, em)):
+            dst[pl.ds(at, buf), :] = rows_in[k, n, 0:buf, :]
+            dst[pl.ds(pl.multiple_of(at + buf, 16), rows - buf), :] = mm(pick, rows_in[k, n, buf:, :]).astype(bf16)
+
+    attn.step_two()
+    for k, partner in enumerate((place.first, place.second, place.third)):
+        got = pltpu.make_async_remote_copy(
+            src_ref=parts.at[place.group], dst_ref=parts.at[place.group],
+            send_sem=vec_send.at[k], recv_sem=vec_recv.at[k], device_id=place.to_first, device_id_type=MESH,
+        )
+        got.wait()
+    vec[...] = jnp.zeros_like(vec)
+    for s in range(4):
+        vec[:, s * part : (s + 1) * part] = parts[s].astype(f32)
+
+    @pl.loop(0, seqs)
+    def _(n):
+        at = pl.ds(pl.multiple_of(n * rows, 16), rows)
+        normal, _ = layer_stats(x[at, :].astype(f32))
+        h1[at, :] = (normal * vec[0:1, :] + vec[1:2, :]).astype(bf16)
+
+    up.step_one()
+    attn.step_three()
+    attn.step_four()
+    attn.step_five()
+    keep_attn = pltpu.make_async_copy(wbuf, w_attn, stores.at[2])
+    keep_attn.start()
+
+    @pl.loop(0, 4)
+    def _(i):
+        h, t = i // 2, i % 2
+        tile = half // 2
+        near = pl.multiple_of(i * tile, tile)
+        for j in range(3):
+            w = wbuf[h, :, pl.ds(pl.multiple_of(j * half + t * tile, tile), tile)]
+            got = mm(h1[...], w)
+            if j != 1:
+                got = got + vec[2 + j // 2 : 3 + j // 2, pl.ds(near, tile)]
+            qkv[:, pl.ds(pl.multiple_of(j * d + near, tile), tile)] = got.astype(bf16)
+
+    up.step_two()
+    downs.step_one()
     low, high, first = head_masks()
     pairs = d // (2 * HEAD)
+    steps = {
+        4: up.step_three,
+        8: up.step_four,
+        12: downs.step_two,
+        20: downs.step_three,
+        26: downs.step_four,
+    }
 
     @pl.loop(0, seqs * pairs)
     def _(i):
+        for when, step in steps.items():
+            pl.when(i == when)(step)
         n, j = i // pairs, i % pairs
         at = pl.ds(pl.multiple_of(n * rows, 16), rows)
         lanes = [pl.ds(pl.multiple_of(j * 2 * HEAD + m * d, 2 * HEAD), 2 * HEAD) for m in range(3)]
         q_pair = two_heads(qkv[at, lanes[0]], low, high)
-        probs = pair_probs(q_pair, qkv[at, lanes[1]], info[4 + n]).astype(bf16)
+        probs = pair_probs(q_pair, qkv[at, lanes[1]], counts[n]).astype(bf16)
         o[at, lanes[0]] = pick_heads(mm(probs, qkv[at, lanes[2]]), first).astype(bf16)
 
-    for e in range(2):
-        core, _ = pieces_of(info, e)
-
-        @pl.loop(0, 2)
-        def _(t):
-            near = pl.ds(pl.multiple_of(core * half + t * (half // 2), half // 2), half // 2)
-            w = wbuf[e, :, pl.ds(pl.multiple_of(3 * half + t * (half // 2), half // 2), half // 2)]
-            r[:, near] = mm(o[...], w) + vec[4:5, near]
+    @pl.loop(0, 4)
+    def _(i):
+        h, t = i // 2, i % 2
+        tile = half // 2
+        near = pl.ds(pl.multiple_of(i * tile, tile), tile)
+        w = wbuf[h, :, pl.ds(pl.multiple_of(3 * half + t * tile, tile), tile)]
+        r[:, near] = mm(o[...], w) + vec[4:5, near]
 
     stats[...] = jnp.zeros_like(stats)
 
     @pl.loop(0, seqs)
     def _(n):
         at = pl.ds(pl.multiple_of(n * rows, 16), rows)
-        valid = lax.broadcasted_iota(jnp.int32, (rows, 1), 0) < info[4 + n]
+        valid = lax.broadcasted_iota(jnp.int32, (rows, 1), 0) < counts[n]
         valid = jnp.where(valid, 1.0, 0.0)
         inputs = x[at, :].astype(f32)
         branch = r[at, :]
@@ -213,40 +374,34 @@
         stats[0:1, :] += jnp.sum(inputs * inputs * valid, axis=0, keepdims=True)
         stats[1:2, :] += jnp.sum(branch * branch * valid, axis=0, keepdims=True)
 
+    up.step_five()
+    downs.step_five()
+    keep_up.wait()
+    keep_down.wait()
+    keep_attn.wait()
+
 
 def feed_kernel(seqs, buf, *refs):
-    info, keep, h2, em, r, vec = refs[:6]
-    ups, downs = refs[6:14], refs[14:22]
-    z_mine, z_yours, u_mine, u_yours, er, ea, out, sums = refs[22:30]
-    wup, wdown, m_acc, t_acc, sem_up, sem_down = refs[30:]
+    info, keep, h2, em, r, vec, ups, downs = refs[:8]
+    z_mine, z_yours, u_mine, u_yours, er, ea, out, sums = refs[8:16]
+    wup, wdown, m_acc, t_acc, sems = refs[16:]
     rows = h2.shape[0] // seqs
     d = h2.shape[1]
     strip = wup.shape[2] // 4
     tile = strip // 2
-    copies = [[], []]
+    copies = []
     for e in range(2):
-        _, owners = pieces_of(info, e)
-        for k in range(4):
-            src = ups[4 * e + k]
-            deep = src.shape[0]
-            copies[e].append(
-                pltpu.make_async_copy(
-                    src,
-                    wup.at[e, pl.ds(pl.multiple_of(owners[k] * deep, deep), deep), :],
-                    sem_up.at[e, k],
-                )
-            )
-            copies[e].append(
-                pltpu.make_async_copy(downs[4 * e + k], wdown.at[e, owners[k]], sem_down.at[e, k])
-            )
-        for one in copies[e]:
-            one.start()
+        core = info[1] ^ e
+        copies.append(pltpu.make_async_copy(ups.at[core], wup.at[e], sems.at[e, 0]))
+        copies.append(pltpu.make_async_copy(downs.at[core], wdown.at[e], sems.at[e, 1]))
+    for one in copies:
+        one.start()
     sums[...] = jnp.zeros_like(sums)
     m_acc[...] = jnp.zeros_like(m_acc)
     t_acc[...] = jnp.zeros_like(t_acc)
     for e, z_out, u_out in ((0, z_mine, u_mine), (1, z_yours, u_yours)):
-        core, _ = pieces_of(info, e)
-        for one in copies[e]:
+        core = info[1] ^ e
+        for one in copies[2 * e : 2 * e + 2]:
             one.wait()
 
         @pl.loop(0, 8)
@@ -255,7 +410,7 @@
             near = pl.ds(pl.multiple_of(i * tile, tile), tile)
             far = (pl.ds(8 + s, 1), pl.ds(pl.multiple_of(core * strip + t * tile, tile), tile))
             w_up = wup[e, :, near]
-            w_down = wdown[e, s, pl.ds(pl.multiple_of(t * tile, tile), tile), :]
+            w_down = wdown[e, near, :]
             u = mm(h2[...], w_up) + vec[far]
             phi = 0.5 * (1.0 + lax.erf(u * root_half))
             z = (u * phi).astype(bf16)
@@ -293,33 +448,24 @@
 
 
 def back_kernel(seqs, *refs):
-    info, ea, qkv = refs[:3]
-    pieces = refs[3:11]
-    mine, yours, sums, wbuf, eo, sems = refs[11:]
+    info, ea, qkv, w_attn, mine, yours, sums, wbuf, eo, sem = refs
     rows = ea.shape[0] // seqs
     d = ea.shape[1]
     half = d // 2
-    copies = fetch_attn(info, pieces, wbuf, sems, 3 * half, half)
-    for one in copies:
-        one.wait()
+    fetch(w_attn, wbuf, sem, 3 * half, half).wait()
 
     @pl.loop(0, 4)
     def _(s):
         near = pl.ds(pl.multiple_of(s * (d // 4), d // 4), d // 4)
-        total = None
-        for e in range(2):
-            core, _ = pieces_of(info, e)
-            part = ea[:, pl.ds(pl.multiple_of(core * half, half), half)]
-            got = mm_nt(part, wbuf[e, near, :])
-            total = got if total is None else total + got
-        eo[:, near] = total.astype(bf16)
+        got = mm_nt(ea[:, 0:half], wbuf[0, near, :]) + mm_nt(ea[:, half:], wbuf[1, near, :])
+        eo[:, near] = got.astype(bf16)
 
     low, high, first = head_masks()
     pairs = half // (2 * HEAD)
     scale = 1.0 / math.sqrt(HEAD)
     sums[...] = jnp.zeros_like(sums)
     for e, dst in ((0, mine), (1, yours)):
-        core, _ = pieces_of(info, e)
+        core = info[1] ^ e
 
         @pl.loop(0, seqs * pairs)
         def _(i):
@@ -344,20 +490,17 @@
 
 
 def input_kernel(seqs, buf, *refs):
-    info, keep, mine, yours, x, er, vec = refs[:7]
-    pieces = refs[7:15]
-    out, sums, wbuf, t_acc, sems = refs[15:]
+    info, keep, mine, yours, x, er, vec, w_attn, out, sums, wbuf, t_acc, sem = refs
     rows = x.shape[0] // seqs
     d = x.shape[1]
     half = d // 2
-    copies = fetch_attn(info, pieces, wbuf, sems, 0, 3 * half)
-    for one in copies:
-        one.wait()
+    fetch(w_attn, wbuf, sem, 0, 3 * half).wait()
+    core = info[1]
 
     @pl.loop(0, 4)
     def _(s):
         near = pl.ds(pl.multiple_of(s * (d // 4), d // 4), d // 4)
-        t_acc[:, near] = mm_nt(mine[...], wbuf[0, near, :]) + mm_nt(yours[...], wbuf[1, near, :])
+        t_acc[:, near] = mm_nt(mine[...], wbuf[core, near, :]) + mm_nt(yours[...], wbuf[1 - core, near, :])
 
     sums[...] = jnp.zeros_like(sums)
 
@@ -451,43 +594,6 @@
     )(info, *state, *quarters, *extra)
 
 
-def cast_kernel(info, src, out):
-    out[...] = src[...].astype(bf16)
-
-
-def half_strips(info, matrix, start, count):
-    deep = matrix.shape[0]
-    strip = 512
-    return pl.pallas_call(
-        cast_kernel,
-        grid_spec=pltpu.PrefetchScalarGridSpec(
-            num_scalar_prefetch=1,
-            grid=(count,),
-            in_specs=[pl.BlockSpec((deep, strip), lambda j, info: (0, 2 * (start + j) + info[1]))],
-            out_specs=pl.BlockSpec((deep, strip), lambda j, info: (0, j)),
-        ),
-        out_shape=sds((deep, strip * count), bf16),
-        compiler_params=params(16),
-        cost_estimate=cost(deep * strip * count, 6 * deep * strip * count),
-    )(info, matrix)
-
-
-def half_rows(info, matrix):
-    deep, wide = matrix.shape[0] // 2, matrix.shape[1]
-    return pl.pallas_call(
-        cast_kernel,
-        grid_spec=pltpu.PrefetchScalarGridSpec(
-            num_scalar_prefetch=1,
-            grid=(2,),
-            in_specs=[pl.BlockSpec((deep // 2, wide), lambda j, info: (2 * info[1] + j, 0))],
-            out_specs=pl.BlockSpec((deep // 2, wide), lambda j, info: (j, 0)),
-        ),
-        out_shape=sds((deep, wide), bf16),
-        compiler_params=params(16),
-        cost_estimate=cost(deep * wide, 6 * deep * wide),
-    )(info, matrix)
-
-
 def add_low(a, b):
     return (a.astype(f32) + b.astype(f32)).astype(bf16)
 
@@ -518,66 +624,51 @@
     swap = lambda v: permute(v, lambda a, b: (a, b ^ 1))
     shift = lambda v, bit: permute(v, lambda a, b: (a, b ^ bit))
 
-    low_vectors = vectors.astype(bf16)
-    vec_parts = [low_vectors] + [
-        permute(low_vectors, functools.partial(lambda flip, a, b: (a ^ flip, b), flip)) for flip in (1, 2, 3)
-    ]
-
-    def gather(own):
-        one = hop_one(own)
-        two = hop_two(own)
-        three = hop_two(one)
-        mine = [own, one, two, three]
-        return mine + [swap(v) for v in mine]
-
-    own_attn = half_strips(info, mats, 0, 4)
-    own_up = half_strips(info, mats, 4, 4)
-    own_down = half_rows(info, down)
-    w_attn = gather(own_attn)
-    own_up, own_down, _ = lax.optimization_barrier((own_up, own_down, w_attn[3]))
-    w_up = gather(own_up)
-    own_down, _ = lax.optimization_barrier((own_down, w_up[3]))
-    w_down = gather(own_down)
-
     keep3 = keep.reshape(seqs, 1, image)
-    x, em, h1, vec = pl.pallas_call(
-        functools.partial(pack_kernel, buf),
-        grid_spec=pltpu.PrefetchScalarGridSpec(
-            num_scalar_prefetch=1,
-            grid=(seqs,),
-            in_specs=[pl.BlockSpec((1, 1, image), lambda n, info: (n, 0, 0))]
-            + [pl.BlockSpec((1, length, d), lambda n, info: (n, 0, 0))] * 2
-            + [pl.BlockSpec((12, vectors.shape[1]), lambda n, info: (0, 0))] * 4,
-            out_specs=[pl.BlockSpec((rows, d), lambda n, info: (n, 0))] * 3
-            + [pl.BlockSpec((16, d), lambda n, info: (0, 0))],
-            scratch_shapes=[pltpu.VMEM((16, d), f32)],
-        ),
-        out_shape=[sds((total, d), bf16)] * 3 + [sds((16, d), f32)],
-        compiler_params=params(40),
-        cost_estimate=cost(8 * total * image * d, 10 * total * d),
-    )(info, keep3, tokens, cot, *vec_parts)
-    h1_got, em_got = swap(h1), swap(em)
-
-    qkv, o, r, h2, stats = pl.pallas_call(
-        functools.partial(attend_kernel, seqs),
-        in_specs=[SMEM_SPEC] + [VMEM_SPEC] * 3 + [ANY_SPEC] * 8,
-        out_specs=[VMEM_SPEC] * 5,
+    deep = mats.shape[0]
+    w_attn, w_up, w_down, x, em, h1, vec, qkv, o, r, h2, stats = pl.pallas_call(
+        functools.partial(attend_kernel, seqs, buf),
+        in_specs=[SMEM_SPEC] + [VMEM_SPEC] * 2 + [ANY_SPEC] * 4,
+        out_specs=[ANY_SPEC] * 3 + [VMEM_SPEC] * 9,
         out_shape=[
+            sds((2, d, 2 * d), bf16),
+            sds((2, d, 2 * d), bf16),
+            sds((2, 2 * d, d), bf16),
+            sds((total, d), bf16),
+            sds((total, d), bf16),
+            sds((total, d), bf16),
+            sds((16, d), f32),
             sds((total, 3 * d), bf16),
             sds((total, d), bf16),
             sds((total, d), f32),
             sds((total, d), bf16),
             sds((8, d), f32),
         ],
-        scratch_shapes=[pltpu.VMEM((2, d, 2 * d), bf16), pltpu.SemaphoreType.DMA((2, 4))],
-        compiler_params=params(56),
-        cost_estimate=cost(2 * total * 4 * d * d * 1.5, 20 * total * d),
-    )(info, h1, x, vec, *w_attn)
+        scratch_shapes=[
+            pltpu.VMEM((2, d, 2 * d), bf16),
+            pltpu.VMEM((2, deep, 2 * d), f32),
+            pltpu.VMEM((half, d), f32),
+            pltpu.VMEM((deep, 2 * d), bf16),
+            pltpu.VMEM((half, d), bf16),
+            pltpu.VMEM((2, seqs, length, d), bf16),
+            pltpu.VMEM((4, 16, d // 4), bf16),
+            pltpu.SemaphoreType.DMA((3, 10)),
+            pltpu.SemaphoreType.DMA((3, 10)),
+            pltpu.SemaphoreType.DMA((3,)),
+            pltpu.SemaphoreType.DMA((3,)),
+            pltpu.SemaphoreType.DMA((9,)),
+            pltpu.SemaphoreType.DMA((3,)),
+            pltpu.SemaphoreType.DMA((2, seqs)),
+        ],
+        compiler_params=params(60, collective_id=0, has_side_effects=True),
+        cost_estimate=cost(2 * total * 4 * d * d * 4, 20 * total * d),
+    )(counts.astype(jnp.int32), keep3, vectors, mats, down, tokens, cot)
+    h1_got, em_got = swap(h1), swap(em)
     o_got, h2_got = swap(o), swap(h2)
 
     z_mine, z_yours, u_mine, u_yours, er, ea, block_output, sums_feed = pl.pallas_call(
         functools.partial(feed_kernel, seqs, buf),
-        in_specs=[SMEM_SPEC] + [VMEM_SPEC] * 5 + [ANY_SPEC] * 16,
+        in_specs=[SMEM_SPEC] + [VMEM_SPEC] * 5 + [ANY_SPEC] * 2,
         out_specs=[VMEM_SPEC] * 8,
         out_shape=[sds((total, 2 * d), bf16)] * 4
         + [
@@ -588,15 +679,14 @@
         ],
         scratch_shapes=[
             pltpu.VMEM((2, d, 2 * d), bf16),
-            pltpu.VMEM((2, 4, half, d), bf16),
+            pltpu.VMEM((2, 2 * d, d), bf16),
             pltpu.VMEM((total, d), f32),
             pltpu.VMEM((total, d), f32),
-            pltpu.SemaphoreType.DMA((2, 4)),
-            pltpu.SemaphoreType.DMA((2, 4)),
+            pltpu.SemaphoreType.DMA((2, 2)),
         ],
         compiler_params=params(60),
         cost_estimate=cost(2 * total * 16 * d * d, 60 * total * d),
-    )(info, keep3, h2, em, r, vec, *w_up, *w_down)
+    )(info, keep3, h2, em, r, vec, w_up, w_down)
 
     z_got, u_got, ea_got = swap(z_yours), swap(u_yours), swap(ea)
 
@@ -633,17 +723,17 @@
 
     e_mine, e_yours, sums_back = pl.pallas_call(
         functools.partial(back_kernel, seqs),
-        in_specs=[SMEM_SPEC] + [VMEM_SPEC] * 2 + [ANY_SPEC] * 8,
+        in_specs=[SMEM_SPEC] + [VMEM_SPEC] * 2 + [ANY_SPEC],
         out_specs=[VMEM_SPEC] * 3,
         out_shape=[sds((total, 3 * half), bf16)] * 2 + [sds((8, d), f32)],
         scratch_shapes=[
             pltpu.VMEM((2, d, half), bf16),
             pltpu.VMEM((total, d), bf16),
-            pltpu.SemaphoreType.DMA((2, 4)),
+            pltpu.SemaphoreType.DMA(()),
         ],
         compiler_params=params(48),
         cost_estimate=cost(2 * total * 4 * d * d, 20 * total * d),
-    )(info, ea, qkv, *w_attn)
+    )(info, ea, qkv, w_attn)
     e_got = swap(e_yours)
     g_qkv = reduce_blocks(
         lambda order: weight_grad(order, h1, h1_got, e_mine, e_got, d // 4, 3 * half, half)
@@ -651,17 +741,17 @@
 
     input_grad, sums_in = pl.pallas_call(
         functools.partial(input_kernel, seqs, buf),
-        in_specs=[SMEM_SPEC] + [VMEM_SPEC] * 6 + [ANY_SPEC] * 8,
+        in_specs=[SMEM_SPEC] + [VMEM_SPEC] * 6 + [ANY_SPEC],
         out_specs=[VMEM_SPEC] * 2,
         out_shape=[sds((seqs, length, d), f32), sds((8, d), f32)],
         scratch_shapes=[
             pltpu.VMEM((2, d, 3 * half), bf16),
             pltpu.VMEM((total, d), f32),
-            pltpu.SemaphoreType.DMA((2, 4)),
+            pltpu.SemaphoreType.DMA(()),
         ],
         compiler_params=params(56),
         cost_estimate=cost(2 * total * 3 * d * d, 20 * total * d),
-    )(info, keep3, e_mine, e_yours, x, er, vec, *w_attn)
+    )(info, keep3, e_mine, e_yours, x, er, vec, w_attn)
 
     squares = jnp.stack([jnp.sum(stats[0]), jnp.sum(stats[1]), jnp.sum(sums_feed[12]), jnp.sum(counts).astype(f32)])
     small = jnp.concatenate(

time: 565 us -> 512 us (0.906)
  waiting for transfers between devices: 225 us -> 142 us
  Pallas kernels: 221 us -> 299 us
  starting transfers between devices: 66.4 us -> 28.2 us
  local copies, waits for them, and re-layouts: 26.4 us -> 17.3 us
    ppermute x65 -> x41, waiting for transfers between devices: 225 us -> 142 us  [permute(): return lax.ppermute(value, BOTH, pairs)]
    pallas_call x5 -> x1, Pallas kernels: 40.4 us -> 119 us  [local(): pl.pallas_call(functools.partial(attend_kernel, seqs, buf), in_specs=[SME...]
    ppermute x65 -> x41, starting transfers between devices: 66.4 us -> 28.2 us  [permute(): return lax.ppermute(value, BOTH, pairs)]
    unnamed x118 -> x52, local copies, waits for them, and re-layouts: 23.8 us -> 13 us
  transfers between devices with their start and end apart: 65 -> 41, of which waited for: 22 -> 13; matrix products, arithmetic and copies ran while one was open for 4% -> 4% of each run, Pallas kernels for 37% -> 25%
where the time goes in v2:
time: 512 us; the launch traced here: 510 us
  Pallas kernels  299 us (58%)
  waiting for transfers between devices  142 us (28%)
  starting transfers between devices  28.2 us (6%)
  other arithmetic  21 us (4%)
  local copies, waits for them, and re-layouts  17.3 us (3%)
    ppermute x41, waiting for transfers between devices, permute(): return lax.ppermute(value, BOTH, pairs)  142 us
    pallas_call x1, Pallas kernels, local(): pl.pallas_call(functools.partial(attend_kernel, seqs, buf), in_specs=[SME...  119 us
    pallas_call x8, Pallas kernels, weight_grad(): pl.pallas_call(grad_kernel, grid_spec=pltpu.PrefetchScalarGridSpec(num_sc...  46.9 us
    pallas_call x4, Pallas kernels, adam_call(): pl.pallas_call(adam_kernel, grid_spec=pltpu.PrefetchScalarGridSpec(num_sc...  43.8 us
    pallas_call x1, Pallas kernels, local(): pl.pallas_call(functools.partial(feed_kernel, seqs, buf), in_specs=[SMEM_...  40.2 us
    pallas_call x1, Pallas kernels, local(): pl.pallas_call(functools.partial(back_kernel, seqs), in_specs=[SMEM_SPEC]...  32.7 us
    ppermute x41, starting transfers between devices, permute(): return lax.ppermute(value, BOTH, pairs)  28.2 us
    pallas_call x1, Pallas kernels, local(): pl.pallas_call(functools.partial(input_kernel, seqs, buf), in_specs=[SMEM...  16.6 us
  transfers between devices with their start and end apart: 41, of which 13 were waited for; matrix products, arithmetic and copies ran while one was open for 4% of the time, Pallas kernels for 25%

profile of v2, /device:TPU:0, one launch (start us, length us, event | category | flops | bytes accessed | tf_op | source)
XLA Modules:
  0.0 510.0 jit_solution(14645298282149020559)
XLA Ops:
  1.5 1.3 reshape.49.refs_1_
  4.0 119.0 %shard_map.235 = (bf16[2,1024,2048]{2,1,0:T(8,128)(2,1)}, bf16[2,1024,2048]{2,1,0:T(8,128)(2,1)}, bf16[2,2048,1024]{2,1,0:T(8,128)(2,1)}, bf16[576,1024]{1,0:T(8...) custom-call(s32[4]{0:T(128)} %copy-done.23, ...), custom_call_target="tpu_custom_call" | custom-call | flops 19327352832 | bytes 11796480 | tf_op jit(solution)/shard_map/pallas_call | solution.py:629
  123.0 40.2 %shard_map.236 = (bf16[576,2048]{1,0:T(8,128)(2,1)}, bf16[576,2048]{1,0:T(8,128)(2,1)}, bf16[576,2048]{1,0:T(8,128)(2,1)}, bf16[576,2048]{1,0:T(8,128)(2,1)}, f3...) custom-call(s32[8]{0:T(128)} %concatenate.6.refs_0_.info, ...), custom_call_target="tpu_custom_call" | custom-call | flops 19327352832 | bytes 35389440 | tf_op jit(solution)/shard_map/pallas_call | solution.py:669
  163.4 1.3 copy-done.6
  164.7 32.7 %shard_map.237 = (bf16[576,1536]{1,0:T(8,128)(2,1)S(1)}, bf16[576,1536]{1,0:T(8,128)(2,1)}, f32[8,1024]{1,0:T(8,128)S(1)}) custom-call(s32[8]{0:T(128)S(1)} %copy-done.15, bf16[576,1024]{1,0:T(8,128)(2,1)S(1)} %copy-done.6, bf16[576,3072]{1,0:T(8,128)(2,1)} %get-tuple-element.64.refs_2_, bf16[2,1024,2048]{2,1,0:T(8,128)(2,1)} %get-tuple-element.65.refs_3_.refs_7_), custom_call_target="tpu_custom_call" | custom-call | flops 4831838208 | bytes 11796480 | tf_op jit(solution)/shard_map/pallas_call | solution.py:724
  200.3 16.6 %shard_map.238 = (f32[4,320,1024]{2,1,0:T(8,128)}, f32[8,1024]{1,0:T(8,128)}) custom-call(s32[8]{0:T(128)} %concatenate.6.refs_0_.info, s32[4,1,256]{2,1,0:T(1,128)} %reshape.49.refs_1_, bf16[576,1536]{1,0:T(8,128)(2,1)} %copy-done.1, bf16[576,1536]{1,0:T(8,128)(2,1)} %get-tuple-element.67.refs_3_, bf16[576,1024]{1,0:T(8,128)(2,1)} %get-tuple-element.68.refs_4_, ...), custom_call_target="tpu_custom_call" | custom-call | flops 3623878656 | bytes 11796480 | tf_op jit(solution)/shard_map/pallas_call | solution.py:742
  217.6 1.4 slice_reduce_fusion.2
  219.7 2.0 maximum_bitcast_fusion
  221.7 1.5 collective-permute-start.36
  223.2 2.8 collective-permute-done.36
  226.3 4.2 collective-permute-done.37
  230.6 1.3 copy-done.7
  231.8 2.9 shard_map.242
  234.7 1.5 collective-permute-start.11
  236.9 4.8 collective-permute-done.39
  241.7 2.4 collective-permute-done.11
  244.2 1.3 copy-done.8
  245.4 3.1 shard_map.241
  248.6 1.3 add_convert_fusion.7
  250.7 1.6 collective-permute-start.28
  252.3 1.5 add.140
  253.8 6.0 %shard_map.240 = bf16[2,256,1536]{2,1,0:T(8,128)(2,1)S(1)} custom-call(s32[3]{0:T(128)S(1)} %add_add_fusion.1.order, bf16[576,1024]{1,0:T(8,128)(2,1)} %get-tuple-element.71.a_own, bf16[576,1024]{1,0:T(8,128)(2,1)} %collective-permute-done.a_got, bf16[576,1536]{1,0:T(8,128)(2,1)S(1)} %copy-done.2, bf16[576,1536]{1,0:T(8,128)(2,1)S(1)} %collective-permute-done.1.b_got), custom_call_target="tpu_custom_call" | custom-call | flops 1811939328 | bytes 4718592 | tf_op jit(solution)/shard_map/pallas_call | solution.py:534
  262.0 8.3 %shard_map.244 = bf16[2,256,2048]{2,1,0:T(8,128)(2,1)S(1)} custom-call(s32[3]{0:T(128)S(1)} %add_add_fusion.1.order, bf16[576,1024]{1,0:T(8,128)(2,1)} %get-tuple-element.56.refs_2_.a_own, bf16[576,1024]{1,0:T(8,128)(2,1)} %collective-permute-done.18.a_got, bf16[576,2048]{1,0:T(8,128)(2,1)S(1)} %copy-done.4, bf16[576,2048]{1,0:T(8,128)(2,1)} %collective-permute-done.19.b_got), custom_call_target="tpu_custom_call" | custom-call | flops 2415919104 | bytes 5898240 | tf_op jit(solution)/shard_map/pallas_call | solution.py:534
  271.5 5.7 %shard_map.239 = bf16[2,256,1536]{2,1,0:T(8,128)(2,1)S(1)} custom-call(s32[3]{0:T(128)S(1)} %add_add_fusion.order, bf16[576,1024]{1,0:T(8,128)(2,1)} %get-tuple-element.71.a_own, bf16[576,1024]{1,0:T(8,128)(2,1)} %collective-permute-done.a_got, bf16[576,1536]{1,0:T(8,128)(2,1)S(1)} %copy-done.2, bf16[576,1536]{1,0:T(8,128)(2,1)S(1)} %collective-permute-done.1.b_got), custom_call_target="tpu_custom_call" | custom-call | flops 1811939328 | bytes 4718592 | tf_op jit(solution)/shard_map/pallas_call | solution.py:534
  277.2 2.7 collective-permute-start.40
  280.9 6.3 %shard_map.249 = bf16[2,512,1024]{2,1,0:T(8,128)(2,1)S(1)} custom-call(s32[3]{0:T(128)S(1)} %add_add_fusion.1.order, bf16[576,2048]{1,0:T(8,128)(2,1)S(1)} %copy-done.3, bf16[576,2048]{1,0:T(8,128)(2,1)} %collective-permute-done.27.a_got, bf16[576,1024]{1,0:T(8,128)(2,1)} %get-tuple-element.57.refs_3_.b_own, bf16[576,1024]{1,0:T(8,128)(2,1)} %collective-permute-done.28.b_got), custom_call_target="tpu_custom_call" | custom-call | flops 2415919104 | bytes 4718592 | tf_op jit(solution)/shard_map/pallas_call | solution.py:534
  288.2 8.3 %shard_map.243 = bf16[2,256,2048]{2,1,0:T(8,128)(2,1)S(1)} custom-call(s32[3]{0:T(128)S(1)} %add_add_fusion.order, bf16[576,1024]{1,0:T(8,128)(2,1)} %get-tuple-element.56.refs_2_.a_own, bf16[576,1024]{1,0:T(8,128)(2,1)} %collective-permute-done.18.a_got, bf16[576,2048]{1,0:T(8,128)(2,1)S(1)} %copy-done.4, bf16[576,2048]{1,0:T(8,128)(2,1)} %collective-permute-done.19.b_got), custom_call_target="tpu_custom_call" | custom-call | flops 2415919104 | bytes 5898240 | tf_op jit(solution)/shard_map/pallas_call | solution.py:534
  296.5 6.3 %shard_map.248 = bf16[2,512,1024]{2,1,0:T(8,128)(2,1)S(1)} custom-call(s32[3]{0:T(128)S(1)} %add_add_fusion.order, bf16[576,2048]{1,0:T(8,128)(2,1)S(1)} %copy-done.3, bf16[576,2048]{1,0:T(8,128)(2,1)} %collective-permute-done.27.a_got, bf16[576,1024]{1,0:T(8,128)(2,1)} %get-tuple-element.57.refs_3_.b_own, bf16[576,1024]{1,0:T(8,128)(2,1)} %collective-permute-done.28.b_got), custom_call_target="tpu_custom_call" | custom-call | flops 2415919104 | bytes 4718592 | tf_op jit(solution)/shard_map/pallas_call | solution.py:534
  302.8 1.8 add_convert_fusion.2
  305.6 2.5 add_convert_fusion.1
  309.4 35.2 %collective-permute-done.29 = bf16[2,512,1024]{2,1,0:T(8,128)(2,1)S(1)} collective-permute-done((bf16[2,512,1024]{2,1,0:T(8,128)(2,1)S(1)}, bf16[2,512,1024]{2,1,0:T(8,128)(2,1)S(1)}, u32[]{:S(2)}, u32[]{:S(2)}) %collective-permute-start.29) | collective-permute-done | bytes 2097184 | tf_op jit(solution)/shard_map/ppermute | solution.py:620
  346.5 14.0 %collective-permute-done.30 = bf16[512,1024]{1,0:T(8,128)(2,1)S(1)} collective-permute-done((bf16[512,1024]{1,0:T(8,128)(2,1)S(1)}, bf16[512,1024]{1,0:T(8,128)(2,1)S(1)}, u32[]{:S(2)}, u32[]{:S(2)}) %collective-permute-start.30) | collective-permute-done | bytes 1048608 | tf_op jit(solution)/shard_map/ppermute | solution.py:620
  361.1 2.1 collective-permute-start.4
  363.3 2.7 collective-permute-start.23
  366.0 20.5 %collective-permute-done.31 = bf16[256,1024]{1,0:T(8,128)(2,1)S(1)} collective-permute-done((bf16[256,1024]{1,0:T(8,128)(2,1)S(1)}, bf16[256,1024]{1,0:T(8,128)(2,1)S(1)}, u32[]{:S(2)}, u32[]{:S(2)}) %collective-permute-start.31) | collective-permute-done | bytes 524320 | tf_op jit(solution)/shard_map/ppermute | solution.py:620
  386.7 5.4 %collective-permute-done.4 = bf16[128,1536]{1,0:T(8,128)(2,1)S(1)} collective-permute-done((bf16[128,1536]{1,0:T(8,128)(2,1)S(1)}, bf16[128,1536]{1,0:T(8,128)(2,1)S(1)}, u32[]{:S(2)}, u32[]{:S(2)}) %collective-permute-start.4) | collective-permute-done | bytes 393248 | tf_op jit(solution)/shard_map/ppermute | solution.py:620
  393.3 5.2 %collective-permute-start.24 = (bf16[128,2048]{1,0:T(8,128)(2,1)S(1)}, bf16[128,2048]{1,0:T(8,128)(2,1)S(1)}, u32[]{:S(2)}, u32[]{:S(2)}) collective-permute-start(bf16[128,2048]{1,0:T(8,128)(2,1)S(1)} %add_convert_fusion.5.g0), channel_id=1, source_target_pairs={{0,2},{1,3},{2,0},{3,1},{4,6},{5,7},{6,4},{7,5},{8,10},{9,11},{10,... | collective-permute-start | bytes 1572872 | tf_op jit(solution)/shard_map/ppermute | solution.py:620
  398.5 25.0 %collective-permute-done.32 = bf16[256,1024]{1,0:T(8,128)(2,1)S(1)} collective-permute-done((bf16[256,1024]{1,0:T(8,128)(2,1)S(1)}, bf16[256,1024]{1,0:T(8,128)(2,1)S(1)}, u32[]{:S(2)}, u32[]{:S(2)}) %collective-permute-start.32) | collective-permute-done | bytes 524320 | tf_op jit(solution)/shard_map/ppermute | solution.py:620
  423.7 6.3 %collective-permute-done.5 = bf16[128,1536]{1,0:T(8,128)(2,1)S(1)} collective-permute-done((bf16[128,1536]{1,0:T(8,128)(2,1)S(1)}, bf16[128,1536]{1,0:T(8,128)(2,1)S(1)}, u32[]{:S(2)}, u32[]{:S(2)}) %collective-permute-start.5) | collective-permute-done | bytes 393248 | tf_op jit(solution)/shard_map/ppermute | solution.py:620
  431.3 2.0 collective-permute-start.15
  433.5 18.9 %collective-permute-done.15.g1 = bf16[128,512]{1,0:T(8,128)(2,1)S(1)} collective-permute-done((bf16[128,512]{1,0:T(8,128)(2,1)S(1)}, bf16[128,512]{1,0:T(8,128)(2,1)S(1)}, u32[]{:S(2)}, u32[]{:S(2)}) %collective-permute-start.15) | collective-permute-done | bytes 131104 | tf_op jit(solution)/shard_map/ppermute | solution.py:620
  452.4 1.3 collective-permute-done.16.g2
  458.3 3.4 copy-done
  461.7 15.1 %shard_map.245 = (f32[256,8192]{1,0:T(8,128)}, f32[256,8192]{1,0:T(8,128)}, f32[256,8192]{1,0:T(8,128)}, bf16[256,8192]{1,0:T(8,128)(2,1)}) custom-call(s32[8]{0:T(128)S(1)} %copy-done.16, f32[256,8192]{1,0:T(8,128)S(1)} %copy-done, f32[256,8192]{1,0:T(8,128)} %f.6, f32[256,8192]{1,0:T(8,128)} %s.6, bf16[128,2048]{1,0:T(8,128)(2,1)S(1)} %add_convert_fusion.5.g0, ...), custom_call_target="tpu_custom_call" | custom-call | flops 20971520 | bytes 29360128 | tf_op jit(solution)/shard_map/pallas_call | solution.py:582
  479.0 5.9 %shard_map.246 = (f32[256,8192]{1,0:T(8,128)}, f32[256,8192]{1,0:T(8,128)}, f32[256,8192]{1,0:T(8,128)}, bf16[256,8192]{1,0:T(8,128)(2,1)}) custom-call(s32[8]{0:T(128)S(1)} %copy-done.16, f32[256,8192]{1,0:T(8,128)S(1)} %copy-done, f32[256,8192]{1,0:T(8,128)} %f.6, ...), custom_call_target="tpu_custom_call", output_to_operand_aliasing={{0}: (8, {}), {1}: (9, {}), {2}: (10, {}), {3}: (11, {})} | custom-call | flops 5242880 | bytes 7340032 | tf_op jit(solution)/shard_map/pallas_call | solution.py:582
  485.0 2.2 copy-done.10
  487.2 11.0 %shard_map.250 = (f32[1024,1024]{1,0:T(8,128)}, f32[1024,1024]{1,0:T(8,128)}, f32[1024,1024]{1,0:T(8,128)}, bf16[1024,1024]{1,0:T(8,128)(2,1)}) custom-call(s32[8]{0:T(128)S(1)} %copy-done.16, f32[1024,1024]{1,0:T(8,128)S(1)} %copy-done.9, f32[1024,1024]{1,0:T(8,128)S(1)} %copy-done.10, f32[1024,1024]{1,0:T(8,128)} %s.7, ...), custom_call_target="tpu_custom_call" | custom-call | flops 20971520 | bytes 29360128 | tf_op jit(solution)/shard_map/pallas_call | solution.py:582
  498.2 11.8 %shard_map.247 = (f32[256,8192]{1,0:T(8,128)}, f32[256,8192]{1,0:T(8,128)}, f32[256,8192]{1,0:T(8,128)}, bf16[256,8192]{1,0:T(8,128)(2,1)}) custom-call(s32[8]{0:T(128)S(1)} %copy-done.16, f32[256,8192]{1,0:T(8,128)S(1)} %bitcast.44, f32[256,8192]{1,0:T(8,128)} %f.6, ...), custom_call_target="tpu_custom_call", output_to_operand_aliasing={{0}: (8, {}), {1}: (9, {}), {2}: (10, {}), {3}: (11, {})} | custom-call | flops 15728640 | bytes 22020096 | tf_op jit(solution)/shard_map/pallas_call | solution.py:582
  (148 shorter events, 27.1 us)
Async XLA Ops:
  123.0 40.4 %copy-start.15 = (s32[8]{0:T(128)S(1)}, s32[8]{0:T(128)}, u32[]{:S(2)}) copy-start(s32[8]{0:T(128)} %concatenate.6.refs_0_.info) | copy-start | bytes 100
  163.3 67.2 %collective-permute-start.10 = (bf16[576,1024]{1,0:T(8,128)(2,1)}, bf16[576,1024]{1,0:T(8,128)(2,1)}, u32[]{:S(2)}, u32[]{:S(2)}) collective-permute-start(bf16[576,1024]{1,0:T(8,128)(2,1)} %get-tuple-element.63.refs_1_.b_own), channel_id=1, source_target_pairs={{0,1},{1,0},{2,3},{3,2},{4,5},{5,4},{6,7},{7,6},{8,9},{9,8},{10,11... | collective-permute-start | bytes 3538952 | tf_op jit(solution)/shard_map/ppermute | solution.py:620
  164.7 34.4 %copy-start.5 = (bf16[576,1024]{1,0:T(8,128)(2,1)S(1)}, bf16[576,1024]{1,0:T(8,128)(2,1)}, u32[]{:S(2)}) copy-start(bf16[576,1024]{1,0:T(8,128)(2,1)} %get-tuple-element.72.a_own) | copy-start | bytes 3538948
  164.7 35.6 %copy-start.19 = (f32[16,1024]{1,0:T(8,128)S(1)}, f32[16,1024]{1,0:T(8,128)}, u32[]{:S(2)}) copy-start(f32[16,1024]{1,0:T(8,128)} %get-tuple-element.89) | copy-start | bytes 196612
  198.6 52.0 %collective-permute-start.1 = (bf16[576,1536]{1,0:T(8,128)(2,1)}, bf16[576,1536]{1,0:T(8,128)(2,1)S(1)}, u32[]{:S(2)}, u32[]{:S(2)}) collective-permute-start(bf16[576,1536]{1,0:T(8,128)(2,1)} %get-tuple-element.67.refs_3_), channel_id=1, source_target_pairs={{0,1},{1,0},{2,3},{3,2},{4,5},{5,4},{6,7},{7,6},{8,9},{9,8},{10,11... | collective-permute-start | bytes 5308424 | tf_op jit(solution)/shard_map/ppermute | solution.py:620
  199.1 31.4 %collective-permute-start.9 = (bf16[576,1024]{1,0:T(8,128)(2,1)S(1)}, bf16[576,1024]{1,0:T(8,128)(2,1)}, u32[]{:S(2)}, u32[]{:S(2)}) collective-permute-start(bf16[576,1024]{1,0:T(8,128)(2,1)S(1)} %copy-done.5), channel_id=1, source_target_pairs={{0,1},{1,0},{2,3},{3,2},{4,5},{5,4},{6,7},{7,6},{8,9},{9,8},{10,11... | collective-permute-start | bytes 3538952 | tf_op jit(solution)/shard_map/ppermute | solution.py:620
  199.1 62.9 %collective-permute-start.19 = (bf16[576,2048]{1,0:T(8,128)(2,1)}, bf16[576,2048]{1,0:T(8,128)(2,1)}, u32[]{:S(2)}, u32[]{:S(2)}) collective-permute-start(bf16[576,2048]{1,0:T(8,128)(2,1)} %get-tuple-element.74), channel_id=1, source_target_pairs={{0,1},{1,0},{2,3},{3,2},{4,5},{5,4},{6,7},{7,6},{8,9},{9,8},{10,11... | collective-permute-start | bytes 7077896 | tf_op jit(solution)/shard_map/ppermute | solution.py:620
  221.7 4.3 collective-permute-start.36
  226.1 4.3 collective-permute-start.37
  230.4 5.8 %collective-permute-start.38 = (f32[16,1024]{1,0:T(8,128)S(1)}, f32[16,1024]{1,0:T(8,128)S(1)}, u32[]{:S(2)}, u32[]{:S(2)}) collective-permute-start(f32[16,1024]{1,0:T(8,128)S(1)} %add.138), channel_id=1, source_target_pairs={{0,1},{1,0},{2,3},{3,2},{4,5},{5,4},{6,7},{7,6},{8,9},{9,8},{10,11... | collective-permute-start | bytes 196616 | tf_op jit(solution)/shard_map/ppermute | solution.py:620
  234.7 9.4 %collective-permute-start.11 = (bf16[2,256,512]{2,1,0:T(8,128)(2,1)S(1)}, bf16[2,256,512]{2,1,0:T(8,128)(2,1)}, u32[]{:S(2)}, u32[]{:S(2)}) collective-permute-start(bf16[2,256,512]{2,1,0:T(8,128)(2,1)S(1)} %shard_map.242), channel_id=1, source_target_pairs={{0,8},{1,17},{2,10},{3,19},{4,12},{5,21},{6,14},{7,23},{8,0},{9,25... | collective-permute-start | bytes 1572872 | tf_op jit(solution)/shard_map/ppermute | solution.py:620
  236.2 14.4 %collective-permute-start = (bf16[576,1024]{1,0:T(8,128)(2,1)}, bf16[576,1024]{1,0:T(8,128)(2,1)}, u32[]{:S(2)}, u32[]{:S(2)}) collective-permute-start(bf16[576,1024]{1,0:T(8,128)(2,1)} %get-tuple-element.71.a_own), channel_id=1, source_target_pairs={{0,1},{1,0},{2,3},{3,2},{4,5},{5,4},{6,7},{7,6},{8,9},{9,8},{10,11... | collective-permute-start | bytes 3538952 | tf_op jit(solution)/shard_map/ppermute | solution.py:620
  236.9 4.8 collective-permute-start.39
  241.7 39.2 %collective-permute-start.27 = (bf16[576,2048]{1,0:T(8,128)(2,1)}, bf16[576,2048]{1,0:T(8,128)(2,1)}, u32[]{:S(2)}, u32[]{:S(2)}) collective-permute-start(bf16[576,2048]{1,0:T(8,128)(2,1)} %get-tuple-element.85), channel_id=1, source_target_pairs={{0,1},{1,0},{2,3},{3,2},{4,5},{5,4},{6,7},{7,6},{8,9},{9,8},{10,11... | collective-permute-start | bytes 7077896 | tf_op jit(solution)/shard_map/ppermute | solution.py:620
  244.1 17.5 %collective-permute-start.18 = (bf16[576,1024]{1,0:T(8,128)(2,1)}, bf16[576,1024]{1,0:T(8,128)(2,1)}, u32[]{:S(2)}, u32[]{:S(2)}) collective-permute-start(bf16[576,1024]{1,0:T(8,128)(2,1)} %get-tuple-element.56.refs_2_.a_own), channel_id=1, source_target_pairs={{0,1},{1,0},{2,3},{3,2},{4,5},{5,4},{6,7},{7,6},{8,9},{9,8},{10,11... | collective-permute-start | bytes 3538952 | tf_op jit(solution)/shard_map/ppermute | solution.py:620
  250.6 9.2 %collective-permute-start.12 = (bf16[256,512]{1,0:T(8,128)(2,1)}, bf16[256,512]{1,0:T(8,128)(2,1)}, u32[]{:S(2)}, u32[]{:S(2)}) collective-permute-start(bf16[256,512]{1,0:T(8,128)(2,1)} %slice_bitcast_fusion.6), channel_id=1, source_target_pairs={{0,16},{1,9},{2,18},{3,11},{4,20},{5,13},{6,22},{7,15},{8,24},{9,1... | collective-permute-start | bytes 786440 | tf_op jit(solution)/shard_map/ppermute | solution.py:620
  250.7 29.9 %collective-permute-start.28 = (bf16[576,1024]{1,0:T(8,128)(2,1)}, bf16[576,1024]{1,0:T(8,128)(2,1)}, u32[]{:S(2)}, u32[]{:S(2)}) collective-permute-start(bf16[576,1024]{1,0:T(8,128)(2,1)} %get-tuple-element.57.refs_3_.b_own), channel_id=1, source_target_pairs={{0,1},{1,0},{2,3},{3,2},{4,5},{5,4},{6,7},{7,6},{8,9},{9,8},{10,11... | collective-permute-start | bytes 3538952 | tf_op jit(solution)/shard_map/ppermute | solution.py:620
  259.8 42.9 %collective-permute-start.2 = (bf16[2,256,1536]{2,1,0:T(8,128)(2,1)S(1)}, bf16[2,256,1536]{2,1,0:T(8,128)(2,1)}, u32[]{:S(2)}, u32[]{:S(2)}) collective-permute-start(bf16[2,256,1536]{2,1,0:T(8,128)(2,1)S(1)} %shard_map.240), channel_id=1, source_target_pairs={{0,8},{1,17},{2,10},{3,19},{4,12},{5,21},{6,14},{7,23},{8,0},{9,25... | collective-permute-start | bytes 4718600 | tf_op jit(solution)/shard_map/ppermute | solution.py:620
  261.6 15.7 %collective-permute-start.13 = (bf16[128,512]{1,0:T(8,128)(2,1)S(1)}, bf16[128,512]{1,0:T(8,128)(2,1)S(1)}, u32[]{:S(2)}, u32[]{:S(2)}) collective-permute-start(bf16[128,512]{1,0:T(8,128)(2,1)S(1)} %constant_dynamic-slice_fusion.2), channel_id=1, source_target_pairs={{0,2},{1,3},{2,0},{3,1},{4,6},{5,7},{6,4},{7,5},{8,10},{9,11},{10,... | collective-permute-start | bytes 393224 | tf_op jit(solution)/shard_map/ppermute | solution.py:620
  270.3 35.3 %collective-permute-start.20 = (bf16[2,256,2048]{2,1,0:T(8,128)(2,1)S(1)}, bf16[2,256,2048]{2,1,0:T(8,128)(2,1)}, u32[]{:S(2)}, u32[]{:S(2)}) collective-permute-start(bf16[2,256,2048]{2,1,0:T(8,128)(2,1)S(1)} %shard_map.244), channel_id=1, source_target_pairs={{0,8},{1,17},{2,10},{3,19},{4,12},{5,21},{6,14},{7,23},{8,0},{9,25... | collective-permute-start | bytes 6291464 | tf_op jit(solution)/shard_map/ppermute | solution.py:620
  277.2 154.0 %collective-permute-start.40 = (f32[16,1024]{1,0:T(8,128)}, f32[16,1024]{1,0:T(8,128)}, u32[]{:S(2)}, u32[]{:S(2)}) collective-permute-start(f32[16,1024]{1,0:T(8,128)} %add.140), channel_id=1, source_target_pairs={{0,4},{1,5},{2,6},{3,7},{4,0},{5,1},{6,2},{7,3},{8,12},{9,13},{10,... | collective-permute-start | bytes 196616 | tf_op jit(solution)/shard_map/ppermute | solution.py:620
  280.6 149.6 %collective-permute-start.14 = (bf16[128,512]{1,0:T(8,128)(2,1)}, bf16[128,512]{1,0:T(8,128)(2,1)}, u32[]{:S(2)}, u32[]{:S(2)}) collective-permute-start(bf16[128,512]{1,0:T(8,128)(2,1)} %add_convert_fusion.11), channel_id=1, source_target_pairs={{0,4},{1,5},{2,6},{3,7},{4,0},{5,1},{6,2},{7,3},{8,12},{9,13},{10,... | collective-permute-start | bytes 393224 | tf_op jit(solution)/shard_map/ppermute | solution.py:620
  287.2 57.3 %collective-permute-start.29 = (bf16[2,512,1024]{2,1,0:T(8,128)(2,1)S(1)}, bf16[2,512,1024]{2,1,0:T(8,128)(2,1)S(1)}, u32[]{:S(2)}, u32[]{:S(2)}) collective-permute-start(bf16[2,512,1024]{2,1,0:T(8,128)(2,1)S(1)} %shard_map.249), channel_id=1, source_target_pairs={{0,8},{1,17},{2,10},{3,19},{4,12},{5,21},{6,14},{7,23},{8,0},{9,25... | collective-permute-start | bytes 6291464 | tf_op jit(solution)/shard_map/ppermute | solution.py:620
  304.6 41.1 %collective-permute-start.3 = (bf16[256,1536]{1,0:T(8,128)(2,1)S(1)}, bf16[256,1536]{1,0:T(8,128)(2,1)S(1)}, u32[]{:S(2)}, u32[]{:S(2)}) collective-permute-start(bf16[256,1536]{1,0:T(8,128)(2,1)S(1)} %slice_bitcast_fusion.4), channel_id=1, source_target_pairs={{0,16},{1,9},{2,18},{3,11},{4,20},{5,13},{6,22},{7,15},{8,24},{9,1... | collective-permute-start | bytes 2359304 | tf_op jit(solution)/shard_map/ppermute | solution.py:620
  308.2 37.7 %collective-permute-start.21 = (bf16[256,2048]{1,0:T(8,128)(2,1)S(1)}, bf16[256,2048]{1,0:T(8,128)(2,1)S(1)}, u32[]{:S(2)}, u32[]{:S(2)}) collective-permute-start(bf16[256,2048]{1,0:T(8,128)(2,1)S(1)} %slice_bitcast_fusion.2), channel_id=1, source_target_pairs={{0,16},{1,9},{2,18},{3,11},{4,20},{5,13},{6,22},{7,15},{8,24},{9,1... | collective-permute-start | bytes 3145736 | tf_op jit(solution)/shard_map/ppermute | solution.py:620
  345.7 14.9 %collective-permute-start.30 = (bf16[512,1024]{1,0:T(8,128)(2,1)S(1)}, bf16[512,1024]{1,0:T(8,128)(2,1)S(1)}, u32[]{:S(2)}, u32[]{:S(2)}) collective-permute-start(bf16[512,1024]{1,0:T(8,128)(2,1)S(1)} %slice_bitcast_fusion), channel_id=1, source_target_pairs={{0,16},{1,9},{2,18},{3,11},{4,20},{5,13},{6,22},{7,15},{8,24},{9,1... | collective-permute-start | bytes 3145736 | tf_op jit(solution)/shard_map/ppermute | solution.py:620
  346.4 16.8 %collective-permute-start.22 = (bf16[128,2048]{1,0:T(8,128)(2,1)S(1)}, bf16[128,2048]{1,0:T(8,128)(2,1)S(1)}, u32[]{:S(2)}, u32[]{:S(2)}) collective-permute-start(bf16[128,2048]{1,0:T(8,128)(2,1)S(1)} %constant_dynamic-slice_fusion.1), channel_id=1, source_target_pairs={{0,2},{1,3},{2,0},{3,1},{4,6},{5,7},{6,4},{7,5},{8,10},{9,11},{10,... | collective-permute-start | bytes 1572872 | tf_op jit(solution)/shard_map/ppermute | solution.py:620
  361.0 25.5 %collective-permute-start.31 = (bf16[256,1024]{1,0:T(8,128)(2,1)S(1)}, bf16[256,1024]{1,0:T(8,128)(2,1)S(1)}, u32[]{:S(2)}, u32[]{:S(2)}) collective-permute-start(bf16[256,1024]{1,0:T(8,128)(2,1)S(1)} %constant_dynamic-slice_fusion), channel_id=1, source_target_pairs={{0,2},{1,3},{2,0},{3,1},{4,6},{5,7},{6,4},{7,5},{8,10},{9,11},{10,... | collective-permute-start | bytes 1572872 | tf_op jit(solution)/shard_map/ppermute | solution.py:620
  361.1 31.0 %collective-permute-start.4 = (bf16[128,1536]{1,0:T(8,128)(2,1)S(1)}, bf16[128,1536]{1,0:T(8,128)(2,1)S(1)}, u32[]{:S(2)}, u32[]{:S(2)}) collective-permute-start(bf16[128,1536]{1,0:T(8,128)(2,1)S(1)} %constant_dynamic-slice_fusion.3), channel_id=1, source_target_pairs={{0,2},{1,3},{2,0},{3,1},{4,6},{5,7},{6,4},{7,5},{8,10},{9,11},{10,... | collective-permute-start | bytes 1179656 | tf_op jit(solution)/shard_map/ppermute | solution.py:620
  363.3 29.8 %collective-permute-start.23 = (bf16[128,2048]{1,0:T(8,128)(2,1)S(1)}, bf16[128,2048]{1,0:T(8,128)(2,1)S(1)}, u32[]{:S(2)}, u32[]{:S(2)}) collective-permute-start(bf16[128,2048]{1,0:T(8,128)(2,1)S(1)} %add_convert_fusion.6), channel_id=1, source_target_pairs={{0,4},{1,5},{2,6},{3,7},{4,0},{5,1},{6,2},{7,3},{8,12},{9,13},{10,... | collective-permute-start | bytes 1572872 | tf_op jit(solution)/shard_map/ppermute | solution.py:620
  386.6 36.8 %collective-permute-start.32 = (bf16[256,1024]{1,0:T(8,128)(2,1)S(1)}, bf16[256,1024]{1,0:T(8,128)(2,1)S(1)}, u32[]{:S(2)}, u32[]{:S(2)}) collective-permute-start(bf16[256,1024]{1,0:T(8,128)(2,1)S(1)} %add_convert_fusion.4), channel_id=1, source_target_pairs={{0,4},{1,5},{2,6},{3,7},{4,0},{5,1},{6,2},{7,3},{8,12},{9,13},{10,... | collective-permute-start | bytes 1572872 | tf_op jit(solution)/shard_map/ppermute | solution.py:620
  392.2 64.8 %copy-start.20 = (f32[12,256]{1,0:T(8,128)S(1)}, f32[12,256]{1,0:T(8,128)}, u32[]{:S(2)}) copy-start(f32[12,256]{1,0:T(8,128)} %refs_2_.1) | copy-start | bytes 36868
  392.2 64.7 %copy-start.21 = (f32[12,256]{1,0:T(8,128)S(1)}, f32[12,256]{1,0:T(8,128)}, u32[]{:S(2)}) copy-start(f32[12,256]{1,0:T(8,128)} %param.20) | copy-start | bytes 36868
  392.2 64.7 %copy-start.22 = (f32[12,256]{1,0:T(8,128)S(1)}, f32[12,256]{1,0:T(8,128)}, u32[]{:S(2)}) copy-start(f32[12,256]{1,0:T(8,128)} %param.23) | copy-start | bytes 36868
  392.2 37.8 %collective-permute-start.5 = (bf16[128,1536]{1,0:T(8,128)(2,1)S(1)}, bf16[128,1536]{1,0:T(8,128)(2,1)S(1)}, u32[]{:S(2)}, u32[]{:S(2)}) collective-permute-start(bf16[128,1536]{1,0:T(8,128)(2,1)S(1)} %add_convert_fusion.9), channel_id=1, source_target_pairs={{0,4},{1,5},{2,6},{3,7},{4,0},{5,1},{6,2},{7,3},{8,12},{9,13},{10,... | collective-permute-start | bytes 1179656 | tf_op jit(solution)/shard_map/ppermute | solution.py:620
  393.3 65.0 %copy-start.16 = (s32[8]{0:T(128)S(1)}, s32[8]{0:T(128)}, u32[]{:S(2)}) copy-start(s32[8]{0:T(128)} %concatenate.6.refs_0_.info) | copy-start | bytes 100
  393.3 40.0 %collective-permute-start.24 = (bf16[128,2048]{1,0:T(8,128)(2,1)S(1)}, bf16[128,2048]{1,0:T(8,128)(2,1)S(1)}, u32[]{:S(2)}, u32[]{:S(2)}) collective-permute-start(bf16[128,2048]{1,0:T(8,128)(2,1)S(1)} %add_convert_fusion.5.g0), channel_id=1, source_target_pairs={{0,2},{1,3},{2,0},{3,1},{4,6},{5,7},{6,4},{7,5},{8,10},{9,11},{10,... | collective-permute-start | bytes 1572872 | tf_op jit(solution)/shard_map/ppermute | solution.py:620
  423.7 30.2 %collective-permute-start.33 = (bf16[256,1024]{1,0:T(8,128)(2,1)S(1)}, bf16[256,1024]{1,0:T(8,128)(2,1)S(1)}, u32[]{:S(2)}, u32[]{:S(2)}) collective-permute-start(bf16[256,1024]{1,0:T(8,128)(2,1)S(1)} %add_convert_fusion.3.g0), channel_id=1, source_target_pairs={{0,2},{1,3},{2,0},{3,1},{4,6},{5,7},{6,4},{7,5},{8,10},{9,11},{10,... | collective-permute-start | bytes 1572872 | tf_op jit(solution)/shard_map/ppermute | solution.py:620
  430.1 26.3 %collective-permute-start.6 = (bf16[128,1536]{1,0:T(8,128)(2,1)S(1)}, bf16[128,1536]{1,0:T(8,128)(2,1)S(1)}, u32[]{:S(2)}, u32[]{:S(2)}) collective-permute-start(bf16[128,1536]{1,0:T(8,128)(2,1)S(1)} %add_convert_fusion.8.g0), channel_id=1, source_target_pairs={{0,2},{1,3},{2,0},{3,1},{4,6},{5,7},{6,4},{7,5},{8,10},{9,11},{10,... | collective-permute-start | bytes 1179656 | tf_op jit(solution)/shard_map/ppermute | solution.py:620
  430.2 26.4 %collective-permute-start.25 = (bf16[128,2048]{1,0:T(8,128)(2,1)S(1)}, bf16[128,2048]{1,0:T(8,128)(2,1)}, u32[]{:S(2)}, u32[]{:S(2)}) collective-permute-start(bf16[128,2048]{1,0:T(8,128)(2,1)S(1)} %add_convert_fusion.5.g0), channel_id=1, source_target_pairs={{0,1},{1,0},{2,3},{3,2},{4,5},{5,4},{6,7},{7,6},{8,9},{9,8},{10,11... | collective-permute-start | bytes 1572872 | tf_op jit(solution)/shard_map/ppermute | solution.py:620
  431.3 21.1 %collective-permute-start.15 = (bf16[128,512]{1,0:T(8,128)(2,1)S(1)}, bf16[128,512]{1,0:T(8,128)(2,1)S(1)}, u32[]{:S(2)}, u32[]{:S(2)}) collective-permute-start(bf16[128,512]{1,0:T(8,128)(2,1)S(1)} %add_convert_fusion.10.g0), channel_id=1, source_target_pairs={{0,2},{1,3},{2,0},{3,1},{4,6},{5,7},{6,4},{7,5},{8,10},{9,11},{10,... | collective-permute-start | bytes 393224 | tf_op jit(solution)/shard_map/ppermute | solution.py:620
  433.3 24.3 %collective-permute-start.26 = (bf16[128,2048]{1,0:T(8,128)(2,1)S(1)}, bf16[128,2048]{1,0:T(8,128)(2,1)}, u32[]{:S(2)}, u32[]{:S(2)}) collective-permute-start(bf16[128,2048]{1,0:T(8,128)(2,1)S(1)} %collective-permute-done.24.g1), channel_id=1, source_target_pairs={{0,1},{1,0},{2,3},{3,2},{4,5},{5,4},{6,7},{7,6},{8,9},{9,8},{10,11... | collective-permute-start | bytes 1572872 | tf_op jit(solution)/shard_map/ppermute | solution.py:620
  452.4 1.3 collective-permute-start.16
  453.7 31.3 %collective-permute-start.34 = (bf16[256,1024]{1,0:T(8,128)(2,1)S(1)}, bf16[256,1024]{1,0:T(8,128)(2,1)}, u32[]{:S(2)}, u32[]{:S(2)}) collective-permute-start(bf16[256,1024]{1,0:T(8,128)(2,1)S(1)} %add_convert_fusion.3.g0), channel_id=1, source_target_pairs={{0,1},{1,0},{2,3},{3,2},{4,5},{5,4},{6,7},{7,6},{8,9},{9,8},{10,11... | collective-permute-start | bytes 1572872 | tf_op jit(solution)/shard_map/ppermute | solution.py:620
  453.9 31.1 %collective-permute-start.35 = (bf16[256,1024]{1,0:T(8,128)(2,1)S(1)}, bf16[256,1024]{1,0:T(8,128)(2,1)}, u32[]{:S(2)}, u32[]{:S(2)}) collective-permute-start(bf16[256,1024]{1,0:T(8,128)(2,1)S(1)} %collective-permute-done.33.g1), channel_id=1, source_target_pairs={{0,1},{1,0},{2,3},{3,2},{4,5},{5,4},{6,7},{7,6},{8,9},{9,8},{10,11... | collective-permute-start | bytes 1572872 | tf_op jit(solution)/shard_map/ppermute | solution.py:620
  456.4 41.8 %collective-permute-start.7 = (bf16[128,1536]{1,0:T(8,128)(2,1)S(1)}, bf16[128,1536]{1,0:T(8,128)(2,1)S(1)}, u32[]{:S(2)}, u32[]{:S(2)}) collective-permute-start(bf16[128,1536]{1,0:T(8,128)(2,1)S(1)} %add_convert_fusion.8.g0), channel_id=1, source_target_pairs={{0,1},{1,0},{2,3},{3,2},{4,5},{5,4},{6,7},{7,6},{8,9},{9,8},{10,11... | collective-permute-start | bytes 1179656 | tf_op jit(solution)/shard_map/ppermute | solution.py:620
  456.6 41.6 %collective-permute-start.8 = (bf16[128,1536]{1,0:T(8,128)(2,1)S(1)}, bf16[128,1536]{1,0:T(8,128)(2,1)}, u32[]{:S(2)}, u32[]{:S(2)}) collective-permute-start(bf16[128,1536]{1,0:T(8,128)(2,1)S(1)} %collective-permute-done.6.g1), channel_id=1, source_target_pairs={{0,1},{1,0},{2,3},{3,2},{4,5},{5,4},{6,7},{7,6},{8,9},{9,8},{10,11... | collective-permute-start | bytes 1179656 | tf_op jit(solution)/shard_map/ppermute | solution.py:620
  457.6 19.2 %collective-permute-start.17 = (bf16[128,512]{1,0:T(8,128)(2,1)S(1)}, bf16[128,512]{1,0:T(8,128)(2,1)S(1)}, u32[]{:S(2)}, u32[]{:S(2)}) collective-permute-start(bf16[128,512]{1,0:T(8,128)(2,1)S(1)} %collective-permute-done.15.g1), channel_id=1, source_target_pairs={{0,1},{1,0},{2,3},{3,2},{4,5},{5,4},{6,7},{7,6},{8,9},{9,8},{10,11... | collective-permute-start | bytes 393224 | tf_op jit(solution)/shard_map/ppermute | solution.py:620
  (19 other events, 139.0 us)

commit v3 on v2

--- a/solution.py
+++ b/solution.py
@@ -216,12 +216,6 @@
     top = jnp.max(raw, axis=-1, keepdims=True)
     exponent = jnp.exp(raw - top)
     return exponent / jnp.sum(exponent, axis=-1, keepdims=True)
-
-
-def fetch(src, buf, sem, start, width):
-    copy = pltpu.make_async_copy(src.at[:, :, pl.ds(start, width)], buf, sem)
-    copy.start()
-    return copy
 
 
 def attend_kernel(seqs, buf, *refs):
@@ -381,26 +375,41 @@
     keep_attn.wait()
 
 
+def swap_start(place, src, dst, send, recv, k):
+    copy = pltpu.make_async_remote_copy(
+        src_ref=src, dst_ref=dst, send_sem=send.at[k], recv_sem=recv.at[k],
+        device_id=place.to_core, device_id_type=MESH,
+    )
+    copy.start()
+    return copy
+
+
 def feed_kernel(seqs, buf, *refs):
-    info, keep, h2, em, r, vec, ups, downs = refs[:8]
-    z_mine, z_yours, u_mine, u_yours, er, ea, out, sums = refs[8:16]
-    wup, wdown, m_acc, t_acc, sems = refs[16:]
+    counts, keep, h2, em, r, vec, h2_hbm, em_hbm, ups, downs = refs[:10]
+    z_mine, u_mine, er, ea, out, sums, h2_got, em_got, z_got, u_got = refs[10:20]
+    wup, wdown, m_acc, t_acc, z_yours, u_yours, sems, send, recv = refs[20:]
     rows = h2.shape[0] // seqs
     d = h2.shape[1]
     strip = wup.shape[2] // 4
     tile = strip // 2
+    place = Place()
     copies = []
     for e in range(2):
-        core = info[1] ^ e
+        core = (1 - place.core) * (1 - e) + place.core * e
         copies.append(pltpu.make_async_copy(ups.at[core], wup.at[e], sems.at[e, 0]))
         copies.append(pltpu.make_async_copy(downs.at[core], wdown.at[e], sems.at[e, 1]))
     for one in copies:
         one.start()
+    place.meet((place.to_core,))
+    swaps = [
+        swap_start(place, em_hbm, em_got, send, recv, 0),
+        swap_start(place, h2_hbm, h2_got, send, recv, 1),
+    ]
     sums[...] = jnp.zeros_like(sums)
     m_acc[...] = jnp.zeros_like(m_acc)
     t_acc[...] = jnp.zeros_like(t_acc)
-    for e, z_out, u_out in ((0, z_mine, u_mine), (1, z_yours, u_yours)):
-        core = info[1] ^ e
+    for e, z_out, u_out in ((0, z_yours, u_yours), (1, z_mine, u_mine)):
+        core = (1 - place.core) * (1 - e) + place.core * e
         for one in copies[2 * e : 2 * e + 2]:
             one.wait()
 
@@ -414,7 +423,7 @@
             u = mm(h2[...], w_up) + vec[far]
             phi = 0.5 * (1.0 + lax.erf(u * root_half))
             z = (u * phi).astype(bf16)
-            z_out[:, near] = z
+            z_out[t, :, pl.ds(pl.multiple_of(s * tile, tile), tile)] = z
             slope = phi + u * jnp.exp(-0.5 * u * u) * inverse_root_two_pi
             eu = (mm_nt(em[...], w_down) * slope).astype(bf16)
             u_out[:, near] = eu
@@ -422,10 +431,14 @@
             t_acc[...] += mm_nt(eu, w_up)
             sums[far] = jnp.sum(eu.astype(f32), axis=0, keepdims=True)
 
+        if e == 0:
+            swaps.append(swap_start(place, z_yours, z_got, send, recv, 2))
+            swaps.append(swap_start(place, u_yours, u_got, send, recv, 3))
+
     @pl.loop(0, seqs)
     def _(n):
         at = pl.ds(pl.multiple_of(n * rows, 16), rows)
-        valid = lax.broadcasted_iota(jnp.int32, (rows, 1), 0) < info[4 + n]
+        valid = lax.broadcasted_iota(jnp.int32, (rows, 1), 0) < counts[n]
         valid = jnp.where(valid, 1.0, 0.0)
         resid = r[at, :]
         m = m_acc[at, :] + vec[7:8, :]
@@ -445,105 +458,350 @@
         sums[6:7, :] += jnp.sum(t, axis=0, keepdims=True)
         sums[7:8, :] += jnp.sum(low, axis=0, keepdims=True)
         sums[12:13, :] += jnp.sum(m * m * valid, axis=0, keepdims=True)
-
-
-def back_kernel(seqs, *refs):
-    info, ea, qkv, w_attn, mine, yours, sums, wbuf, eo, sem = refs
-    rows = ea.shape[0] // seqs
-    d = ea.shape[1]
-    half = d // 2
-    fetch(w_attn, wbuf, sem, 3 * half, half).wait()
+    for one in swaps:
+        one.wait()
+
+
+class Timeline:
+    def __init__(self):
+        self.steps = []
+
+    def add(self, when, step):
+        self.steps.append((when, len(self.steps), step))
+        self.steps.sort(key=lambda one: one[:2])
+
+    def until(self, when):
+        while self.steps and self.steps[0][0] <= when:
+            self.steps.pop(0)[2]()
+
+    def during(self, count, start, gap):
+        due = []
+        while self.steps and self.steps[0][0] < start + count * gap:
+            when, _, step = self.steps.pop(0)
+            due.append((min(max(int((when - start) / gap), 0), count - 1), step))
+
+        def run(turn):
+            for at, step in due:
+                pl.when(turn == at)(step)
+
+        return run
+
+
+class Reduce:
+    def __init__(self, place, bits, g, r1, r2, r3, r4, total, send, recv):
+        self.place, self.bits, self.g, self.r1, self.r2, self.r3, self.r4 = place, bits, g, r1, r2, r3, r4
+        self.total, self.send, self.recv = total, send, recv
+        self.half = g.shape[1] // 2
+        self.hold = r2.at[pl.ds(0, self.half)]
+        self.slots = [r1.at[n // 2 % 2, pl.ds(n % 2 * self.half, self.half)] for n in range(len(bits))]
+
+    def copy(self, k):
+        p = self.place
+        half = self.half
+        mine, other = p.level * half, (1 - p.level) * half
+        at = lambda start: pl.ds(pl.multiple_of(start, 16), half)
+        plans = [
+            (self.g.at[p.third], self.r1.at[1], p.to_first),
+            (self.g.at[p.first], self.r1.at[0], p.to_first),
+            (self.g.at[p.second], self.r2, p.to_second),
+            (self.g.at[p.group, at(other)], self.r3, p.to_bit(2)),
+            (self.hold, self.total.at[p.core, at(mine)], p.to_bit(2)),
+            (self.hold, self.total.at[p.core, at(mine)], p.to_core),
+            (self.total.at[p.core, at(other)], self.total.at[p.core, at(other)], p.to_core),
+        ]
+        for n, bit in enumerate(self.bits):
+            plans.append((self.slots[n], self.r4.at[n], p.to_bit(bit)))
+        src, dst, device = plans[k]
+        return pltpu.make_async_remote_copy(
+            src_ref=src, dst_ref=dst, send_sem=self.send.at[k], recv_sem=self.recv.at[k],
+            device_id=device, device_id_type=MESH,
+        )
+
+    def begin(self):
+        self.copy(0).start()
+        self.copy(1).start()
+
+    def pass_second(self):
+        self.copy(0).wait_recv()
+        at = self.place.second
+        self.g[at] = (self.g[at].astype(f32) + self.r1[1].astype(f32)).astype(bf16)
+        self.copy(2).start()
+
+    def pass_replica(self):
+        self.copy(1).wait_recv()
+        self.copy(2).wait_recv()
+        at = self.place.group
+        self.g[at] = (self.g[at].astype(f32) + self.r1[0].astype(f32) + self.r2[...].astype(f32)).astype(bf16)
+        self.copy(3).start()
+
+    def pass_bit(self, n):
+        p = self.place
+        if n == 0:
+            self.copy(3).wait_recv()
+            at = pl.ds(pl.multiple_of(p.level * self.half, 16), self.half)
+            value = self.g[p.group, at].astype(f32) + self.r3[...].astype(f32)
+        else:
+            self.copy(6 + n).wait_recv()
+            value = self.slots[n - 1][...].astype(f32) + self.r4[n - 1].astype(f32)
+        if n < len(self.bits):
+            self.slots[n][...] = value.astype(bf16)
+            self.copy(7 + n).start()
+        else:
+            self.hold[...] = value.astype(bf16)
+            self.copy(4).start()
+            self.copy(5).start()
+            self.stay().start()
+
+    def stay(self):
+        p = self.place
+        at = pl.ds(pl.multiple_of(p.level * self.half, 16), self.half)
+        return pltpu.make_async_copy(self.hold, self.total.at[p.core, at], self.send.at[7 + len(self.bits)])
+
+    def pass_core(self):
+        self.copy(4).wait_recv()
+        self.copy(6).start()
+
+    def finish(self):
+        self.copy(5).wait_recv()
+        self.copy(6).wait_recv()
+        for k in range(7 + len(self.bits)):
+            self.copy(k).wait_send()
+        self.stay().wait()
+
+
+def tail_kernel(seqs, buf, bits, sizes, *refs):
+    counts, keep, qkv, x, er, vec, stats, sums_feed = refs[:8]
+    z_mine, z_got, em, em_got, h2, h2_got, u_mine, u_got, o, ea, h1, w_attn = refs[8:20]
+    chunks = len(sizes)
+    small, out = refs[20:22]
+    totals = refs[22 : 22 + chunks]
+    o_got, ea_got, h1_got, e_got = refs[22 + chunks : 26 + chunks]
+    scratch = refs[26 + chunks :]
+    wbuf, eo, e, t_acc, stage, sides, small_in = scratch[:7]
+    buffers = [scratch[7 + k * chunks : 7 + (k + 1) * chunks] for k in range(5)]
+    send, recv, w_sem, ea_sem, side_sems, stage_sem, swap_send, swap_recv, small_send, small_recv = scratch[7 + 5 * chunks :]
+    total, d = eo.shape
+    rows = total // seqs
+    half, quarter = d // 2, d // 4
+    place = Place()
+    core = place.core
+
+    o_weight = pltpu.make_async_copy(w_attn.at[:, :, pl.ds(3 * half, half)], wbuf.at[:, :, pl.ds(0, half)], w_sem)
+    o_weight.start()
+    ea_all = e.at[0, :, pl.ds(0, d)]
+    take_ea = pltpu.make_async_copy(ea, ea_all, ea_sem)
+    take_ea.start()
+
+    mine_cols = pl.ds(pl.multiple_of(core * half, half), half)
+    left = [(z_mine.at[0], z_got.at[0]), (z_mine.at[1], z_got.at[1]), (h2, h2_got), (h2, h2_got), (o, o_got), (h1, h1_got), (h1, h1_got)]
+    right = [
+        (em, em_got), (em, em_got),
+        (u_mine.at[:, pl.ds(0, d)], u_got.at[:, pl.ds(0, d)]), (u_mine.at[:, pl.ds(d, d)], u_got.at[:, pl.ds(d, d)]),
+        (ea.at[:, mine_cols], ea_got.at[:, mine_cols]),
+        (e.at[core, :, pl.ds(0, d)], e_got.at[:, pl.ds(0, d)]), (e.at[core, :, pl.ds(d, half)], e_got.at[:, pl.ds(d, half)]),
+    ]
+
+    def side_copies(k):
+        found = []
+        for side, pairs in enumerate((left, right)):
+            wide = sizes[k] if side else d
+            for which, src in enumerate(pairs[k]):
+                dst = sides.at[k % 2, side, pl.ds(which * total, total), pl.ds(0, wide)]
+                found.append(pltpu.make_async_copy(src, dst, side_sems.at[k % 2, side, which]))
+        return found
+
+    def load_sides(k):
+        for one in side_copies(k):
+            one.start()
+
+    load_sides(0)
+    load_sides(1)
+    partners = [place.to_first, place.to_second, place.to_core, place.to_bit(2)] + [place.to_bit(b) for b in bits]
+    place.meet(partners)
+    swaps = [
+        swap_start(place, o, o_got, swap_send, swap_recv, 0),
+        swap_start(place, ea, ea_got, swap_send, swap_recv, 1),
+        swap_start(place, h1, h1_got, swap_send, swap_recv, 2),
+    ]
+    sent_e = pltpu.make_async_remote_copy(
+        src_ref=e.at[1 - core], dst_ref=e_got, send_sem=swap_send.at[3], recv_sem=swap_recv.at[3],
+        device_id=place.to_core, device_id_type=MESH,
+    )
+    reduces = [
+        Reduce(place, bits, *(buffers[b][k] for b in range(5)), totals[k], send.at[k], recv.at[k]) for k in range(chunks)
+    ]
+
+    def gradient(k):
+        for one in side_copies(k):
+            one.wait()
+        wide = sizes[k]
+
+        @pl.loop(0, 4)
+        def _(i):
+            near = place.first * (1 - i // 2) + place.group * (i // 2)
+            over = ((i + 1) // 2) % 2
+            bit_two = (1 - core) * flip(near, 2) + core * flip(near, 1)
+            owner = near * (1 - over) + bit_two * over
+            cols = pl.ds(pl.multiple_of(owner * quarter, quarter), quarter)
+            reduces[k].g[owner] = mm_tn(sides[k % 2, 0, :, cols], sides[k % 2, 1, :, 0:wide]).astype(bf16)
+
+    line = Timeline()
+    start = 3.0
+    for k in range(chunks):
+        size = sizes[k] / d
+        if k == 5:
+            start = max(start, 58.0)
+        one = reduces[k]
+        line.add(start, one.begin)
+        when = start + 9.0 * size + 2
+        line.add(when, one.pass_second)
+        when = start + 17.0 * size + 3
+        line.add(when, one.pass_replica)
+        when += 7 * size + 2
+        for n in range(len(bits) + 1):
+            line.add(when, functools.partial(one.pass_bit, n))
+            when += 10 * size + 2
+        line.add(when, one.pass_core)
+        line.add(when + 6 * size + 3, one.finish)
+        start += 17.0 * size
+
+    gradient(0)
+    load_sides(2)
+    line.until(3)
+    gradient(1)
+    load_sides(3)
+    line.until(6)
+    gradient(2)
+    for one in swaps[:2]:
+        one.wait()
+    load_sides(4)
+    line.until(9)
+    gradient(3)
+    line.until(12)
+    gradient(4)
+    swaps[2].wait()
+    line.until(14)
+    o_weight.wait()
+    take_ea.wait()
 
     @pl.loop(0, 4)
     def _(s):
-        near = pl.ds(pl.multiple_of(s * (d // 4), d // 4), d // 4)
-        got = mm_nt(ea[:, 0:half], wbuf[0, near, :]) + mm_nt(ea[:, half:], wbuf[1, near, :])
+        near = pl.ds(pl.multiple_of(s * quarter, quarter), quarter)
+        got = mm_nt(ea_all[:, 0:half], wbuf[0, near, 0:half]) + mm_nt(ea_all[:, half:], wbuf[1, near, 0:half])
         eo[:, near] = got.astype(bf16)
 
+    in_weight = pltpu.make_async_copy(w_attn.at[:, :, pl.ds(0, 3 * half)], wbuf, w_sem)
+    in_weight.start()
+    line.until(17)
     low, high, first = head_masks()
     pairs = half // (2 * HEAD)
     scale = 1.0 / math.sqrt(HEAD)
-    sums[...] = jnp.zeros_like(sums)
-    for e, dst in ((0, mine), (1, yours)):
-        core = info[1] ^ e
-
-        @pl.loop(0, seqs * pairs)
-        def _(i):
-            n, j = i // pairs, i % pairs
-            at = pl.ds(pl.multiple_of(n * rows, 16), rows)
-            far = core * half + j * 2 * HEAD
-            lanes = [pl.ds(pl.multiple_of(far + m * d, 2 * HEAD), 2 * HEAD) for m in range(3)]
-            k_pair = qkv[at, lanes[1]]
-            q_both = two_heads(qkv[at, lanes[0]], low, high)
-            probs = pair_probs(q_both, k_pair, info[4 + n])
-            eo_both = two_heads(eo[at, lanes[0]], low, high)
-            ep = mm_nt(eo_both, qkv[at, lanes[2]])
-            inner = jnp.sum(probs * ep, axis=-1, keepdims=True)
-            es = (probs * (ep - inner)).astype(bf16)
-            ev = mm_tn(probs.astype(bf16), eo_both).astype(bf16)
-            eq = (pick_heads(mm(es, k_pair), first) * scale).astype(bf16)
-            ek = (mm_tn(es, q_both) * scale).astype(bf16)
-            for m, value in enumerate((eq, ek, ev)):
-                dst[at, pl.ds(pl.multiple_of(m * half + j * 2 * HEAD, 2 * HEAD), 2 * HEAD)] = value
-            sums[2:3, lanes[0]] += jnp.sum(eq.astype(f32), axis=0, keepdims=True)
-            sums[3:4, lanes[0]] += jnp.sum(ev.astype(f32), axis=0, keepdims=True)
-
-
-def input_kernel(seqs, buf, *refs):
-    info, keep, mine, yours, x, er, vec, w_attn, out, sums, wbuf, t_acc, sem = refs
-    rows = x.shape[0] // seqs
-    d = x.shape[1]
-    half = d // 2
-    fetch(w_attn, wbuf, sem, 0, 3 * half).wait()
-    core = info[1]
+    small[...] = jnp.zeros_like(small)
+    turns = seqs * pairs
+
+    due = line.during(2 * turns, 17.0, 0.9)
+
+    @pl.loop(0, 2 * turns)
+    def _(i):
+        pl.when(i == turns)(sent_e.start)
+        due(i)
+        h = (1 - core) * (1 - i // turns) + core * (i // turns)
+        n, j = (i % turns) // pairs, i % pairs
+        at = pl.ds(pl.multiple_of(n * rows, 16), rows)
+        far = h * half + j * 2 * HEAD
+        lanes = [pl.ds(pl.multiple_of(far + m * d, 2 * HEAD), 2 * HEAD) for m in range(3)]
+        k_pair = qkv[at, lanes[1]]
+        q_both = two_heads(qkv[at, lanes[0]], low, high)
+        probs = pair_probs(q_both, k_pair, counts[n])
+        eo_both = two_heads(eo[at, lanes[0]], low, high)
+        ep = mm_nt(eo_both, qkv[at, lanes[2]])
+        inner = jnp.sum(probs * ep, axis=-1, keepdims=True)
+        es = (probs * (ep - inner)).astype(bf16)
+        ev = mm_tn(probs.astype(bf16), eo_both).astype(bf16)
+        eq = (pick_heads(mm(es, k_pair), first) * scale).astype(bf16)
+        ek = (mm_tn(es, q_both) * scale).astype(bf16)
+        for m, value in enumerate((eq, ek, ev)):
+            e[h, at, pl.ds(pl.multiple_of(m * half + j * 2 * HEAD, 2 * HEAD), 2 * HEAD)] = value
+        small[2:3, lanes[0]] += jnp.sum(eq.astype(f32), axis=0, keepdims=True)
+        small[3:4, lanes[0]] += jnp.sum(ev.astype(f32), axis=0, keepdims=True)
+
+    sent_e.wait()
+    load_sides(5)
+    load_sides(6)
+    gradient(5)
+    line.until(48)
+    gradient(6)
+    line.until(52)
+    in_weight.wait()
+
+    due_in = line.during(4, 52.0, 1.5)
 
     @pl.loop(0, 4)
     def _(s):
-        near = pl.ds(pl.multiple_of(s * (d // 4), d // 4), d // 4)
-        t_acc[:, near] = mm_nt(mine[...], wbuf[core, near, :]) + mm_nt(yours[...], wbuf[1 - core, near, :])
-
-    sums[...] = jnp.zeros_like(sums)
+        due_in(s)
+        near = pl.ds(pl.multiple_of(s * quarter, quarter), quarter)
+        t_acc[:, near] = mm_nt(e[0], wbuf[0, near, :]) + mm_nt(e[1], wbuf[1, near, :])
+
+    due_out = line.during(seqs, 58.0, 2.5)
 
     @pl.loop(0, seqs)
     def _(n):
+        due_out(n)
         at = pl.ds(pl.multiple_of(n * rows, 16), rows)
         normal, inverse = layer_stats(x[at, :].astype(f32))
         t = t_acc[at, :]
         grad = er[at, :] + norm_back(t, normal, inverse, vec[0:1, :])
-        sums[0:1, :] += jnp.sum(t * normal, axis=0, keepdims=True)
-        sums[1:2, :] += jnp.sum(t, axis=0, keepdims=True)
-        out[n, 0:buf, :] = grad[0:buf]
+        small[0:1, :] += jnp.sum(t * normal, axis=0, keepdims=True)
+        small[1:2, :] += jnp.sum(t, axis=0, keepdims=True)
+        write = pltpu.make_async_copy(stage, out.at[n], stage_sem)
+
+        @pl.when(n > 0)
+        def _():
+            write.wait()
+
+        stage[0:buf, :] = grad[0:buf]
         pick = picker(keep[n], rows - buf)
         rest = grad[buf:]
-        high = rest.astype(bf16)
-        rest = rest - high.astype(f32)
+        top = rest.astype(bf16)
+        rest = rest - top.astype(f32)
         middle = rest.astype(bf16)
-        low = (rest - middle.astype(f32)).astype(bf16)
-        out[n, buf:, :] = mm_tn(pick, high) + mm_tn(pick, middle) + mm_tn(pick, low)
-
-
-def grad_kernel(order, a_own, a_got, b_own, b_got, out):
-    left = jnp.concatenate([a_own[...], a_got[...]], axis=0)
-    right = jnp.concatenate([b_own[...], b_got[...]], axis=0)
-    out[0] = mm_tn(left, right).astype(bf16)
-
-
-def weight_grad(order, a_own, a_got, b_own, b_got, deep, wide, tile, b_start=0):
-    rows = a_own.shape[0]
-    blocks = 2
-    return pl.pallas_call(
-        grad_kernel,
-        grid_spec=pltpu.PrefetchScalarGridSpec(
-            num_scalar_prefetch=1,
-            grid=(blocks, wide // tile),
-            in_specs=[pl.BlockSpec((rows, deep), lambda i, j, order: (0, order[i]))] * 2
-            + [pl.BlockSpec((rows, tile), lambda i, j, order: (0, order[2] * b_start + j))] * 2,
-            out_specs=pl.BlockSpec((1, deep, tile), lambda i, j, order: (i, 0, j)),
-        ),
-        out_shape=sds((blocks, deep, wide), bf16),
-        compiler_params=params(40),
-        cost_estimate=cost(4 * rows * deep * wide * blocks, 4 * rows * (deep * 2 + wide)),
-    )(order, a_own, a_got, b_own, b_got)
+        bottom = (rest - middle.astype(f32)).astype(bf16)
+        stage[buf:, :] = mm_tn(pick, top) + mm_tn(pick, middle) + mm_tn(pick, bottom)
+        write.start()
+
+    pltpu.make_async_copy(stage, out.at[0], stage_sem).wait()
+
+    small[4:12, :] = sums_feed[4:12, :]
+    kept = counts[0]
+    for n in range(1, seqs):
+        kept = kept + counts[n]
+    lane = lax.broadcasted_iota(jnp.int32, (1, d), 1)
+    tally = jnp.where(lane == 3, kept.astype(f32), 0.0)
+    for k, row in enumerate((stats[0:1, :], stats[1:2, :], sums_feed[12:13, :])):
+        tally = tally + jnp.where(lane == k, jnp.sum(row, axis=1, keepdims=True), 0.0)
+    small[12:13, :] = tally
+    hops = [place.to_first, place.to_second] + [place.to_bit(b) for b in (1, 2, *bits)]
+    small_in[0, 0] = small[...]
+
+    def hop(k):
+        return pltpu.make_async_remote_copy(
+            src_ref=small_in.at[k, 0], dst_ref=small_in.at[k, 1], send_sem=small_send.at[k], recv_sem=small_recv.at[k],
+            device_id=hops[k], device_id_type=MESH,
+        )
+
+    def small_step(k):
+        if k > 0:
+            hop(k - 1).wait()
+            value = small_in[k - 1, 0] + small_in[k - 1, 1]
+            if k == len(hops):
+                small[...] = value
+                return
+            small_in[k, 0] = value
+        hop(k).start()
+
+    for k in range(len(hops) + 1):
+        line.add(68.0 + 6 * k, functools.partial(small_step, k))
+    line.until(1e9)
 
 
 def adam_math(w, f, s, grad, rate, decay):
@@ -555,47 +813,30 @@
     return w - rate * (update + decay * w), first_new, second_new
 
 
-def adam_kernel(info, w, f, s, g0, g1, g2, g3, *rest):
+def adam_kernel(w, f, s, grad, *rest):
     w_out, f_out, s_out, low_out = rest[-4:]
-    quarter = pl.program_id(0)
-    for k, part in enumerate((g0, g1, g2, g3)):
-
-        @pl.when(quarter == k)
-        def _():
-            new, first, second = adam_math(
-                w[...], f[...], s[...], part[...].astype(f32), rate_matrix, weight_decay
-            )
-            w_out[...] = new
-            f_out[...] = first
-            s_out[...] = second
-            low_out[...] = new.astype(bf16)
-
-
-def adam_call(info, state, quarters, block, grid_width, place, grad_place, aliased=None):
+    new, first, second = adam_math(w[...], f[...], s[...], grad[0].astype(f32), rate_matrix, weight_decay)
+    w_out[...] = new
+    f_out[...] = first
+    s_out[...] = second
+    low_out[...] = new.astype(bf16)
+
+
+def adam_call(state, grad, grid, block, place, grad_place, previous=None):
     spec = pl.BlockSpec(block, place)
     shape = state[0].shape
-    grads = [
-        pl.BlockSpec(block, functools.partial(lambda k, i, j, info: grad_place(jnp.where(i == k, j, 0)), k))
-        for k in range(4)
-    ]
-    extra = [] if aliased is None else list(aliased)
+    extra = [] if previous is None else list(previous)
+    size = grid[0] * grid[1] * block[0] * block[1]
     return pl.pallas_call(
         adam_kernel,
-        grid_spec=pltpu.PrefetchScalarGridSpec(
-            num_scalar_prefetch=1,
-            grid=(4, grid_width),
-            in_specs=[spec] * 3 + grads + [ANY_SPEC] * len(extra),
-            out_specs=[spec] * 4,
-        ),
+        grid=grid,
+        in_specs=[spec] * 3 + [pl.BlockSpec((1, *block), grad_place)] + [ANY_SPEC] * len(extra),
+        out_specs=[spec] * 4,
         out_shape=[sds(shape, f32)] * 3 + [sds(shape, bf16)],
-        input_output_aliases={8 + k: k for k in range(len(extra))},
+        input_output_aliases={4 + k: k for k in range(len(extra))},
         compiler_params=params(40),
-        cost_estimate=cost(20 * 4 * grid_width * block[0] * block[1], 28 * 4 * grid_width * block[0] * block[1]),
-    )(info, *state, *quarters, *extra)
-
-
-def add_low(a, b):
-    return (a.astype(f32) + b.astype(f32)).astype(bf16)
+        cost_estimate=cost(20 * size, 28 * size),
+    )(*state, grad, *extra)
 
 
 def local(groups, replicas, *args):
@@ -606,23 +847,8 @@
     rows = -(-(buf + KEEP_MAX) // 16) * 16
     total = seqs * rows
     half = d // 2
-    group, replica = lax.axis_index("group"), lax.axis_index("dp")
-    core, level = replica % 2, (replica // 2) % 2
-    counts = buf + jnp.sum(keep, axis=1)
-    info = jnp.concatenate([jnp.stack([group, core, level, 0 * core]), counts]).astype(jnp.int32)
-
-    def permute(value, target):
-        pairs = []
-        for a in range(groups):
-            for b in range(replicas):
-                to_a, to_b = target(a, b)
-                pairs.append((a * replicas + b, to_a * replicas + to_b))
-        return lax.ppermute(value, BOTH, pairs)
-
-    hop_one = lambda v: permute(v, lambda a, b: (a ^ (1 + b % 2), b))
-    hop_two = lambda v: permute(v, lambda a, b: (a ^ (2 - b % 2), b))
-    swap = lambda v: permute(v, lambda a, b: (a, b ^ 1))
-    shift = lambda v, bit: permute(v, lambda a, b: (a, b ^ bit))
+    group = lax.axis_index("group")
+    counts = (buf + jnp.sum(keep, axis=1)).astype(jnp.int32)
 
     keep3 = keep.reshape(seqs, 1, image)
     deep = mats.shape[0]
@@ -662,149 +888,109 @@
         ],
         compiler_params=params(60, collective_id=0, has_side_effects=True),
         cost_estimate=cost(2 * total * 4 * d * d * 4, 20 * total * d),
-    )(counts.astype(jnp.int32), keep3, vectors, mats, down, tokens, cot)
-    h1_got, em_got = swap(h1), swap(em)
-    o_got, h2_got = swap(o), swap(h2)
-
-    z_mine, z_yours, u_mine, u_yours, er, ea, block_output, sums_feed = pl.pallas_call(
+    )(counts, keep3, vectors, mats, down, tokens, cot)
+    z_mine, u_mine, er, ea, block_output, sums_feed, h2_got, em_got, z_got, u_got = pl.pallas_call(
         functools.partial(feed_kernel, seqs, buf),
-        in_specs=[SMEM_SPEC] + [VMEM_SPEC] * 5 + [ANY_SPEC] * 2,
-        out_specs=[VMEM_SPEC] * 8,
-        out_shape=[sds((total, 2 * d), bf16)] * 4
-        + [
+        in_specs=[SMEM_SPEC] + [VMEM_SPEC] * 5 + [ANY_SPEC] * 4,
+        out_specs=[VMEM_SPEC] * 6 + [ANY_SPEC] * 4,
+        out_shape=[
+            sds((2, total, d), bf16),
+            sds((total, 2 * d), bf16),
             sds((total, d), f32),
             sds((total, d), bf16),
             sds((seqs, length, d), bf16),
             sds((16, d), f32),
+            sds((total, d), bf16),
+            sds((total, d), bf16),
+            sds((2, total, d), bf16),
+            sds((total, 2 * d), bf16),
         ],
         scratch_shapes=[
             pltpu.VMEM((2, d, 2 * d), bf16),
             pltpu.VMEM((2, 2 * d, d), bf16),
             pltpu.VMEM((total, d), f32),
             pltpu.VMEM((total, d), f32),
+            pltpu.VMEM((2, total, d), bf16),
+            pltpu.VMEM((total, 2 * d), bf16),
             pltpu.SemaphoreType.DMA((2, 2)),
+            pltpu.SemaphoreType.DMA((4,)),
+            pltpu.SemaphoreType.DMA((4,)),
         ],
-        compiler_params=params(60),
+        compiler_params=params(60, collective_id=1, has_side_effects=True),
         cost_estimate=cost(2 * total * 16 * d * d, 60 * total * d),
-    )(info, keep3, h2, em, r, vec, w_up, w_down)
-
-    z_got, u_got, ea_got = swap(z_yours), swap(u_yours), swap(ea)
-
-    first, second = core + 1, 2 - core
-    send_order = jnp.stack([group ^ first, group ^ 3, core]).astype(jnp.int32)
-    keep_order = jnp.stack([group, group ^ second, core]).astype(jnp.int32)
-
-    def reduce_blocks(make):
-        sent = make(send_order)
-        got = hop_one(sent)
-        kept = make(keep_order)
-        kept = add_low(kept, got)
-        mine = add_low(kept[0], hop_two(kept[1]))
-        deep = mine.shape[0] // 2
-        give = lax.dynamic_slice(mine, ((1 - level) * deep, 0), (deep, mine.shape[1]))
-        hold = lax.dynamic_slice(mine, (level * deep, 0), (deep, mine.shape[1]))
-        hold = add_low(hold, shift(give, 2))
-        bit = 4
-        while bit < replicas:
-            hold = add_low(hold, shift(hold, bit))
-            bit *= 2
-        other = shift(hold, 2)
-        return hold, other, swap(hold), swap(other)
-
-    g_down = reduce_blocks(
-        lambda order: weight_grad(order, z_mine, z_got, em, em_got, half, d, half)
-    )
-
-    def up_and_out(order):
-        return weight_grad(order, h2, h2_got, u_mine, u_got, d // 4, 2 * d, half)
-
-    g_up = reduce_blocks(up_and_out)
-    g_out = reduce_blocks(lambda order: weight_grad(order, o, o_got, ea, ea_got, d // 4, half, half, 1))
-
-    e_mine, e_yours, sums_back = pl.pallas_call(
-        functools.partial(back_kernel, seqs),
-        in_specs=[SMEM_SPEC] + [VMEM_SPEC] * 2 + [ANY_SPEC],
-        out_specs=[VMEM_SPEC] * 3,
-        out_shape=[sds((total, 3 * half), bf16)] * 2 + [sds((8, d), f32)],
-        scratch_shapes=[
-            pltpu.VMEM((2, d, half), bf16),
-            pltpu.VMEM((total, d), bf16),
-            pltpu.SemaphoreType.DMA(()),
-        ],
-        compiler_params=params(48),
-        cost_estimate=cost(2 * total * 4 * d * d, 20 * total * d),
-    )(info, ea, qkv, w_attn)
-    e_got = swap(e_yours)
-    g_qkv = reduce_blocks(
-        lambda order: weight_grad(order, h1, h1_got, e_mine, e_got, d // 4, 3 * half, half)
-    )
-
-    input_grad, sums_in = pl.pallas_call(
-        functools.partial(input_kernel, seqs, buf),
-        in_specs=[SMEM_SPEC] + [VMEM_SPEC] * 6 + [ANY_SPEC],
-        out_specs=[VMEM_SPEC] * 2,
-        out_shape=[sds((seqs, length, d), f32), sds((8, d), f32)],
+    )(counts, keep3, h2, em, r, vec, h2, em, w_up, w_down)
+
+    bits = []
+    while (4 << len(bits)) < replicas:
+        bits.append(4 << len(bits))
+    sizes = (d, d, d, d, half, d, half)
+    chunks, steps = len(sizes), 7 + len(bits)
+    quarter = d // 4
+    found = pl.pallas_call(
+        functools.partial(tail_kernel, seqs, buf, tuple(bits), sizes),
+        in_specs=[SMEM_SPEC] + [VMEM_SPEC] * 7 + [ANY_SPEC] * 12,
+        out_specs=[VMEM_SPEC, ANY_SPEC] + [ANY_SPEC] * (chunks + 4),
+        out_shape=[sds((16, d), f32), sds((seqs, length, d), f32)]
+        + [sds((2, quarter, wide), bf16) for wide in sizes]
+        + [sds((total, d), bf16)] * 3
+        + [sds((total, 3 * half), bf16)],
         scratch_shapes=[
             pltpu.VMEM((2, d, 3 * half), bf16),
+            pltpu.VMEM((total, d), bf16),
+            pltpu.VMEM((2, total, 3 * half), bf16),
             pltpu.VMEM((total, d), f32),
+            pltpu.VMEM((length, d), f32),
+            pltpu.VMEM((2, 2, 2 * total, d), bf16),
+            pltpu.VMEM((4 + len(bits), 2, 16, d), f32),
+        ]
+        + [pltpu.VMEM((4, quarter, wide), bf16) for wide in sizes]
+        + [pltpu.VMEM((2, quarter, wide), bf16) for wide in sizes]
+        + [pltpu.VMEM((quarter, wide), bf16) for wide in sizes]
+        + [pltpu.VMEM((quarter // 2, wide), bf16) for wide in sizes]
+        + [pltpu.VMEM((len(bits), quarter // 2, wide), bf16) for wide in sizes]
+        + [
+            pltpu.SemaphoreType.DMA((chunks, steps + 1)),
+            pltpu.SemaphoreType.DMA((chunks, steps)),
             pltpu.SemaphoreType.DMA(()),
+            pltpu.SemaphoreType.DMA(()),
+            pltpu.SemaphoreType.DMA((2, 2, 2)),
+            pltpu.SemaphoreType.DMA(()),
+            pltpu.SemaphoreType.DMA((4,)),
+            pltpu.SemaphoreType.DMA((4,)),
+            pltpu.SemaphoreType.DMA((4 + len(bits),)),
+            pltpu.SemaphoreType.DMA((4 + len(bits),)),
         ],
-        compiler_params=params(56),
-        cost_estimate=cost(2 * total * 3 * d * d, 20 * total * d),
-    )(info, keep3, e_mine, e_yours, x, er, vec, w_attn)
-
-    squares = jnp.stack([jnp.sum(stats[0]), jnp.sum(stats[1]), jnp.sum(sums_feed[12]), jnp.sum(counts).astype(f32)])
-    small = jnp.concatenate(
-        [
-            sums_in[0:2],
-            sums_back[2:4],
-            sums_feed[4:12],
-            jnp.pad(squares.reshape(1, 4), ((0, 3), (0, d - 4))),
-        ]
-    )
-    bit = 1
-    while bit < groups:
-        small = small + permute(small, functools.partial(lambda flip, a, b: (a ^ flip, b), bit))
-        bit *= 2
-    bit = 1
-    while bit < replicas:
-        small = small + shift(small, bit)
-        bit *= 2
+        compiler_params=params(61, collective_id=2, has_side_effects=True),
+        cost_estimate=cost(2 * total * 16 * d * d, 100 * total * d),
+    )(counts, keep3, qkv, x, er, vec, stats, sums_feed, z_mine, z_got, em, em_got, h2, h2_got, u_mine, u_got, o, ea, h1, w_attn)
+    small, input_grad = found[:2]
+    grads = found[2 : 2 + chunks]
     branch_rms = jnp.sqrt(small[12, 0:3] / (small[12, 3] * d))
     part = vectors.shape[1]
     grad_vectors = lax.dynamic_slice(small, (0, group * part), (12, part))
 
-    def core_of(k, info):
-        return info[1] ^ (k // 2)
-
-    def level_of(k, info):
-        return info[2] ^ (k % 2)
-
-    new_down = adam_call(
-        info,
-        (down, f_down, s_down),
-        g_down,
-        (down.shape[0] // 4, half),
-        2,
-        lambda i, j, info: (2 * core_of(i, info) + level_of(i, info), j),
-        lambda j: (0, j),
-    )
-
-    def adam_mats(quarters, first_strip, strips, previous):
-        return adam_call(
-            info,
+    new_down = None
+    for k in range(2):
+        new_down = adam_call(
+            (down, f_down, s_down),
+            grads[k],
+            (2, 2),
+            (quarter, half),
+            lambda h, j, k=k: (2 * h + k, j),
+            lambda h, j: (h, 0, j),
+            new_down,
+        )
+    new_mats = None
+    for k, first_strip in ((2, 4), (3, 6), (4, 3), (5, 0), (6, 2)):
+        new_mats = adam_call(
             (mats, f_mats, s_mats),
-            quarters,
-            (mats.shape[0] // 2, half),
-            strips,
-            lambda i, j, info: (level_of(i, info), 2 * (first_strip + j) + core_of(i, info)),
-            lambda j: (0, j),
-            previous,
+            grads[k],
+            (2, sizes[k] // half),
+            (quarter, half),
+            lambda h, j, at=first_strip: (0, 2 * (at + j) + h),
+            lambda h, j: (h, 0, j),
+            new_mats,
         )
-
-    new_mats = adam_mats(g_up, 4, 4, None)
-    new_mats = adam_mats(g_out, 3, 1, new_mats)
-    new_mats = adam_mats(g_qkv, 0, 3, new_mats)
     new_vectors, first_vectors, second_vectors = adam_math(
         vectors, f_vectors, s_vectors, grad_vectors, rate_vector, 0.0
     )

time: 512 us -> 382 us (0.75)
  waiting for transfers between devices: 142 us -> 0 us
  Pallas kernels: 299 us -> 358 us
  starting transfers between devices: 28.2 us -> 0 us
  other arithmetic: 21 us -> 3.89 us
    ppermute x41 -> x0, waiting for transfers between devices: 142 us -> none  [permute(): return lax.ppermute(value, BOTH, pairs)]
    pallas_call x14 -> x8, Pallas kernels: 140 us -> 200 us  [the longest x1 165 us: local(): pl.pallas_call(functools.partial(tail_kernel, seqs, buf, tuple(bits), siz...]
    ppermute x41 -> x0, starting transfers between devices: 28.2 us -> none  [permute(): return lax.ppermute(value, BOTH, pairs)]
    convert_element_type x16 -> x0, other arithmetic: 11.1 us -> none  [add_low(): return (a.astype(f32) + b.astype(f32)).astype(bf16)]
    unnamed x52 -> x32, local copies, waits for them, and re-layouts: 13 us -> 14.9 us
  transfers between devices with their start and end apart: 41 -> 0, of which waited for: 13 -> 0; matrix products, arithmetic and copies ran while one was open for 4% -> 0% of each run, Pallas kernels for 25% -> 0%
where the time goes in v3:
time: 382 us; the launch traced here: 381 us
  Pallas kernels  358 us (94%)
  local copies, waits for them, and re-layouts  17.5 us (5%)
  other arithmetic  3.89 us (1%)
    pallas_call x1, Pallas kernels, local(): pl.pallas_call(functools.partial(tail_kernel, seqs, buf, tuple(bits), siz...  165 us
    pallas_call x1, Pallas kernels, local(): pl.pallas_call(functools.partial(attend_kernel, seqs, buf), in_specs=[SME...  119 us
    pallas_call x1, Pallas kernels, local(): pl.pallas_call(functools.partial(feed_kernel, seqs, buf), in_specs=[SMEM_...  39.7 us
    pallas_call x7, Pallas kernels, adam_call(): pl.pallas_call(adam_kernel, grid=grid, in_specs=[spec] * 3 + [pl.BlockSpe...  34.3 us
    unnamed x32, local copies, waits for them, and re-layouts  14.9 us

profile of v3, /device:TPU:0, one launch (start us, length us, event | category | flops | bytes accessed | tf_op | source)
XLA Modules:
  0.0 381.0 jit_solution(9567138382106170377)
XLA Ops:
  0.6 0.8 reduce_sum.9
  1.5 0.5 broadcast_add_fusion.refs_0_
  2.0 1.3 reshape.38.refs_1_
  3.2 118.9 %shard_map.235 = (bf16[2,1024,2048]{2,1,0:T(8,128)(2,1)}, bf16[2,1024,2048]{2,1,0:T(8,128)(2,1)}, bf16[2,2048,1024]{2,1,0:T(8,128)(2,1)}, bf16[576,1024]{1,0:T(8...) custom-call(s32[4]{0:T(128)} %broadcast_add_fusion.refs_0_, ...), custom_call_target="tpu_custom_call" | custom-call | flops 19327352832 | bytes 11796480 | tf_op jit(solution)/shard_map/pallas_call | solution.py:855
  122.1 39.7 %shard_map.236 = (bf16[2,576,1024]{2,1,0:T(8,128)(2,1)}, bf16[576,2048]{1,0:T(8,128)(2,1)}, f32[576,1024]{1,0:T(8,128)}, bf16[576,1024]{1,0:T(8,128)(2,1)}, bf16...) custom-call(s32[4]{0:T(128)} %broadcast_add_fusion.refs_0_, ...), custom_call_target="tpu_custom_call" | custom-call | flops 19327352832 | bytes 35389440 | tf_op jit(solution)/shard_map/pallas_call | solution.py:892
  161.8 165.4 %shard_map.237 = (f32[16,1024]{1,0:T(8,128)}, f32[4,320,1024]{2,1,0:T(8,128)}, bf16[2,256,1024]{2,1,0:T(8,128)(2,1)}, bf16[2,256,1024]{2,1,0:T(8,128)(2,1)}, bf1...) custom-call(s32[4]{0:T(128)} %broadcast_add_fusion.refs_0_, ...), custom_call_target="tpu_custom_call" | custom-call | flops 19327352832 | bytes 58982400 | tf_op jit(solution)/shard_map/pallas_call | solution.py:929
  327.2 0.0 copy-start
  327.3 3.4 copy-done
  330.6 0.0 copy-start.7
  330.6 1.2 copy-done.7
  331.9 0.0 copy-start.6
  331.9 6.3 %shard_map.238 = (f32[256,8192]{1,0:T(8,128)}, f32[256,8192]{1,0:T(8,128)}, f32[256,8192]{1,0:T(8,128)}, bf16[256,8192]{1,0:T(8,128)(2,1)}) custom-call(f32[256,8192]{1,0:T(8,128)S(1)} %copy-done, f32[256,8192]{1,0:T(8,128)} %f.11, f32[256,8192]{1,0:T(8,128)} %s.11, bf16[2,256,1024]{2,1,0:T(8,128)(2,1)S(1)} %copy-done.7), custom_call_target="tpu_custom_call" | custom-call | flops 10485760 | bytes 14680064 | tf_op jit(solution)/shard_map/pallas_call | solution.py:830
  338.1 0.0 copy-done.6
  338.1 0.0 copy-start.10
  338.1 6.3 %shard_map.239 = (f32[256,8192]{1,0:T(8,128)}, f32[256,8192]{1,0:T(8,128)}, f32[256,8192]{1,0:T(8,128)}, bf16[256,8192]{1,0:T(8,128)(2,1)}) custom-call(f32[256,8192]{1,0:T(8,128)S(1)} %copy-done, f32[256,8192]{1,0:T(8,128)} %f.11, f32[256,8192]{1,0:T(8,128)} %s.11, ...), custom_call_target="tpu_custom_call", output_to_operand_aliasing={{0}: (4, {}), {1}: (5, {}), {2}: (6, {}), {3}: (7, {})} | custom-call | flops 10485760 | bytes 14680064 | tf_op jit(solution)/shard_map/pallas_call | solution.py:830
  344.4 0.0 copy-done.10
  344.4 0.0 copy-start.5
  344.4 3.6 shard_map.240
  348.0 0.0 copy-done.5
  348.0 0.0 copy-start.9
  348.0 6.3 %shard_map.241 = (f32[256,8192]{1,0:T(8,128)}, f32[256,8192]{1,0:T(8,128)}, f32[256,8192]{1,0:T(8,128)}, bf16[256,8192]{1,0:T(8,128)(2,1)}) custom-call(f32[256,8192]{1,0:T(8,128)S(1)} %copy-done, f32[256,8192]{1,0:T(8,128)} %f.11, f32[256,8192]{1,0:T(8,128)} %s.11, ...), custom_call_target="tpu_custom_call", output_to_operand_aliasing={{0}: (4, {}), {1}: (5, {}), {2}: (6, {}), {3}: (7, {})} | custom-call | flops 10485760 | bytes 14680064 | tf_op jit(solution)/shard_map/pallas_call | solution.py:830
  354.2 0.0 copy-done.9
  354.2 0.0 copy-start.1
  354.3 0.0 copy-start.2
  354.3 0.0 copy-start.3
  354.3 0.0 copy-start.8
  354.3 3.7 shard_map.242
  358.0 0.0 copy-done.1
  358.0 1.7 copy-done.2
  359.7 1.2 copy-done.3
  360.9 0.2 copy-done.8
  361.1 0.0 copy-start.4
  361.1 4.1 %shard_map.243 = (f32[1024,1024]{1,0:T(8,128)}, f32[1024,1024]{1,0:T(8,128)}, f32[1024,1024]{1,0:T(8,128)}, bf16[1024,1024]{1,0:T(8,128)(2,1)}) custom-call(f32[1024,1024]{1,0:T(8,128)S(1)} %copy-done.1, f32[1024,1024]{1,0:T(8,128)S(1)} %copy-done.2, f32[1024,1024]{1,0:T(8,128)S(1)} %copy-done.3, bf16[2,256,1024]{2,1,0:T(8,128)(2,1)S(1)} %copy-done.8), custom_call_target="tpu_custom_call" | custom-call | flops 10485760 | bytes 14680064 | tf_op jit(solution)/shard_map/pallas_call | solution.py:830
  365.2 0.0 copy-done.4
  365.2 0.0 copy-start.12
  365.2 0.0 copy-start.13
  365.2 0.0 copy-start.14
  365.2 0.0 copy-start.11
  365.2 4.1 %shard_map.244 = (f32[1024,1024]{1,0:T(8,128)}, f32[1024,1024]{1,0:T(8,128)}, f32[1024,1024]{1,0:T(8,128)}, bf16[1024,1024]{1,0:T(8,128)(2,1)}) custom-call(f32[1024,1024]{1,0:T(8,128)S(1)} %copy-done.1, f32[1024,1024]{1,0:T(8,128)S(1)} %copy-done.2, ...), custom_call_target="tpu_custom_call", output_to_operand_aliasing={{0}: (4, {}), {1}: (5, {}), {2}: (6, {}), {3}: (7, {})} | custom-call | flops 10485760 | bytes 14680064 | tf_op jit(solution)/shard_map/pallas_call | solution.py:830
  369.4 0.0 copy-done.12
  369.4 0.0 copy-done.13
  369.4 0.0 copy-done.14
  369.4 1.4 fusion.1
  370.7 1.3 slice.7
  372.6 1.2 sqrt_bitcast_fusion
  373.8 0.0 copy-done.11
  373.8 1.5 copy.69
  375.3 5.7 %copy.70 = f32[4,320,1024]{2,1,0:T(8,128)} copy(f32[4,320,1024]{2,1,0:T(8,128)} %get-tuple-element.153) | data formatting | bytes 10485760
Async XLA Ops:
  327.2 3.4 copy-start
  330.6 1.2 copy-start.7
  331.9 6.3 %copy-start.6 = (bf16[2,256,1024]{2,1,0:T(8,128)(2,1)S(1)}, bf16[2,256,1024]{2,1,0:T(8,128)(2,1)}, u32[]{:S(2)}) copy-start(bf16[2,256,1024]{2,1,0:T(8,128)(2,1)} %get-tuple-element.100.grad) | copy-start | bytes 3145732
  338.1 6.3 %copy-start.10 = (bf16[2,256,512]{2,1,0:T(8,128)(2,1)S(1)}, bf16[2,256,512]{2,1,0:T(8,128)(2,1)}, u32[]{:S(2)}) copy-start(bf16[2,256,512]{2,1,0:T(8,128)(2,1)} %get-tuple-element.99.grad) | copy-start | bytes 1572868
  344.4 3.6 copy-start.5
  348.0 6.3 %copy-start.9 = (bf16[2,256,512]{2,1,0:T(8,128)(2,1)S(1)}, bf16[2,256,512]{2,1,0:T(8,128)(2,1)}, u32[]{:S(2)}) copy-start(bf16[2,256,512]{2,1,0:T(8,128)(2,1)} %get-tuple-element.97.grad) | copy-start | bytes 1572868
  354.2 3.7 copy-start.1
  354.3 5.4 %copy-start.2 = (f32[1024,1024]{1,0:T(8,128)S(1)}, f32[1024,1024]{1,0:T(8,128)}, u32[]{:S(2)}) copy-start(f32[1024,1024]{1,0:T(8,128)} %f.13) | copy-start | bytes 12582916
  354.3 6.6 %copy-start.3 = (f32[1024,1024]{1,0:T(8,128)S(1)}, f32[1024,1024]{1,0:T(8,128)}, u32[]{:S(2)}) copy-start(f32[1024,1024]{1,0:T(8,128)} %s.13) | copy-start | bytes 12582916
  354.3 6.8 %copy-start.8 = (bf16[2,256,1024]{2,1,0:T(8,128)(2,1)S(1)}, bf16[2,256,1024]{2,1,0:T(8,128)(2,1)}, u32[]{:S(2)}) copy-start(bf16[2,256,1024]{2,1,0:T(8,128)(2,1)} %get-tuple-element.120.grad) | copy-start | bytes 3145732
  361.1 4.1 %copy-start.4 = (bf16[2,256,1024]{2,1,0:T(8,128)(2,1)S(1)}, bf16[2,256,1024]{2,1,0:T(8,128)(2,1)}, u32[]{:S(2)}) copy-start(bf16[2,256,1024]{2,1,0:T(8,128)(2,1)} %get-tuple-element.119.grad) | copy-start | bytes 3145732
  365.2 4.2 %copy-start.12 = (f32[12,256]{1,0:T(8,128)S(1)}, f32[12,256]{1,0:T(8,128)}, u32[]{:S(2)}) copy-start(f32[12,256]{1,0:T(8,128)} %refs_2_.1) | copy-start | bytes 36868
  365.2 4.2 %copy-start.13 = (f32[12,256]{1,0:T(8,128)S(1)}, f32[12,256]{1,0:T(8,128)}, u32[]{:S(2)}) copy-start(f32[12,256]{1,0:T(8,128)} %param.20) | copy-start | bytes 36868
  365.2 4.2 %copy-start.14 = (f32[12,256]{1,0:T(8,128)S(1)}, f32[12,256]{1,0:T(8,128)}, u32[]{:S(2)}) copy-start(f32[12,256]{1,0:T(8,128)} %param.23) | copy-start | bytes 36868
  365.2 8.6 %copy-start.11 = (bf16[4,320,1024]{2,1,0:T(8,128)(2,1)S(1)}, bf16[4,320,1024]{2,1,0:T(8,128)(2,1)}, u32[]{:S(2)}) copy-start(bf16[4,320,1024]{2,1,0:T(8,128)(2,1)} %get-tuple-element.152) | copy-start | bytes 7864324

commit v4 on v3

--- a/solution.py
+++ b/solution.py
@@ -112,61 +112,82 @@
         pl.semaphore_wait(barrier, len(partners))
 
 
+class Timeline:
+    def __init__(self):
+        self.steps = []
+
+    def add(self, when, step):
+        self.steps.append((when, len(self.steps), step))
+        self.steps.sort(key=lambda one: one[:2])
+
+    def until(self, when):
+        while self.steps and self.steps[0][0] <= when:
+            self.steps.pop(0)[2]()
+
+    def during(self, count, start, gap):
+        due = []
+        while self.steps and self.steps[0][0] < start + count * gap:
+            when, _, step = self.steps.pop(0)
+            due.append((min(max(int((when - start) / gap), 0), count - 1), step))
+
+        def run(turn):
+            for at, step in due:
+                pl.when(turn == at)(step)
+
+        return run
+
+
 class Gather:
-    def __init__(self, place, own, full, send, recv):
-        self.place, self.own, self.full, self.send, self.recv = place, own, full, send, recv
+    def __init__(self, place, own, full, cols, send, recv):
+        self.place, self.own, self.full, self.cols, self.send, self.recv = place, own, full, cols, send, recv
         deep = own.shape[0]
         self.deep, self.strip = deep, 5 * deep // 16
         self.main = deep - self.strip
         self.main_at = place.level * self.strip
         self.strip_at = place.level * self.main
 
-    def block(self, owner, start, size):
+    def block(self, owner, start, size, core=None):
         at = pl.multiple_of(owner * self.deep + start, 16)
-        return self.full.at[self.place.core, pl.ds(at, size), :]
-
-    def make(self, k, owner, start, size, device):
-        view = self.block(owner, start, size)
+        return self.full.at[self.place.core if core is None else core, pl.ds(at, size), self.cols]
+
+    def whole(self, owner, core=None):
+        return self.block(owner, 0, self.deep, core)
+
+    def copy(self, k):
+        p = self.place
+        main, strip, whole = (self.main_at, self.main), (self.strip_at, self.strip), (0, self.deep)
+        owner, (at, size), device = (
+            (p.group, main, p.to_first),
+            (p.group, main, p.to_second),
+            (p.first, main, p.to_second),
+            (p.first, strip, p.to_bit(2)),
+            (p.second, strip, p.to_bit(2)),
+            (p.third, strip, p.to_bit(2)),
+            (p.group, whole, p.to_core),
+            (p.first, whole, p.to_core),
+            (p.second, whole, p.to_core),
+            (p.third, whole, p.to_core),
+        )[k]
+        dst = self.block(owner, at, size)
+        src = dst
+        if k in (0, 1, 6):
+            src = self.own.at[pl.ds(pl.multiple_of(at, 16) if k < 6 else 0, size), :]
         return pltpu.make_async_remote_copy(
-            src_ref=view, dst_ref=view, send_sem=self.send.at[k], recv_sem=self.recv.at[k],
+            src_ref=src, dst_ref=dst, send_sem=self.send.at[k], recv_sem=self.recv.at[k],
             device_id=device, device_id_type=MESH,
         )
 
-    def plan(self, k):
-        p = self.place
-        main, strip, whole = (self.main_at, self.main), (self.strip_at, self.strip), (0, self.deep)
-        return (
-            (p.group, *main, p.to_first),
-            (p.group, *main, p.to_second),
-            (p.first, *main, p.to_second),
-            (p.first, *strip, p.to_bit(2)),
-            (p.second, *strip, p.to_bit(2)),
-            (p.third, *strip, p.to_bit(2)),
-            (p.group, *whole, p.to_core),
-            (p.first, *whole, p.to_core),
-            (p.second, *whole, p.to_core),
-            (p.third, *whole, p.to_core),
-        )[k]
-
     def start(self, *ks):
         for k in ks:
-            owner, at, size, device = self.plan(k)
-            if k in (0, 1, 6):
-                start = pl.multiple_of(at, 16) if k < 6 else 0
-                pltpu.make_async_remote_copy(
-                    src_ref=self.own.at[pl.ds(start, size), :], dst_ref=self.block(owner, at, size),
-                    send_sem=self.send.at[k], recv_sem=self.recv.at[k], device_id=device, device_id_type=MESH,
-                ).start()
-            else:
-                self.make(k, owner, at, size, device).start()
+            self.copy(k).start()
 
     def arrived(self, *ks):
         for k in ks:
-            self.make(k, *self.plan(k)).wait_recv()
+            self.copy(k).wait_recv()
 
     def sent(self, *ks):
         for k in ks:
-            self.make(k, *self.plan(k)).wait_send()
+            self.copy(k).wait_send()
 
     def step_one(self):
         self.start(0, 1, 6)
@@ -177,14 +198,16 @@
         self.arrived(1)
         self.start(4)
 
-    def step_three(self):
-        self.arrived(2)
-        self.start(5)
+    def step_near(self):
         self.arrived(3)
         self.start(7)
         self.arrived(4)
         self.start(8)
 
+    def step_third(self):
+        self.arrived(2)
+        self.start(5)
+
     def step_four(self):
         self.arrived(5)
         self.start(9)
@@ -192,6 +215,14 @@
     def step_five(self):
         self.arrived(6, 7, 8, 9)
         self.sent(*range(10))
+
+    def schedule(self, line, start, size):
+        line.add(start, self.step_one)
+        line.add(start + 8 * size + 2, self.step_two)
+        line.add(start + 12 * size + 4, self.step_third)
+        line.add(start + 14 * size + 4.5, self.step_near)
+        line.add(start + 16 * size + 6, self.step_four)
+        line.add(start + 17 * size + 8, self.step_five)
 
 
 def head_masks():
@@ -220,8 +251,8 @@
 
 def attend_kernel(seqs, buf, *refs):
     counts, keep, vectors, mats, down, tokens, cot = refs[:7]
-    w_attn, w_up, w_down, x, em, h1, vec, qkv, o, r, h2, stats = refs[7:19]
-    wbuf, wide, tall, low_up, low_down, rows_in, parts, send, recv, vec_send, vec_recv, loads, stores, reads = refs[19:]
+    w_attn, w_up, w_down, own_down, x_out, em_out, h1_out, qkv_out, o_out, r_out, h2_out, vec, stats = refs[7:20]
+    x, em, h1, qkv, o, r, h2, outs, wbuf, wide, tall, low_up, low_down, rows_in, parts, send, recv, vec_send, vec_recv, loads, stores, reads = refs[20:]
     rows = h1.shape[0] // seqs
     d = h1.shape[1]
     half = d // 2
@@ -257,86 +288,98 @@
             send_sem=vec_send.at[k], recv_sem=vec_recv.at[k], device_id=partner, device_id_type=MESH,
         ).start()
 
-    for one in takes[:4]:
-        one.wait()
-    own = wbuf.at[core, pl.ds(pl.multiple_of(place.group * deep, deep), deep), :]
-    own[...] = wide[0].astype(bf16)
-    attn = Gather(place, own, wbuf, send.at[0], recv.at[0])
-    attn.step_one()
-    for one in takes[4:]:
-        one.wait()
-    low_up[...] = wide[1].astype(bf16)
-    low_down[...] = tall[...].astype(bf16)
-    up = Gather(place, low_up, w_up, send.at[1], recv.at[1])
-    downs = Gather(place, low_down, w_down, send.at[2], recv.at[2])
-    keep_up = pltpu.make_async_copy(low_up, up.block(place.group, 0, deep), stores.at[0])
-    keep_down = pltpu.make_async_copy(low_down, downs.block(place.group, 0, half), stores.at[1])
-    keep_up.start()
-    keep_down.start()
+    own_rows = pl.ds(pl.multiple_of(place.group * deep, deep), deep)
+    line = Timeline()
+    attn = []
+    for j in range(4):
+        cols = pl.ds(j * half, half)
+        own = wbuf.at[core, own_rows, cols]
+        takes[j].wait()
+        own[...] = wide[0, :, cols].astype(bf16)
+        attn.append(Gather(place, own, wbuf, cols, send.at[j], recv.at[j]))
+        attn[j].schedule(line, 3.0 * j, 0.5)
+        if j == 0:
+            line.until(0)
+    ups = []
+    for j in range(2):
+        cols = pl.ds(j * d, d)
+        for one in takes[4 + 2 * j : 6 + 2 * j]:
+            one.wait()
+        low_up[j] = wide[1, :, cols].astype(bf16)
+        ups.append(Gather(place, low_up.at[j], w_up, cols, send.at[4 + j], recv.at[4 + j]))
+        ups[j].schedule(line, 14.0 + 10 * j, 1.0)
+    takes[8].wait()
+    for j in range(2):
+        low_down[j] = tall[j * deep : (j + 1) * deep, :].astype(bf16)
+    early = Gather(place, low_down.at[0], w_down, pl.ds(0, d), send.at[6], recv.at[6])
+    early.schedule(line, 34.0, 1.0)
+    keeps = [
+        pltpu.make_async_copy(one.own, one.whole(place.group), stores.at[k]) for k, one in enumerate(ups + [early])
+    ]
+    keeps.append(pltpu.make_async_copy(low_down.at[1], own_down, stores.at[3]))
+    for one in keeps:
+        one.start()
+
+    def keep_out(k, src, dst):
+        one = pltpu.make_async_copy(src, dst, outs.at[k])
+        one.start()
+        keeps.append(one)
 
     for one in reads_in:
         one.wait()
+    due_pack = line.during(seqs, 4.0, 1.0)
 
     @pl.loop(0, seqs)
     def _(n):
+        due_pack(n)
         at = pl.multiple_of(n * rows, 16)
         pick = picker(keep[n], rows - buf)
         for k, dst in ((0, x), (1, em)):
             dst[pl.ds(at, buf), :] = rows_in[k, n, 0:buf, :]
             dst[pl.ds(pl.multiple_of(at + buf, 16), rows - buf), :] = mm(pick, rows_in[k, n, buf:, :]).astype(bf16)
 
-    attn.step_two()
-    for k, partner in enumerate((place.first, place.second, place.third)):
-        got = pltpu.make_async_remote_copy(
+    for k in range(3):
+        pltpu.make_async_remote_copy(
             src_ref=parts.at[place.group], dst_ref=parts.at[place.group],
             send_sem=vec_send.at[k], recv_sem=vec_recv.at[k], device_id=place.to_first, device_id_type=MESH,
-        )
-        got.wait()
+        ).wait()
     vec[...] = jnp.zeros_like(vec)
     for s in range(4):
         vec[:, s * part : (s + 1) * part] = parts[s].astype(f32)
+    due_norm = line.during(seqs, 8.0, 0.7)
 
     @pl.loop(0, seqs)
     def _(n):
+        due_norm(n)
         at = pl.ds(pl.multiple_of(n * rows, 16), rows)
         normal, _ = layer_stats(x[at, :].astype(f32))
         h1[at, :] = (normal * vec[0:1, :] + vec[1:2, :]).astype(bf16)
 
-    up.step_one()
-    attn.step_three()
-    attn.step_four()
-    attn.step_five()
-    keep_attn = pltpu.make_async_copy(wbuf, w_attn, stores.at[2])
-    keep_attn.start()
-
-    @pl.loop(0, 4)
-    def _(i):
-        h, t = i // 2, i % 2
-        tile = half // 2
-        near = pl.multiple_of(i * tile, tile)
-        for j in range(3):
+    keep_out(0, x, x_out)
+    keep_out(1, em, em_out)
+    keep_out(2, h1, h1_out)
+    tile = half // 2
+    for j in range(3):
+        line.until(3.0 * j + 17 * 0.5 + 8)
+
+        @pl.loop(0, 4)
+        def _(i):
+            h, t = i // 2, i % 2
+            near = pl.multiple_of(i * tile, tile)
             w = wbuf[h, :, pl.ds(pl.multiple_of(j * half + t * tile, tile), tile)]
             got = mm(h1[...], w)
             if j != 1:
                 got = got + vec[2 + j // 2 : 3 + j // 2, pl.ds(near, tile)]
             qkv[:, pl.ds(pl.multiple_of(j * d + near, tile), tile)] = got.astype(bf16)
 
-    up.step_two()
-    downs.step_one()
+    keep_out(3, qkv, qkv_out)
     low, high, first = head_masks()
     pairs = d // (2 * HEAD)
-    steps = {
-        4: up.step_three,
-        8: up.step_four,
-        12: downs.step_two,
-        20: downs.step_three,
-        26: downs.step_four,
-    }
+    due = line.during(seqs * pairs, 23.5, 0.6)
 
     @pl.loop(0, seqs * pairs)
     def _(i):
-        for when, step in steps.items():
-            pl.when(i == when)(step)
+        due(i)
         n, j = i // pairs, i % pairs
         at = pl.ds(pl.multiple_of(n * rows, 16), rows)
         lanes = [pl.ds(pl.multiple_of(j * 2 * HEAD + m * d, 2 * HEAD), 2 * HEAD) for m in range(3)]
@@ -344,18 +387,25 @@
         probs = pair_probs(q_pair, qkv[at, lanes[1]], counts[n]).astype(bf16)
         o[at, lanes[0]] = pick_heads(mm(probs, qkv[at, lanes[2]]), first).astype(bf16)
 
+    keep_attn = pltpu.make_async_copy(wbuf, w_attn, stores.at[4])
+    keep_attn.start()
+    keep_out(4, o, o_out)
+    due_mix = line.during(4, 43.0, 1.0)
+
     @pl.loop(0, 4)
     def _(i):
+        due_mix(i)
         h, t = i // 2, i % 2
-        tile = half // 2
         near = pl.ds(pl.multiple_of(i * tile, tile), tile)
         w = wbuf[h, :, pl.ds(pl.multiple_of(3 * half + t * tile, tile), tile)]
         r[:, near] = mm(o[...], w) + vec[4:5, near]
 
+    due_last = line.during(seqs, 47.0, 1.5)
     stats[...] = jnp.zeros_like(stats)
 
     @pl.loop(0, seqs)
     def _(n):
+        due_last(n)
         at = pl.ds(pl.multiple_of(n * rows, 16), rows)
         valid = lax.broadcasted_iota(jnp.int32, (rows, 1), 0) < counts[n]
         valid = jnp.where(valid, 1.0, 0.0)
@@ -368,11 +418,112 @@
         stats[0:1, :] += jnp.sum(inputs * inputs * valid, axis=0, keepdims=True)
         stats[1:2, :] += jnp.sum(branch * branch * valid, axis=0, keepdims=True)
 
-    up.step_five()
-    downs.step_five()
-    keep_up.wait()
-    keep_down.wait()
+    keep_out(5, r, r_out)
+    keep_out(6, h2, h2_out)
+    line.until(1e9)
+    for one in keeps:
+        one.wait()
     keep_attn.wait()
+
+
+class Reduce:
+    def __init__(self, place, bits, g, r1, r2, r3, r4, total, send, recv):
+        self.place, self.bits, self.g, self.r1, self.r2, self.r3, self.r4 = place, bits, g, r1, r2, r3, r4
+        self.total, self.send, self.recv = total, send, recv
+        self.half = g.shape[1] // 2
+        self.hold = r2.at[pl.ds(0, self.half)]
+        self.slots = [r1.at[n // 2 % 2, pl.ds(n % 2 * self.half, self.half)] for n in range(len(bits))]
+
+    def copy(self, k):
+        p = self.place
+        half = self.half
+        mine, other = p.level * half, (1 - p.level) * half
+        at = lambda start: pl.ds(pl.multiple_of(start, 16), half)
+        plans = [
+            lambda: (self.g.at[p.third], self.r1.at[1], p.to_first),
+            lambda: (self.g.at[p.first], self.r1.at[0], p.to_first),
+            lambda: (self.g.at[p.second], self.r2, p.to_second),
+            lambda: (self.g.at[p.group, at(other)], self.r3, p.to_bit(2)),
+            lambda: (self.hold, self.total.at[p.core, at(mine)], p.to_bit(2)),
+            lambda: (self.hold, self.total.at[p.core, at(mine)], p.to_core),
+            lambda: (self.total.at[p.core, at(other)], self.total.at[p.core, at(other)], p.to_core),
+        ]
+        for n, bit in enumerate(self.bits):
+            plans.append(lambda n=n, bit=bit: (self.slots[n], self.r4.at[n], p.to_bit(bit)))
+        src, dst, device = plans[k]()
+        return pltpu.make_async_remote_copy(
+            src_ref=src, dst_ref=dst, send_sem=self.send.at[k], recv_sem=self.recv.at[k],
+            device_id=device, device_id_type=MESH,
+        )
+
+    def begin(self):
+        self.copy(0).start()
+        self.copy(1).start()
+
+    def sent(self, *ks):
+        for k in ks:
+            self.copy(k).wait_send()
+
+    def pass_second(self):
+        self.copy(0).wait_recv()
+        at = self.place.second
+        self.g[at] = (self.g[at].astype(f32) + self.r1[1].astype(f32)).astype(bf16)
+        self.copy(2).start()
+
+    def settle(self):
+        self.copy(1).wait_recv()
+        self.copy(2).wait_recv()
+        at = self.place.group
+        self.g[at] = (self.g[at].astype(f32) + self.r1[0].astype(f32) + self.r2[...].astype(f32)).astype(bf16)
+
+    def pass_replica(self):
+        self.settle()
+        self.copy(3).start()
+
+    def pass_bit(self, n):
+        p = self.place
+        if n == 0:
+            self.copy(3).wait_recv()
+            at = pl.ds(pl.multiple_of(p.level * self.half, 16), self.half)
+            value = self.g[p.group, at].astype(f32) + self.r3[...].astype(f32)
+        else:
+            self.copy(6 + n).wait_recv()
+            value = self.slots[n - 1][...].astype(f32) + self.r4[n - 1].astype(f32)
+        if n < len(self.bits):
+            self.slots[n][...] = value.astype(bf16)
+            self.copy(7 + n).start()
+        else:
+            self.hold[...] = value.astype(bf16)
+            self.copy(4).start()
+            self.copy(5).start()
+            self.stay().start()
+
+    def stay(self):
+        p = self.place
+        at = pl.ds(pl.multiple_of(p.level * self.half, 16), self.half)
+        return pltpu.make_async_copy(self.hold, self.total.at[p.core, at], self.send.at[7 + len(self.bits)])
+
+    def pass_core(self):
+        self.copy(4).wait_recv()
+        self.copy(6).start()
+
+    def finish(self, start=0):
+        self.copy(5).wait_recv()
+        self.copy(6).wait_recv()
+        self.sent(*range(start, 7 + len(self.bits)))
+        self.stay().wait()
+
+
+def block_grads(place, sides, wide, g):
+    quarter = sides.shape[2] // 4
+
+    @pl.loop(0, 4)
+    def _(i):
+        near = place.first * (1 - i // 2) + place.group * (i // 2)
+        over = ((i + 1) // 2) % 2
+        owner = near * (1 - over) + ((1 - place.core) * flip(near, 2) + place.core * flip(near, 1)) * over
+        cols = pl.ds(pl.multiple_of(owner * quarter, quarter), quarter)
+        g[owner] = mm_tn(sides[0, :, cols], sides[1, :, 0:wide]).astype(bf16)
 
 
 def swap_start(place, src, dst, send, recv, k):
@@ -385,55 +536,108 @@
 
 
 def feed_kernel(seqs, buf, *refs):
-    counts, keep, h2, em, r, vec, h2_hbm, em_hbm, ups, downs = refs[:10]
-    z_mine, u_mine, er, ea, out, sums, h2_got, em_got, z_got, u_got = refs[10:20]
-    wup, wdown, m_acc, t_acc, z_yours, u_yours, sems, send, recv = refs[20:]
-    rows = h2.shape[0] // seqs
-    d = h2.shape[1]
+    counts, keep, h2, em, r, vec, h2_hbm, em_hbm, ups, downs, own_down = refs[:11]
+    er, ea, out, sums, part_sum, z_mine, z_got, u_mine, u_got, h2_got, em_got = refs[11:22]
+    wup, wdown, m_acc, t_acc, z_all, u_all, sides, g, r1, r2 = refs[22:32]
+    sems, send, recv, g_send, g_recv, k_sems, t_send, t_recv, r_send, r_recv = refs[32:]
+    total, d = h2.shape
+    rows = total // seqs
     strip = wup.shape[2] // 4
     tile = strip // 2
     place = Place()
-    copies = []
-    for e in range(2):
-        core = (1 - place.core) * (1 - e) + place.core * e
-        copies.append(pltpu.make_async_copy(ups.at[core], wup.at[e], sems.at[e, 0]))
-        copies.append(pltpu.make_async_copy(downs.at[core], wdown.at[e], sems.at[e, 1]))
-    for one in copies:
+    core = place.core
+    late = Gather(place, wdown.at[1, core, pl.ds(pl.multiple_of(place.group * tile, tile), tile)], wdown.at[1], pl.ds(0, d), g_send, g_recv)
+    take_own = pltpu.make_async_copy(own_down, late.own, sems.at[0])
+    take_own.start()
+    takes = [pltpu.make_async_copy(downs, wdown.at[0], sems.at[1])]
+    takes += [pltpu.make_async_copy(ups.at[h], wup.at[h], sems.at[2 + h]) for h in range(2)]
+    for one in takes:
         one.start()
-    place.meet((place.to_core,))
+    place.meet((place.to_core, place.to_second, place.to_first, place.to_bit(2)))
+    take_own.wait()
+    late.step_one()
     swaps = [
         swap_start(place, em_hbm, em_got, send, recv, 0),
         swap_start(place, h2_hbm, h2_got, send, recv, 1),
     ]
+    reduce = Reduce(place, (), g, r1, r2, None, None, None, r_send, r_recv)
+    sides[1, 0:total, :] = em[...]
+    take_em = pltpu.make_async_copy(em_got, sides.at[1, pl.ds(total, total)], sems.at[4])
     sums[...] = jnp.zeros_like(sums)
     m_acc[...] = jnp.zeros_like(m_acc)
     t_acc[...] = jnp.zeros_like(t_acc)
-    for e, z_out, u_out in ((0, z_yours, u_yours), (1, z_mine, u_mine)):
-        core = (1 - place.core) * (1 - e) + place.core * e
-        for one in copies[2 * e : 2 * e + 2]:
-            one.wait()
+    for one in takes:
+        one.wait()
+
+    def tile_copies(k, s, t, away):
+        cols = pl.ds(pl.multiple_of(s * tile, tile), tile)
+        z_to = sides.at[0, pl.ds(0 if not away else total, total), cols] if t == 0 else (z_got if away else z_mine).at[:, cols]
+        pairs = (
+            (z_all.at[(1 - core) if away else core, t, :, cols], z_to),
+            (u_all.at[(1 - core) if away else core, t, :, cols], (u_got if away else u_mine).at[t, :, cols]),
+        )
+        if not away:
+            return [pltpu.make_async_copy(src, dst, k_sems.at[k, n]) for n, (src, dst) in enumerate(pairs)]
+        return [
+            pltpu.make_async_remote_copy(
+                src_ref=src, dst_ref=dst, send_sem=t_send.at[k, n], recv_sem=t_recv.at[k, n],
+                device_id=place.to_core, device_id_type=MESH,
+            )
+            for n, (src, dst) in enumerate(pairs)
+        ]
+
+    def late_last():
+        late.arrived(6, 7, 8, 9)
+        late.sent(*range(10))
+
+    def begin():
+        take_em.wait()
+        for k in range(4):
+            tile_copies(k, 0, 0, False)[0].wait()
+            tile_copies(k, 0, 0, True)[0].wait()
+        block_grads(place, sides, d, g)
+        reduce.begin()
+
+    steps = ({2: swaps[0].wait, 3: late.step_two, 4: late.step_third, 5: late.step_near, 6: late.step_four, 7: late_last},
+             {0: begin, 4: reduce.pass_second, 7: reduce.settle})
+
+    for t in range(2):
 
         @pl.loop(0, 8)
         def _(i):
-            s, t = i // 2, i % 2
-            near = pl.ds(pl.multiple_of(i * tile, tile), tile)
-            far = (pl.ds(8 + s, 1), pl.ds(pl.multiple_of(core * strip + t * tile, tile), tile))
-            w_up = wup[e, :, near]
-            w_down = wdown[e, near, :]
+            for when, step in steps[t].items():
+                pl.when(i == when)(step)
+            if t == 0:
+                pl.when(i == 2)(take_em.start)
+            turn, away = i // 2, i % 2
+            h = (1 - core) * away + core * (1 - away)
+            near = place.group * (1 - turn % 2) + place.first * (turn % 2)
+            over = turn // 2
+            s = near * (1 - over) + ((1 - core) * flip(near, 2) + core * flip(near, 1)) * over
+            cols = pl.ds(pl.multiple_of(s * strip + t * tile, tile), tile)
+            far = (pl.ds(8 + s, 1), pl.ds(pl.multiple_of(h * strip + t * tile, tile), tile))
+            near = pl.ds(pl.multiple_of(s * tile, tile), tile)
+            w_up = wup[h, :, cols]
+            w_down = wdown[t, h, near, :]
             u = mm(h2[...], w_up) + vec[far]
             phi = 0.5 * (1.0 + lax.erf(u * root_half))
             z = (u * phi).astype(bf16)
-            z_out[t, :, pl.ds(pl.multiple_of(s * tile, tile), tile)] = z
+            z_all[h, t, :, near] = z
             slope = phi + u * jnp.exp(-0.5 * u * u) * inverse_root_two_pi
             eu = (mm_nt(em[...], w_down) * slope).astype(bf16)
-            u_out[:, near] = eu
+            u_all[h, t, :, near] = eu
             m_acc[...] += mm(z, w_down)
             t_acc[...] += mm_nt(eu, w_up)
             sums[far] = jnp.sum(eu.astype(f32), axis=0, keepdims=True)
-
-        if e == 0:
-            swaps.append(swap_start(place, z_yours, z_got, send, recv, 2))
-            swaps.append(swap_start(place, u_yours, u_got, send, recv, 3))
+            for side in range(2):
+
+                @pl.when(away == side)
+                def _():
+                    for one in tile_copies(4 * t + turn, s, t, side == 1):
+                        one.start()
+
+    share = pltpu.make_async_copy(g.at[place.group], part_sum, sems.at[0])
+    share.start()
 
     @pl.loop(0, seqs)
     def _(n):
@@ -458,128 +662,26 @@
         sums[6:7, :] += jnp.sum(t, axis=0, keepdims=True)
         sums[7:8, :] += jnp.sum(low, axis=0, keepdims=True)
         sums[12:13, :] += jnp.sum(m * m * valid, axis=0, keepdims=True)
-    for one in swaps:
-        one.wait()
-
-
-class Timeline:
-    def __init__(self):
-        self.steps = []
-
-    def add(self, when, step):
-        self.steps.append((when, len(self.steps), step))
-        self.steps.sort(key=lambda one: one[:2])
-
-    def until(self, when):
-        while self.steps and self.steps[0][0] <= when:
-            self.steps.pop(0)[2]()
-
-    def during(self, count, start, gap):
-        due = []
-        while self.steps and self.steps[0][0] < start + count * gap:
-            when, _, step = self.steps.pop(0)
-            due.append((min(max(int((when - start) / gap), 0), count - 1), step))
-
-        def run(turn):
-            for at, step in due:
-                pl.when(turn == at)(step)
-
-        return run
-
-
-class Reduce:
-    def __init__(self, place, bits, g, r1, r2, r3, r4, total, send, recv):
-        self.place, self.bits, self.g, self.r1, self.r2, self.r3, self.r4 = place, bits, g, r1, r2, r3, r4
-        self.total, self.send, self.recv = total, send, recv
-        self.half = g.shape[1] // 2
-        self.hold = r2.at[pl.ds(0, self.half)]
-        self.slots = [r1.at[n // 2 % 2, pl.ds(n % 2 * self.half, self.half)] for n in range(len(bits))]
-
-    def copy(self, k):
-        p = self.place
-        half = self.half
-        mine, other = p.level * half, (1 - p.level) * half
-        at = lambda start: pl.ds(pl.multiple_of(start, 16), half)
-        plans = [
-            (self.g.at[p.third], self.r1.at[1], p.to_first),
-            (self.g.at[p.first], self.r1.at[0], p.to_first),
-            (self.g.at[p.second], self.r2, p.to_second),
-            (self.g.at[p.group, at(other)], self.r3, p.to_bit(2)),
-            (self.hold, self.total.at[p.core, at(mine)], p.to_bit(2)),
-            (self.hold, self.total.at[p.core, at(mine)], p.to_core),
-            (self.total.at[p.core, at(other)], self.total.at[p.core, at(other)], p.to_core),
-        ]
-        for n, bit in enumerate(self.bits):
-            plans.append((self.slots[n], self.r4.at[n], p.to_bit(bit)))
-        src, dst, device = plans[k]
-        return pltpu.make_async_remote_copy(
-            src_ref=src, dst_ref=dst, send_sem=self.send.at[k], recv_sem=self.recv.at[k],
-            device_id=device, device_id_type=MESH,
-        )
-
-    def begin(self):
-        self.copy(0).start()
-        self.copy(1).start()
-
-    def pass_second(self):
-        self.copy(0).wait_recv()
-        at = self.place.second
-        self.g[at] = (self.g[at].astype(f32) + self.r1[1].astype(f32)).astype(bf16)
-        self.copy(2).start()
-
-    def pass_replica(self):
-        self.copy(1).wait_recv()
-        self.copy(2).wait_recv()
-        at = self.place.group
-        self.g[at] = (self.g[at].astype(f32) + self.r1[0].astype(f32) + self.r2[...].astype(f32)).astype(bf16)
-        self.copy(3).start()
-
-    def pass_bit(self, n):
-        p = self.place
-        if n == 0:
-            self.copy(3).wait_recv()
-            at = pl.ds(pl.multiple_of(p.level * self.half, 16), self.half)
-            value = self.g[p.group, at].astype(f32) + self.r3[...].astype(f32)
-        else:
-            self.copy(6 + n).wait_recv()
-            value = self.slots[n - 1][...].astype(f32) + self.r4[n - 1].astype(f32)
-        if n < len(self.bits):
-            self.slots[n][...] = value.astype(bf16)
-            self.copy(7 + n).start()
-        else:
-            self.hold[...] = value.astype(bf16)
-            self.copy(4).start()
-            self.copy(5).start()
-            self.stay().start()
-
-    def stay(self):
-        p = self.place
-        at = pl.ds(pl.multiple_of(p.level * self.half, 16), self.half)
-        return pltpu.make_async_copy(self.hold, self.total.at[p.core, at], self.send.at[7 + len(self.bits)])
-
-    def pass_core(self):
-        self.copy(4).wait_recv()
-        self.copy(6).start()
-
-    def finish(self):
-        self.copy(5).wait_recv()
-        self.copy(6).wait_recv()
-        for k in range(7 + len(self.bits)):
-            self.copy(k).wait_send()
-        self.stay().wait()
+    swaps[1].wait()
+    reduce.sent(0, 1, 2)
+    share.wait()
+    for k in range(8):
+        for away in (False, True):
+            for one in tile_copies(k, 0, k // 4, away)[0 if k >= 4 else 1 :]:
+                one.wait()
 
 
 def tail_kernel(seqs, buf, bits, sizes, *refs):
     counts, keep, qkv, x, er, vec, stats, sums_feed = refs[:8]
-    z_mine, z_got, em, em_got, h2, h2_got, u_mine, u_got, o, ea, h1, w_attn = refs[8:20]
+    part_sum, z_mine, z_got, em, em_got, h2, h2_got, u_mine, u_got, o, ea, h1, w_attn = refs[8:21]
     chunks = len(sizes)
-    small, out = refs[20:22]
-    totals = refs[22 : 22 + chunks]
-    o_got, ea_got, h1_got, e_got = refs[22 + chunks : 26 + chunks]
-    scratch = refs[26 + chunks :]
+    small, out = refs[21:23]
+    totals = refs[23 : 23 + chunks]
+    o_got, ea_got, h1_got, e_got = refs[23 + chunks : 27 + chunks]
+    scratch = refs[27 + chunks :]
     wbuf, eo, e, t_acc, stage, sides, small_in = scratch[:7]
     buffers = [scratch[7 + k * chunks : 7 + (k + 1) * chunks] for k in range(5)]
-    send, recv, w_sem, ea_sem, side_sems, stage_sem, swap_send, swap_recv, small_send, small_recv = scratch[7 + 5 * chunks :]
+    send, recv, w_sem, ea_sem, first_sem, side_sems, stage_sem, swap_send, swap_recv, small_send, small_recv = scratch[7 + 5 * chunks :]
     total, d = eo.shape
     rows = total // seqs
     half, quarter = d // 2, d // 4
@@ -593,10 +695,10 @@
     take_ea.start()
 
     mine_cols = pl.ds(pl.multiple_of(core * half, half), half)
-    left = [(z_mine.at[0], z_got.at[0]), (z_mine.at[1], z_got.at[1]), (h2, h2_got), (h2, h2_got), (o, o_got), (h1, h1_got), (h1, h1_got)]
+    left = [None, (z_mine, z_got), (h2, h2_got), (h2, h2_got), (o, o_got), (h1, h1_got), (h1, h1_got)]
     right = [
-        (em, em_got), (em, em_got),
-        (u_mine.at[:, pl.ds(0, d)], u_got.at[:, pl.ds(0, d)]), (u_mine.at[:, pl.ds(d, d)], u_got.at[:, pl.ds(d, d)]),
+        None, (em, em_got),
+        (u_mine.at[0], u_got.at[0]), (u_mine.at[1], u_got.at[1]),
         (ea.at[:, mine_cols], ea_got.at[:, mine_cols]),
         (e.at[core, :, pl.ds(0, d)], e_got.at[:, pl.ds(0, d)]), (e.at[core, :, pl.ds(d, half)], e_got.at[:, pl.ds(d, half)]),
     ]
@@ -614,8 +716,8 @@
         for one in side_copies(k):
             one.start()
 
-    load_sides(0)
     load_sides(1)
+    load_sides(2)
     partners = [place.to_first, place.to_second, place.to_core, place.to_bit(2)] + [place.to_bit(b) for b in bits]
     place.meet(partners)
     swaps = [
@@ -631,56 +733,51 @@
         Reduce(place, bits, *(buffers[b][k] for b in range(5)), totals[k], send.at[k], recv.at[k]) for k in range(chunks)
     ]
 
+    first_sum = pltpu.make_async_copy(part_sum, buffers[0][0].at[place.group], first_sem)
+    first_sum.start()
+
     def gradient(k):
         for one in side_copies(k):
             one.wait()
-        wide = sizes[k]
-
-        @pl.loop(0, 4)
-        def _(i):
-            near = place.first * (1 - i // 2) + place.group * (i // 2)
-            over = ((i + 1) // 2) % 2
-            bit_two = (1 - core) * flip(near, 2) + core * flip(near, 1)
-            owner = near * (1 - over) + bit_two * over
-            cols = pl.ds(pl.multiple_of(owner * quarter, quarter), quarter)
-            reduces[k].g[owner] = mm_tn(sides[k % 2, 0, :, cols], sides[k % 2, 1, :, 0:wide]).astype(bf16)
+        block_grads(place, sides.at[k % 2], sizes[k], reduces[k].g)
 
     line = Timeline()
     start = 3.0
     for k in range(chunks):
         size = sizes[k] / d
         if k == 5:
-            start = max(start, 58.0)
+            start = max(start, 44.0)
         one = reduces[k]
-        line.add(start, one.begin)
-        when = start + 9.0 * size + 2
-        line.add(when, one.pass_second)
-        when = start + 17.0 * size + 3
-        line.add(when, one.pass_replica)
+        when = 0.0
+        if k:
+            line.add(start, one.begin)
+            when = start + 9.0 * size + 2
+            line.add(when, one.pass_second)
+            when = start + 17.0 * size + 3
+            line.add(when, one.pass_replica)
+            start += 17.0 * size
         when += 7 * size + 2
         for n in range(len(bits) + 1):
             line.add(when, functools.partial(one.pass_bit, n))
             when += 10 * size + 2
         line.add(when, one.pass_core)
-        line.add(when + 6 * size + 3, one.finish)
-        start += 17.0 * size
-
-    gradient(0)
-    load_sides(2)
-    line.until(3)
+        line.add(when + 6 * size + 3, functools.partial(one.finish, 0 if k else 3))
+
     gradient(1)
     load_sides(3)
-    line.until(6)
+    first_sum.wait()
+    reduces[0].copy(3).start()
+    line.until(3)
     gradient(2)
     for one in swaps[:2]:
         one.wait()
     load_sides(4)
+    line.until(6)
+    gradient(3)
     line.until(9)
-    gradient(3)
-    line.until(12)
     gradient(4)
     swaps[2].wait()
-    line.until(14)
+    line.until(12)
     o_weight.wait()
     take_ea.wait()
 
@@ -692,14 +789,14 @@
 
     in_weight = pltpu.make_async_copy(w_attn.at[:, :, pl.ds(0, 3 * half)], wbuf, w_sem)
     in_weight.start()
-    line.until(17)
+    line.until(15)
     low, high, first = head_masks()
     pairs = half // (2 * HEAD)
     scale = 1.0 / math.sqrt(HEAD)
     small[...] = jnp.zeros_like(small)
     turns = seqs * pairs
 
-    due = line.during(2 * turns, 17.0, 0.9)
+    due = line.during(2 * turns, 15.0, 0.7)
 
     @pl.loop(0, 2 * turns)
     def _(i):
@@ -729,12 +826,12 @@
     load_sides(5)
     load_sides(6)
     gradient(5)
-    line.until(48)
+    line.until(42)
     gradient(6)
-    line.until(52)
+    line.until(45)
     in_weight.wait()
 
-    due_in = line.during(4, 52.0, 1.5)
+    due_in = line.during(4, 45.0, 1.2)
 
     @pl.loop(0, 4)
     def _(s):
@@ -742,7 +839,7 @@
         near = pl.ds(pl.multiple_of(s * quarter, quarter), quarter)
         t_acc[:, near] = mm_nt(e[0], wbuf[0, near, :]) + mm_nt(e[1], wbuf[1, near, :])
 
-    due_out = line.during(seqs, 58.0, 2.5)
+    due_out = line.during(seqs, 50.0, 3.0)
 
     @pl.loop(0, seqs)
     def _(n):
@@ -800,7 +897,7 @@
         hop(k).start()
 
     for k in range(len(hops) + 1):
-        line.add(68.0 + 6 * k, functools.partial(small_step, k))
+        line.add(63.0 + 5 * k, functools.partial(small_step, k))
     line.until(1e9)
 
 
@@ -852,83 +949,104 @@
 
     keep3 = keep.reshape(seqs, 1, image)
     deep = mats.shape[0]
-    w_attn, w_up, w_down, x, em, h1, vec, qkv, o, r, h2, stats = pl.pallas_call(
+    w_attn, w_up, w_down, own_down, x, em, h1, qkv, o, r, h2, vec, stats = pl.pallas_call(
         functools.partial(attend_kernel, seqs, buf),
         in_specs=[SMEM_SPEC] + [VMEM_SPEC] * 2 + [ANY_SPEC] * 4,
-        out_specs=[ANY_SPEC] * 3 + [VMEM_SPEC] * 9,
+        out_specs=[ANY_SPEC] * 11 + [VMEM_SPEC] * 2,
         out_shape=[
             sds((2, d, 2 * d), bf16),
             sds((2, d, 2 * d), bf16),
-            sds((2, 2 * d, d), bf16),
+            sds((2, d, d), bf16),
+            sds((deep, d), bf16),
             sds((total, d), bf16),
             sds((total, d), bf16),
             sds((total, d), bf16),
-            sds((16, d), f32),
             sds((total, 3 * d), bf16),
             sds((total, d), bf16),
             sds((total, d), f32),
             sds((total, d), bf16),
+            sds((16, d), f32),
             sds((8, d), f32),
         ],
         scratch_shapes=[
+            pltpu.VMEM((total, d), bf16),
+            pltpu.VMEM((total, d), bf16),
+            pltpu.VMEM((total, d), bf16),
+            pltpu.VMEM((total, 3 * d), bf16),
+            pltpu.VMEM((total, d), bf16),
+            pltpu.VMEM((total, d), f32),
+            pltpu.VMEM((total, d), bf16),
+            pltpu.SemaphoreType.DMA((7,)),
             pltpu.VMEM((2, d, 2 * d), bf16),
             pltpu.VMEM((2, deep, 2 * d), f32),
             pltpu.VMEM((half, d), f32),
-            pltpu.VMEM((deep, 2 * d), bf16),
-            pltpu.VMEM((half, d), bf16),
+            pltpu.VMEM((2, deep, d), bf16),
+            pltpu.VMEM((2, deep, d), bf16),
             pltpu.VMEM((2, seqs, length, d), bf16),
             pltpu.VMEM((4, 16, d // 4), bf16),
-            pltpu.SemaphoreType.DMA((3, 10)),
-            pltpu.SemaphoreType.DMA((3, 10)),
+            pltpu.SemaphoreType.DMA((7, 10)),
+            pltpu.SemaphoreType.DMA((7, 10)),
             pltpu.SemaphoreType.DMA((3,)),
             pltpu.SemaphoreType.DMA((3,)),
             pltpu.SemaphoreType.DMA((9,)),
-            pltpu.SemaphoreType.DMA((3,)),
+            pltpu.SemaphoreType.DMA((5,)),
             pltpu.SemaphoreType.DMA((2, seqs)),
         ],
         compiler_params=params(60, collective_id=0, has_side_effects=True),
         cost_estimate=cost(2 * total * 4 * d * d * 4, 20 * total * d),
     )(counts, keep3, vectors, mats, down, tokens, cot)
-    z_mine, u_mine, er, ea, block_output, sums_feed, h2_got, em_got, z_got, u_got = pl.pallas_call(
+    quarter = d // 4
+    er, ea, block_output, sums_feed, part_sum, z_mine, z_got, u_mine, u_got, h2_got, em_got = pl.pallas_call(
         functools.partial(feed_kernel, seqs, buf),
-        in_specs=[SMEM_SPEC] + [VMEM_SPEC] * 5 + [ANY_SPEC] * 4,
-        out_specs=[VMEM_SPEC] * 6 + [ANY_SPEC] * 4,
+        in_specs=[SMEM_SPEC] + [VMEM_SPEC] * 5 + [ANY_SPEC] * 5,
+        out_specs=[VMEM_SPEC] * 4 + [ANY_SPEC] * 7,
         out_shape=[
-            sds((2, total, d), bf16),
-            sds((total, 2 * d), bf16),
             sds((total, d), f32),
             sds((total, d), bf16),
             sds((seqs, length, d), bf16),
             sds((16, d), f32),
+            sds((quarter, d), bf16),
             sds((total, d), bf16),
             sds((total, d), bf16),
             sds((2, total, d), bf16),
-            sds((total, 2 * d), bf16),
+            sds((2, total, d), bf16),
+            sds((total, d), bf16),
+            sds((total, d), bf16),
         ],
         scratch_shapes=[
             pltpu.VMEM((2, d, 2 * d), bf16),
-            pltpu.VMEM((2, 2 * d, d), bf16),
+            pltpu.VMEM((2, 2, d, d), bf16),
             pltpu.VMEM((total, d), f32),
             pltpu.VMEM((total, d), f32),
-            pltpu.VMEM((2, total, d), bf16),
-            pltpu.VMEM((total, 2 * d), bf16),
-            pltpu.SemaphoreType.DMA((2, 2)),
-            pltpu.SemaphoreType.DMA((4,)),
-            pltpu.SemaphoreType.DMA((4,)),
+            pltpu.VMEM((2, 2, total, d), bf16),
+            pltpu.VMEM((2, 2, total, d), bf16),
+            pltpu.VMEM((2, 2 * total, d), bf16),
+            pltpu.VMEM((4, quarter, d), bf16),
+            pltpu.VMEM((2, quarter, d), bf16),
+            pltpu.VMEM((quarter, d), bf16),
+            pltpu.SemaphoreType.DMA((5,)),
+            pltpu.SemaphoreType.DMA((2,)),
+            pltpu.SemaphoreType.DMA((2,)),
+            pltpu.SemaphoreType.DMA((10,)),
+            pltpu.SemaphoreType.DMA((10,)),
+            pltpu.SemaphoreType.DMA((8, 2)),
+            pltpu.SemaphoreType.DMA((8, 2)),
+            pltpu.SemaphoreType.DMA((8, 2)),
+            pltpu.SemaphoreType.DMA((7,)),
+            pltpu.SemaphoreType.DMA((7,)),
         ],
-        compiler_params=params(60, collective_id=1, has_side_effects=True),
+        compiler_params=params(61, collective_id=1, has_side_effects=True),
         cost_estimate=cost(2 * total * 16 * d * d, 60 * total * d),
-    )(counts, keep3, h2, em, r, vec, h2, em, w_up, w_down)
+    )(counts, keep3, h2, em, r, vec, h2, em, w_up, w_down, own_down)
 
     bits = []
     while (4 << len(bits)) < replicas:
         bits.append(4 << len(bits))
     sizes = (d, d, d, d, half, d, half)
     chunks, steps = len(sizes), 7 + len(bits)
-    quarter = d // 4
     found = pl.pallas_call(
         functools.partial(tail_kernel, seqs, buf, tuple(bits), sizes),
-        in_specs=[SMEM_SPEC] + [VMEM_SPEC] * 7 + [ANY_SPEC] * 12,
+        in_specs=[SMEM_SPEC] + [VMEM_SPEC] * 7 + [ANY_SPEC] * 13,
         out_specs=[VMEM_SPEC, ANY_SPEC] + [ANY_SPEC] * (chunks + 4),
         out_shape=[sds((16, d), f32), sds((seqs, length, d), f32)]
         + [sds((2, quarter, wide), bf16) for wide in sizes]
@@ -953,6 +1071,7 @@
             pltpu.SemaphoreType.DMA((chunks, steps)),
             pltpu.SemaphoreType.DMA(()),
             pltpu.SemaphoreType.DMA(()),
+            pltpu.SemaphoreType.DMA(()),
             pltpu.SemaphoreType.DMA((2, 2, 2)),
             pltpu.SemaphoreType.DMA(()),
             pltpu.SemaphoreType.DMA((4,)),
@@ -962,7 +1081,7 @@
         ],
         compiler_params=params(61, collective_id=2, has_side_effects=True),
         cost_estimate=cost(2 * total * 16 * d * d, 100 * total * d),
-    )(counts, keep3, qkv, x, er, vec, stats, sums_feed, z_mine, z_got, em, em_got, h2, h2_got, u_mine, u_got, o, ea, h1, w_attn)
+    )(counts, keep3, qkv, x, er, vec, stats, sums_feed, part_sum, z_mine, z_got, em, em_got, h2, h2_got, u_mine, u_got, o, ea, h1, w_attn)
     small, input_grad = found[:2]
     grads = found[2 : 2 + chunks]
     branch_rms = jnp.sqrt(small[12, 0:3] / (small[12, 3] * d))
@@ -981,7 +1100,17 @@
             new_down,
         )
     new_mats = None
-    for k, first_strip in ((2, 4), (3, 6), (4, 3), (5, 0), (6, 2)):
+    for t in range(2):
+        new_mats = adam_call(
+            (mats, f_mats, s_mats),
+            grads[2 + t],
+            (2, 4),
+            (quarter, quarter),
+            lambda h, j, t=t: (0, 16 + 4 * j + 2 * h + t),
+            lambda h, j: (h, 0, j),
+            new_mats,
+        )
+    for k, first_strip in ((4, 3), (5, 0), (6, 2)):
         new_mats = adam_call(
             (mats, f_mats, s_mats),
             grads[k],

time: 382 us -> 356 us (0.932)
  Pallas kernels: 358 us -> 331 us
    pallas_call x1, Pallas kernels: 119 us -> 87.9 us  [local(): pl.pallas_call(functools.partial(attend_kernel, seqs, buf), in_specs=[SME...]
    pallas_call x1, Pallas kernels: 39.7 us -> 61.9 us  [local(): pl.pallas_call(functools.partial(feed_kernel, seqs, buf), in_specs=[SMEM_...]
    pallas_call x1, Pallas kernels: 165 us -> 144 us  [local(): pl.pallas_call(functools.partial(tail_kernel, seqs, buf, tuple(bits), siz...]
where the time goes in v4:
time: 356 us; the launch traced here: 354 us
  Pallas kernels  331 us (93%)
  local copies, waits for them, and re-layouts  17.5 us (5%)
  other arithmetic  3.89 us (1%)
    pallas_call x1, Pallas kernels, local(): pl.pallas_call(functools.partial(tail_kernel, seqs, buf, tuple(bits), siz...  144 us
    pallas_call x1, Pallas kernels, local(): pl.pallas_call(functools.partial(attend_kernel, seqs, buf), in_specs=[SME...  87.9 us
    pallas_call x1, Pallas kernels, local(): pl.pallas_call(functools.partial(feed_kernel, seqs, buf), in_specs=[SMEM_...  61.9 us
    pallas_call x7, Pallas kernels, adam_call(): pl.pallas_call(adam_kernel, grid=grid, in_specs=[spec] * 3 + [pl.BlockSpe...  37.3 us
    unnamed x32, local copies, waits for them, and re-layouts  14.9 us

profile of v4, /device:TPU:0, one launch (start us, length us, event | category | flops | bytes accessed | tf_op | source)
XLA Modules:
  0.0 353.6 jit_solution(3520651232277166768)
XLA Ops:
  0.6 0.8 reduce_sum.9
  1.5 0.5 broadcast_add_fusion.refs_0_
  2.0 1.3 reshape.38.refs_1_
  3.2 87.9 %shard_map.235 = (bf16[2,1024,2048]{2,1,0:T(8,128)(2,1)}, bf16[2,1024,2048]{2,1,0:T(8,128)(2,1)}, bf16[2,1024,1024]{2,1,0:T(8,128)(2,1)}, bf16[256,1024]{1,0:T(8...) custom-call(s32[4]{0:T(128)} %broadcast_add_fusion.refs_0_, ...), custom_call_target="tpu_custom_call" | custom-call | flops 19327352832 | bytes 11796480 | tf_op jit(solution)/shard_map/pallas_call | solution.py:952
  91.1 61.9 %shard_map.236 = (f32[576,1024]{1,0:T(8,128)}, bf16[576,1024]{1,0:T(8,128)(2,1)}, bf16[4,320,1024]{2,1,0:T(8,128)(2,1)}, f32[16,1024]{1,0:T(8,128)}, bf16[256,10...) custom-call(s32[4]{0:T(128)} %broadcast_add_fusion.refs_0_, ...), custom_call_target="tpu_custom_call" | custom-call | flops 19327352832 | bytes 35389440 | tf_op jit(solution)/shard_map/pallas_call | solution.py:999
  153.1 143.7 %shard_map.237 = (f32[16,1024]{1,0:T(8,128)}, f32[4,320,1024]{2,1,0:T(8,128)}, bf16[2,256,1024]{2,1,0:T(8,128)(2,1)}, bf16[2,256,1024]{2,1,0:T(8,128)(2,1)}, bf1...) custom-call(s32[4]{0:T(128)} %broadcast_add_fusion.refs_0_, ...), custom_call_target="tpu_custom_call" | custom-call | flops 19327352832 | bytes 58982400 | tf_op jit(solution)/shard_map/pallas_call | solution.py:1047
  296.8 0.0 copy-start
  296.8 3.4 copy-done
  300.2 0.0 copy-start.7
  300.2 1.2 copy-done.7
  301.4 0.0 copy-start.6
  301.4 7.8 %shard_map.238 = (f32[256,8192]{1,0:T(8,128)}, f32[256,8192]{1,0:T(8,128)}, f32[256,8192]{1,0:T(8,128)}, bf16[256,8192]{1,0:T(8,128)(2,1)}) custom-call(f32[256,8192]{1,0:T(8,128)S(1)} %copy-done, f32[256,8192]{1,0:T(8,128)} %f.11, f32[256,8192]{1,0:T(8,128)} %s.11, bf16[2,256,1024]{2,1,0:T(8,128)(2,1)S(1)} %copy-done.7), custom_call_target="tpu_custom_call" | custom-call | flops 10485760 | bytes 14680064 | tf_op jit(solution)/shard_map/pallas_call | solution.py:927
  309.2 0.0 copy-done.6
  309.2 0.0 copy-start.10
  309.2 7.8 %shard_map.239 = (f32[256,8192]{1,0:T(8,128)}, f32[256,8192]{1,0:T(8,128)}, f32[256,8192]{1,0:T(8,128)}, bf16[256,8192]{1,0:T(8,128)(2,1)}) custom-call(f32[256,8192]{1,0:T(8,128)S(1)} %copy-done, f32[256,8192]{1,0:T(8,128)} %f.11, f32[256,8192]{1,0:T(8,128)} %s.11, ...), custom_call_target="tpu_custom_call", output_to_operand_aliasing={{0}: (4, {}), {1}: (5, {}), {2}: (6, {}), {3}: (7, {})} | custom-call | flops 10485760 | bytes 14680064 | tf_op jit(solution)/shard_map/pallas_call | solution.py:927
  316.9 0.0 copy-done.10
  316.9 0.0 copy-start.5
  316.9 3.6 %shard_map.240 = (f32[256,8192]{1,0:T(8,128)}, f32[256,8192]{1,0:T(8,128)}, f32[256,8192]{1,0:T(8,128)}, bf16[256,8192]{1,0:T(8,128)(2,1)}) custom-call(f32[256,8192]{1,0:T(8,128)S(1)} %copy-done, f32[256,8192]{1,0:T(8,128)} %f.11, f32[256,8192]{1,0:T(8,128)} %s.11, ...), custom_call_target="tpu_custom_call", output_to_operand_aliasing={{0}: (4, {}), {1}: (5, {}), {2}: (6, {}), {3}: (7, {})} | custom-call | flops 5242880 | bytes 7340032 | tf_op jit(solution)/shard_map/pallas_call | solution.py:927
  320.5 0.0 copy-done.5
  320.5 0.0 copy-start.9
  320.5 6.3 %shard_map.241 = (f32[256,8192]{1,0:T(8,128)}, f32[256,8192]{1,0:T(8,128)}, f32[256,8192]{1,0:T(8,128)}, bf16[256,8192]{1,0:T(8,128)(2,1)}) custom-call(f32[256,8192]{1,0:T(8,128)S(1)} %copy-done, f32[256,8192]{1,0:T(8,128)} %f.11, f32[256,8192]{1,0:T(8,128)} %s.11, ...), custom_call_target="tpu_custom_call", output_to_operand_aliasing={{0}: (4, {}), {1}: (5, {}), {2}: (6, {}), {3}: (7, {})} | custom-call | flops 10485760 | bytes 14680064 | tf_op jit(solution)/shard_map/pallas_call | solution.py:927
  326.8 0.0 copy-done.9
  326.8 0.0 copy-start.1
  326.8 0.0 copy-start.2
  326.8 0.0 copy-start.3
  326.8 0.0 copy-start.8
  326.8 3.7 %shard_map.242 = (f32[256,8192]{1,0:T(8,128)}, f32[256,8192]{1,0:T(8,128)}, f32[256,8192]{1,0:T(8,128)}, bf16[256,8192]{1,0:T(8,128)(2,1)}) custom-call(f32[256,8192]{1,0:T(8,128)S(1)} %copy-done, f32[256,8192]{1,0:T(8,128)} %f.11, f32[256,8192]{1,0:T(8,128)} %s.11, ...), custom_call_target="tpu_custom_call", output_to_operand_aliasing={{0}: (4, {}), {1}: (5, {}), {2}: (6, {}), {3}: (7, {})} | custom-call | flops 5242880 | bytes 7340032 | tf_op jit(solution)/shard_map/pallas_call | solution.py:927
  330.5 0.0 copy-done.1
  330.5 1.7 copy-done.2
  332.2 1.2 copy-done.3
  333.4 0.2 copy-done.8
  333.6 0.0 copy-start.4
  333.6 4.1 %shard_map.243 = (f32[1024,1024]{1,0:T(8,128)}, f32[1024,1024]{1,0:T(8,128)}, f32[1024,1024]{1,0:T(8,128)}, bf16[1024,1024]{1,0:T(8,128)(2,1)}) custom-call(f32[1024,1024]{1,0:T(8,128)S(1)} %copy-done.1, f32[1024,1024]{1,0:T(8,128)S(1)} %copy-done.2, f32[1024,1024]{1,0:T(8,128)S(1)} %copy-done.3, bf16[2,256,1024]{2,1,0:T(8,128)(2,1)S(1)} %copy-done.8), custom_call_target="tpu_custom_call" | custom-call | flops 10485760 | bytes 14680064 | tf_op jit(solution)/shard_map/pallas_call | solution.py:927
  337.7 0.0 copy-done.4
  337.7 0.0 copy-start.12
  337.7 0.0 copy-start.13
  337.7 0.0 copy-start.14
  337.7 0.0 copy-start.11
  337.7 4.1 %shard_map.244 = (f32[1024,1024]{1,0:T(8,128)}, f32[1024,1024]{1,0:T(8,128)}, f32[1024,1024]{1,0:T(8,128)}, bf16[1024,1024]{1,0:T(8,128)(2,1)}) custom-call(f32[1024,1024]{1,0:T(8,128)S(1)} %copy-done.1, f32[1024,1024]{1,0:T(8,128)S(1)} %copy-done.2, ...), custom_call_target="tpu_custom_call", output_to_operand_aliasing={{0}: (4, {}), {1}: (5, {}), {2}: (6, {}), {3}: (7, {})} | custom-call | flops 10485760 | bytes 14680064 | tf_op jit(solution)/shard_map/pallas_call | solution.py:927
  341.9 0.0 copy-done.12
  341.9 0.0 copy-done.13
  341.9 0.0 copy-done.14
  341.9 1.4 fusion.1
  343.2 1.3 slice.7
  345.2 1.2 sqrt_bitcast_fusion
  346.4 0.0 copy-done.11
  346.4 1.5 copy.69
  347.9 5.7 %copy.70 = f32[4,320,1024]{2,1,0:T(8,128)} copy(f32[4,320,1024]{2,1,0:T(8,128)} %get-tuple-element.157) | data formatting | bytes 10485760
Async XLA Ops:
  296.8 3.4 copy-start
  300.2 1.2 copy-start.7
  301.4 7.8 %copy-start.6 = (bf16[2,256,1024]{2,1,0:T(8,128)(2,1)S(1)}, bf16[2,256,1024]{2,1,0:T(8,128)(2,1)}, u32[]{:S(2)}) copy-start(bf16[2,256,1024]{2,1,0:T(8,128)(2,1)} %get-tuple-element.104.grad) | copy-start | bytes 3145732
  309.2 7.8 %copy-start.10 = (bf16[2,256,512]{2,1,0:T(8,128)(2,1)S(1)}, bf16[2,256,512]{2,1,0:T(8,128)(2,1)}, u32[]{:S(2)}) copy-start(bf16[2,256,512]{2,1,0:T(8,128)(2,1)} %get-tuple-element.103.grad) | copy-start | bytes 1572868
  316.9 3.6 %copy-start.5 = (bf16[2,256,1024]{2,1,0:T(8,128)(2,1)S(1)}, bf16[2,256,1024]{2,1,0:T(8,128)(2,1)}, u32[]{:S(2)}) copy-start(bf16[2,256,1024]{2,1,0:T(8,128)(2,1)} %get-tuple-element.102.grad) | copy-start | bytes 3145732
  320.5 6.3 %copy-start.9 = (bf16[2,256,512]{2,1,0:T(8,128)(2,1)S(1)}, bf16[2,256,512]{2,1,0:T(8,128)(2,1)}, u32[]{:S(2)}) copy-start(bf16[2,256,512]{2,1,0:T(8,128)(2,1)} %get-tuple-element.101.grad) | copy-start | bytes 1572868
  326.8 3.7 %copy-start.1 = (f32[1024,1024]{1,0:T(8,128)S(1)}, f32[1024,1024]{1,0:T(8,128)}, u32[]{:S(2)}) copy-start(f32[1024,1024]{1,0:T(8,128)} %w.13) | copy-start | bytes 12582916
  326.8 5.4 %copy-start.2 = (f32[1024,1024]{1,0:T(8,128)S(1)}, f32[1024,1024]{1,0:T(8,128)}, u32[]{:S(2)}) copy-start(f32[1024,1024]{1,0:T(8,128)} %f.13) | copy-start | bytes 12582916
  326.8 6.6 %copy-start.3 = (f32[1024,1024]{1,0:T(8,128)S(1)}, f32[1024,1024]{1,0:T(8,128)}, u32[]{:S(2)}) copy-start(f32[1024,1024]{1,0:T(8,128)} %s.13) | copy-start | bytes 12582916
  326.8 6.8 %copy-start.8 = (bf16[2,256,1024]{2,1,0:T(8,128)(2,1)S(1)}, bf16[2,256,1024]{2,1,0:T(8,128)(2,1)}, u32[]{:S(2)}) copy-start(bf16[2,256,1024]{2,1,0:T(8,128)(2,1)} %get-tuple-element.124.grad) | copy-start | bytes 3145732
  333.6 4.1 %copy-start.4 = (bf16[2,256,1024]{2,1,0:T(8,128)(2,1)S(1)}, bf16[2,256,1024]{2,1,0:T(8,128)(2,1)}, u32[]{:S(2)}) copy-start(bf16[2,256,1024]{2,1,0:T(8,128)(2,1)} %get-tuple-element.123.grad) | copy-start | bytes 3145732
  337.7 4.2 %copy-start.12 = (f32[12,256]{1,0:T(8,128)S(1)}, f32[12,256]{1,0:T(8,128)}, u32[]{:S(2)}) copy-start(f32[12,256]{1,0:T(8,128)} %refs_2_.1) | copy-start | bytes 36868
  337.7 4.2 %copy-start.13 = (f32[12,256]{1,0:T(8,128)S(1)}, f32[12,256]{1,0:T(8,128)}, u32[]{:S(2)}) copy-start(f32[12,256]{1,0:T(8,128)} %param.20) | copy-start | bytes 36868
  337.7 4.2 %copy-start.14 = (f32[12,256]{1,0:T(8,128)S(1)}, f32[12,256]{1,0:T(8,128)}, u32[]{:S(2)}) copy-start(f32[12,256]{1,0:T(8,128)} %param.23) | copy-start | bytes 36868
  337.7 8.6 %copy-start.11 = (bf16[4,320,1024]{2,1,0:T(8,128)(2,1)S(1)}, bf16[4,320,1024]{2,1,0:T(8,128)(2,1)}, u32[]{:S(2)}) copy-start(bf16[4,320,1024]{2,1,0:T(8,128)(2,1)} %get-tuple-element.156) | copy-start | bytes 7864324

commit v5 on v4

--- a/solution.py
+++ b/solution.py
@@ -29,6 +29,30 @@
 SMEM_SPEC = pl.BlockSpec(memory_space=pltpu.SMEM)
 ANY_SPEC = pl.BlockSpec(memory_space=pl.ANY)
 MIB = 1 << 20
+GATHER = dict(attn=3.0, up=18.0, up_gap=10.0, down=38.0, two=2.0, third=4.0, near=4.5, four=6.0, five=8.0, loop=23.5, gap=0.9)
+FEED = (4, 6, 7, 9, 10, 15)
+TAIL = {
+    0: ((0, 2), (1, -1), (1, 0)),
+    2: ((2, -1), (0, 3)),
+    6: ((1, 1), (2, 0)),
+    7: ((3, -1),),
+    8: ((1, 2),),
+    10: ((0, 4),),
+    13: ((4, -1), (2, 1)),
+    14: ((1, 3),),
+    15: ((3, 0),),
+    18: ((0, 5),),
+    20: ((2, 2),),
+    26: ((3, 1), (2, 3)),
+    32: ((4, 0), (1, 4)),
+    34: ((3, 2), (5, -1), (4, 1), (5, 0), (2, 4)),
+    36: ((4, 2),),
+    37: ((3, 3), (5, 1), (6, -1), (1, 5)),
+    38: ((4, 3),),
+    40: ((5, 2),),
+    41: ((3, 4),),
+    42: ((1, 6), (6, 0), (5, 3), (6, 1), (9, 10), (3, 5), (9, 11), (0, 6), (9, 12), (6, 2), (9, 13), (4, 4), (6, 3), (9, 14), (5, 4), (2, 5), (9, 15), (6, 4), (5, 5), (4, 5), (3, 6), (6, 5), (9, 16), (5, 6), (2, 6), (4, 6), (6, 6)),
+}
 
 
 def mm(a, b):
@@ -218,11 +242,11 @@
 
     def schedule(self, line, start, size):
         line.add(start, self.step_one)
-        line.add(start + 8 * size + 2, self.step_two)
-        line.add(start + 12 * size + 4, self.step_third)
-        line.add(start + 14 * size + 4.5, self.step_near)
-        line.add(start + 16 * size + 6, self.step_four)
-        line.add(start + 17 * size + 8, self.step_five)
+        line.add(start + 8 * size + GATHER["two"], self.step_two)
+        line.add(start + 12 * size + GATHER["third"], self.step_third)
+        line.add(start + 14 * size + GATHER["near"], self.step_near)
+        line.add(start + 16 * size + GATHER["four"], self.step_four)
+        line.add(start + 17 * size + GATHER["five"], self.step_five)
 
 
 def head_masks():
@@ -297,7 +321,7 @@
         takes[j].wait()
         own[...] = wide[0, :, cols].astype(bf16)
         attn.append(Gather(place, own, wbuf, cols, send.at[j], recv.at[j]))
-        attn[j].schedule(line, 3.0 * j, 0.5)
+        attn[j].schedule(line, GATHER["attn"] * j, 0.5)
         if j == 0:
             line.until(0)
     ups = []
@@ -307,12 +331,12 @@
             one.wait()
         low_up[j] = wide[1, :, cols].astype(bf16)
         ups.append(Gather(place, low_up.at[j], w_up, cols, send.at[4 + j], recv.at[4 + j]))
-        ups[j].schedule(line, 14.0 + 10 * j, 1.0)
+        ups[j].schedule(line, GATHER["up"] + GATHER["up_gap"] * j, 1.0)
     takes[8].wait()
     for j in range(2):
         low_down[j] = tall[j * deep : (j + 1) * deep, :].astype(bf16)
     early = Gather(place, low_down.at[0], w_down, pl.ds(0, d), send.at[6], recv.at[6])
-    early.schedule(line, 34.0, 1.0)
+    early.schedule(line, GATHER["down"], 1.0)
     keeps = [
         pltpu.make_async_copy(one.own, one.whole(place.group), stores.at[k]) for k, one in enumerate(ups + [early])
     ]
@@ -360,7 +384,7 @@
     keep_out(2, h1, h1_out)
     tile = half // 2
     for j in range(3):
-        line.until(3.0 * j + 17 * 0.5 + 8)
+        line.until(GATHER["attn"] * j + 17 * 0.5 + GATHER["five"])
 
         @pl.loop(0, 4)
         def _(i):
@@ -375,7 +399,9 @@
     keep_out(3, qkv, qkv_out)
     low, high, first = head_masks()
     pairs = d // (2 * HEAD)
-    due = line.during(seqs * pairs, 23.5, 0.6)
+    loop_at, turn = GATHER["loop"], GATHER["gap"]
+    due = line.during(seqs * pairs, loop_at, turn)
+    mix_at = loop_at + seqs * pairs * turn
 
     @pl.loop(0, seqs * pairs)
     def _(i):
@@ -390,7 +416,7 @@
     keep_attn = pltpu.make_async_copy(wbuf, w_attn, stores.at[4])
     keep_attn.start()
     keep_out(4, o, o_out)
-    due_mix = line.during(4, 43.0, 1.0)
+    due_mix = line.during(4, mix_at, 1.0)
 
     @pl.loop(0, 4)
     def _(i):
@@ -400,7 +426,7 @@
         w = wbuf[h, :, pl.ds(pl.multiple_of(3 * half + t * tile, tile), tile)]
         r[:, near] = mm(o[...], w) + vec[4:5, near]
 
-    due_last = line.during(seqs, 47.0, 1.5)
+    due_last = line.during(seqs, mix_at + 4, 1.5)
     stats[...] = jnp.zeros_like(stats)
 
     @pl.loop(0, seqs)
@@ -536,10 +562,10 @@
 
 
 def feed_kernel(seqs, buf, *refs):
-    counts, keep, h2, em, r, vec, h2_hbm, em_hbm, ups, downs, own_down = refs[:11]
-    er, ea, out, sums, part_sum, z_mine, z_got, u_mine, u_got, h2_got, em_got = refs[11:22]
-    wup, wdown, m_acc, t_acc, z_all, u_all, sides, g, r1, r2 = refs[22:32]
-    sems, send, recv, g_send, g_recv, k_sems, t_send, t_recv, r_send, r_recv = refs[32:]
+    counts, keep, h2, em, vec, h2_hbm, em_hbm, r_hbm, ups, downs, own_down = refs[:11]
+    sums, er_hbm, ea_hbm, out_hbm, part_sum, z_mine, z_got, u_mine, u_got, h2_got, em_got = refs[11:22]
+    r, er, ea, out, wup, wdown, m_acc, t_acc, z_all, u_all, sides, g, r1, r2 = refs[22:36]
+    sems, w_sems, o_sems, send, recv, g_send, g_recv, k_sems, t_send, t_recv, r_send, r_recv = refs[36:]
     total, d = h2.shape
     rows = total // seqs
     strip = wup.shape[2] // 4
@@ -549,10 +575,28 @@
     late = Gather(place, wdown.at[1, core, pl.ds(pl.multiple_of(place.group * tile, tile), tile)], wdown.at[1], pl.ds(0, d), g_send, g_recv)
     take_own = pltpu.make_async_copy(own_down, late.own, sems.at[0])
     take_own.start()
-    takes = [pltpu.make_async_copy(downs, wdown.at[0], sems.at[1])]
-    takes += [pltpu.make_async_copy(ups.at[h], wup.at[h], sems.at[2 + h]) for h in range(2)]
-    for one in takes:
-        one.start()
+    take_r = pltpu.make_async_copy(r_hbm, r, sems.at[1])
+
+    def owner_at(turn):
+        near = place.group * (1 - turn % 2) + place.first * (turn % 2)
+        over = turn // 2
+        return near * (1 - over) + ((1 - core) * flip(near, 2) + core * flip(near, 1)) * over
+
+    def takes(i):
+        turn, away = i // 2, i % 2
+        h = (1 - core) * away + core * (1 - away)
+        s = owner_at(turn)
+        cols = pl.ds(pl.multiple_of(s * strip, strip), strip)
+        at = pl.ds(pl.multiple_of(s * tile, tile), tile)
+        return [
+            pltpu.make_async_copy(ups.at[h, :, cols], wup.at[h, :, cols], w_sems.at[i, 0]),
+            pltpu.make_async_copy(downs.at[h, at], wdown.at[0, h, at], w_sems.at[i, 1]),
+        ]
+
+    for i in range(8):
+        for one in takes(i):
+            one.start()
+    take_r.start()
     place.meet((place.to_core, place.to_second, place.to_first, place.to_bit(2)))
     take_own.wait()
     late.step_one()
@@ -566,8 +610,6 @@
     sums[...] = jnp.zeros_like(sums)
     m_acc[...] = jnp.zeros_like(m_acc)
     t_acc[...] = jnp.zeros_like(t_acc)
-    for one in takes:
-        one.wait()
 
     def tile_copies(k, s, t, away):
         cols = pl.ds(pl.multiple_of(s * tile, tile), tile)
@@ -586,8 +628,11 @@
             for n, (src, dst) in enumerate(pairs)
         ]
 
+    def late_own():
+        late.arrived(6)
+
     def late_last():
-        late.arrived(6, 7, 8, 9)
+        late.arrived(7, 8, 9)
         late.sent(*range(10))
 
     def begin():
@@ -598,22 +643,23 @@
         block_grads(place, sides, d, g)
         reduce.begin()
 
-    steps = ({2: swaps[0].wait, 3: late.step_two, 4: late.step_third, 5: late.step_near, 6: late.step_four, 7: late_last},
-             {0: begin, 4: reduce.pass_second, 7: reduce.settle})
+    due = [(2, swaps[0].wait), (7, late_own), (8, begin)]
+    due += zip(FEED, (late.step_two, late.step_third, late.step_near, late.step_four, late_last, reduce.pass_second))
+    orders = [[(when - 8 * t, step) for when, step in due if when // 8 == t] for t in range(2)]
 
     for t in range(2):
 
         @pl.loop(0, 8)
         def _(i):
-            for when, step in steps[t].items():
+            for when, step in orders[t]:
                 pl.when(i == when)(step)
             if t == 0:
                 pl.when(i == 2)(take_em.start)
+                for one in takes(i):
+                    one.wait()
             turn, away = i // 2, i % 2
             h = (1 - core) * away + core * (1 - away)
-            near = place.group * (1 - turn % 2) + place.first * (turn % 2)
-            over = turn // 2
-            s = near * (1 - over) + ((1 - core) * flip(near, 2) + core * flip(near, 1)) * over
+            s = owner_at(turn)
             cols = pl.ds(pl.multiple_of(s * strip + t * tile, tile), tile)
             far = (pl.ds(8 + s, 1), pl.ds(pl.multiple_of(h * strip + t * tile, tile), tile))
             near = pl.ds(pl.multiple_of(s * tile, tile), tile)
@@ -636,8 +682,15 @@
                     for one in tile_copies(4 * t + turn, s, t, side == 1):
                         one.start()
 
-    share = pltpu.make_async_copy(g.at[place.group], part_sum, sems.at[0])
-    share.start()
+    take_r.wait()
+
+    def results(n):
+        at = pl.ds(pl.multiple_of(n * rows, 16), rows)
+        return [
+            pltpu.make_async_copy(er.at[at], er_hbm.at[at], o_sems.at[n, 0]),
+            pltpu.make_async_copy(ea.at[at], ea_hbm.at[at], o_sems.at[n, 1]),
+            pltpu.make_async_copy(out.at[n], out_hbm.at[n], o_sems.at[n, 2]),
+        ]
 
     @pl.loop(0, seqs)
     def _(n):
@@ -662,6 +715,14 @@
         sums[6:7, :] += jnp.sum(t, axis=0, keepdims=True)
         sums[7:8, :] += jnp.sum(low, axis=0, keepdims=True)
         sums[12:13, :] += jnp.sum(m * m * valid, axis=0, keepdims=True)
+        for one in results(n):
+            one.start()
+    reduce.settle()
+    share = pltpu.make_async_copy(g.at[place.group], part_sum, sems.at[0])
+    share.start()
+    for n in range(seqs):
+        for one in results(n):
+            one.wait()
     swaps[1].wait()
     reduce.sent(0, 1, 2)
     share.wait()
@@ -672,13 +733,15 @@
 
 
 def tail_kernel(seqs, buf, bits, sizes, *refs):
-    counts, keep, qkv, x, er, vec, stats, sums_feed = refs[:8]
+    counts, keep, vec, stats, sums_feed, qkv_hbm, x_hbm, er_hbm = refs[:8]
     part_sum, z_mine, z_got, em, em_got, h2, h2_got, u_mine, u_got, o, ea, h1, w_attn = refs[8:21]
     chunks = len(sizes)
     small, out = refs[21:23]
     totals = refs[23 : 23 + chunks]
     o_got, ea_got, h1_got, e_got = refs[23 + chunks : 27 + chunks]
     scratch = refs[27 + chunks :]
+    qkv, x, er, in_sems = scratch[:4]
+    scratch = scratch[4:]
     wbuf, eo, e, t_acc, stage, sides, small_in = scratch[:7]
     buffers = [scratch[7 + k * chunks : 7 + (k + 1) * chunks] for k in range(5)]
     send, recv, w_sem, ea_sem, first_sem, side_sems, stage_sem, swap_send, swap_recv, small_send, small_recv = scratch[7 + 5 * chunks :]
@@ -718,6 +781,12 @@
 
     load_sides(1)
     load_sides(2)
+    inputs = [
+        pltpu.make_async_copy(src, dst, in_sems.at[k])
+        for k, (src, dst) in enumerate(((qkv_hbm, qkv), (x_hbm, x), (er_hbm, er)))
+    ]
+    for one in inputs:
+        one.start()
     partners = [place.to_first, place.to_second, place.to_core, place.to_bit(2)] + [place.to_bit(b) for b in bits]
     place.meet(partners)
     swaps = [
@@ -741,45 +810,58 @@
             one.wait()
         block_grads(place, sides.at[k % 2], sizes[k], reduces[k].g)
 
-    line = Timeline()
-    start = 3.0
-    for k in range(chunks):
-        size = sizes[k] / d
-        if k == 5:
-            start = max(start, 44.0)
+    def act(k, step):
+        if k == 9:
+            last = step == 16
+            for n in range(step - 10, len(hops) + 1 if last else step - 9):
+                small_step(n)
+            return
         one = reduces[k]
-        when = 0.0
-        if k:
-            line.add(start, one.begin)
-            when = start + 9.0 * size + 2
-            line.add(when, one.pass_second)
-            when = start + 17.0 * size + 3
-            line.add(when, one.pass_replica)
-            start += 17.0 * size
-        when += 7 * size + 2
-        for n in range(len(bits) + 1):
-            line.add(when, functools.partial(one.pass_bit, n))
-            when += 10 * size + 2
-        line.add(when, one.pass_core)
-        line.add(when + 6 * size + 3, functools.partial(one.finish, 0 if k else 3))
-
-    gradient(1)
-    load_sides(3)
-    first_sum.wait()
-    reduces[0].copy(3).start()
-    line.until(3)
-    gradient(2)
-    for one in swaps[:2]:
-        one.wait()
-    load_sides(4)
-    line.until(6)
-    gradient(3)
-    line.until(9)
-    gradient(4)
-    swaps[2].wait()
-    line.until(12)
+        if step == -1:
+            gradient(k)
+            if k == 1:
+                load_sides(3)
+            if k == 2:
+                for swap in swaps[:2]:
+                    swap.wait()
+                load_sides(4)
+        elif step == 0:
+            one.begin()
+        elif step == 1:
+            one.pass_second()
+        elif step == 2 and k == 0:
+            first_sum.wait()
+            one.copy(3).start()
+        elif step == 2:
+            one.pass_replica()
+        elif step == 3:
+            one.pass_bit(0)
+        elif step == 4:
+            for n in range(1, len(bits) + 1):
+                one.pass_bit(n)
+        elif step == 5:
+            one.pass_core()
+        else:
+            one.finish(0 if k else 3)
+
+    def due(slot, turn=None, count=1):
+        for n in range(count):
+            steps = TAIL.get(slot + n, ())
+
+            def run(steps=steps):
+                for k, step in steps:
+                    act(k, step)
+
+            if turn is None:
+                run()
+            elif steps:
+                pl.when(turn == n)(run)
+
+    due(0)
     o_weight.wait()
     take_ea.wait()
+    for one in inputs:
+        one.wait()
 
     @pl.loop(0, 4)
     def _(s):
@@ -789,19 +871,18 @@
 
     in_weight = pltpu.make_async_copy(w_attn.at[:, :, pl.ds(0, 3 * half)], wbuf, w_sem)
     in_weight.start()
-    line.until(15)
     low, high, first = head_masks()
     pairs = half // (2 * HEAD)
     scale = 1.0 / math.sqrt(HEAD)
     small[...] = jnp.zeros_like(small)
     turns = seqs * pairs
 
-    due = line.during(2 * turns, 15.0, 0.7)
+    planned = 32
 
     @pl.loop(0, 2 * turns)
     def _(i):
         pl.when(i == turns)(sent_e.start)
-        due(i)
+        due(1, i, planned)
         h = (1 - core) * (1 - i // turns) + core * (i // turns)
         n, j = (i % turns) // pairs, i % pairs
         at = pl.ds(pl.multiple_of(n * rows, 16), rows)
@@ -822,28 +903,21 @@
         small[2:3, lanes[0]] += jnp.sum(eq.astype(f32), axis=0, keepdims=True)
         small[3:4, lanes[0]] += jnp.sum(ev.astype(f32), axis=0, keepdims=True)
 
+    due(1 + planned)
     sent_e.wait()
+    swaps[2].wait()
     load_sides(5)
     load_sides(6)
-    gradient(5)
-    line.until(42)
-    gradient(6)
-    line.until(45)
     in_weight.wait()
-
-    due_in = line.during(4, 45.0, 1.2)
-
     @pl.loop(0, 4)
     def _(s):
-        due_in(s)
+        due(2 + planned, s, 4)
         near = pl.ds(pl.multiple_of(s * quarter, quarter), quarter)
         t_acc[:, near] = mm_nt(e[0], wbuf[0, near, :]) + mm_nt(e[1], wbuf[1, near, :])
 
-    due_out = line.during(seqs, 50.0, 3.0)
-
     @pl.loop(0, seqs)
     def _(n):
-        due_out(n)
+        due(6 + planned, n, 4)
         at = pl.ds(pl.multiple_of(n * rows, 16), rows)
         normal, inverse = layer_stats(x[at, :].astype(f32))
         t = t_acc[at, :]
@@ -896,9 +970,7 @@
             small_in[k, 0] = value
         hop(k).start()
 
-    for k in range(len(hops) + 1):
-        line.add(63.0 + 5 * k, functools.partial(small_step, k))
-    line.until(1e9)
+    due(10 + planned)
 
 
 def adam_math(w, f, s, grad, rate, decay):
@@ -906,34 +978,73 @@
     second_new = beta_second * s + (1.0 - beta_second) * grad * grad
     fix_first = 1.0 - beta_first**STEP
     fix_second = 1.0 - beta_second**STEP
-    update = first_new / fix_first / (jnp.sqrt(second_new / fix_second) + adam_epsilon)
+    update = first_new * (1.0 / fix_first) / (jnp.sqrt(second_new * (1.0 / fix_second)) + adam_epsilon)
     return w - rate * (update + decay * w), first_new, second_new
 
 
-def adam_kernel(w, f, s, grad, *rest):
-    w_out, f_out, s_out, low_out = rest[-4:]
-    new, first, second = adam_math(w[...], f[...], s[...], grad[0].astype(f32), rate_matrix, weight_decay)
-    w_out[...] = new
-    f_out[...] = first
-    s_out[...] = second
-    low_out[...] = new.astype(bf16)
-
-
-def adam_call(state, grad, grid, block, place, grad_place, previous=None):
-    spec = pl.BlockSpec(block, place)
-    shape = state[0].shape
-    extra = [] if previous is None else list(previous)
-    size = grid[0] * grid[1] * block[0] * block[1]
+def adam_kernel(columns, info, *refs):
+    (w, f, s, wd, fd, sd, wv, fv, sv, small, d0, d1, u0, u1, go, g1, g2) = refs[:17]
+    mats, downs, vecs = refs[17:21], refs[21:25], refs[25:29]
+    step = pl.program_id(0)
+
+    def put(outs, state, grad, rate, decay):
+        new, first, second = adam_math(*(one[...] for one in state), grad, rate, decay)
+        for out, value in zip(outs, (new, first, second, new.astype(bf16))):
+            out[...] = value
+
+    def when(lowest, count, *parts):
+        @pl.when((step >= lowest) & (step < lowest + count))
+        def _():
+            grad = jnp.concatenate([part[h] for h in range(2) for part in parts], axis=1)
+            put(mats, (w, f, s), grad.astype(f32), rate_matrix, weight_decay)
+
+    when(0, 2, g1)
+    when(2, 1, g2)
+    when(3, 1, go)
+    when(4, 4, u0, u1)
+    for k, part in ((0, d0), (1, d1)):
+
+        @pl.when((step >= columns) & ((step - columns) % 2 == k))
+        def _():
+            put(downs, (wd, fd, sd), part[0].astype(f32), rate_matrix, weight_decay)
+
+    @pl.when(step == 0)
+    def _():
+        size = wv.shape[1]
+        grad = small[0:12, pl.ds(pl.multiple_of(info[0] * size, size), size)]
+        put(vecs, (wv, fv, sv), grad, rate_vector, 0.0)
+
+
+def adam_call(group, mats, downs, vecs, small, grads):
+    deep, wide = mats[0].shape
+    tile = downs[0].shape[1]
+    columns, rest = wide // tile, downs[0].shape[0] // deep
+    clip = lambda value, most: jnp.clip(value, 0, most - 1)
+    block = (deep, tile)
+    mat = pl.BlockSpec(block, lambda i, info: (0, clip(i, columns)))
+    row = lambda i: clip(i - columns, rest)
+    down = pl.BlockSpec(block, lambda i, info: (row(i), 0))
+    vec = pl.BlockSpec(vecs[0].shape, lambda i, info: (0, 0))
+    small_spec = pl.BlockSpec(small.shape, lambda i, info: (0, 0))
+    down_grad = pl.BlockSpec((1, *block), lambda i, info: (row(i) // 2, 0, 0))
+    halves = lambda start, count, width: pl.BlockSpec((2, deep, width), lambda i, info: (0, 0, clip(i - start, count)))
+    shapes = []
+    for state in (mats, downs, vecs):
+        shapes += [sds(state[0].shape, f32)] * 3 + [sds(state[0].shape, bf16)]
+    size = sum(one[0].size for one in (mats, downs))
     return pl.pallas_call(
-        adam_kernel,
-        grid=grid,
-        in_specs=[spec] * 3 + [pl.BlockSpec((1, *block), grad_place)] + [ANY_SPEC] * len(extra),
-        out_specs=[spec] * 4,
-        out_shape=[sds(shape, f32)] * 3 + [sds(shape, bf16)],
-        input_output_aliases={4 + k: k for k in range(len(extra))},
-        compiler_params=params(40),
+        functools.partial(adam_kernel, columns),
+        grid_spec=pltpu.PrefetchScalarGridSpec(
+            num_scalar_prefetch=1,
+            grid=(columns + rest,),
+            in_specs=[mat] * 3 + [down] * 3 + [vec] * 3 + [small_spec] + [down_grad] * 2
+            + [halves(4, 4, tile // 4)] * 2 + [halves(3, 1, tile // 2), halves(0, 2, tile // 2), halves(2, 1, tile // 2)],
+            out_specs=[mat] * 4 + [down] * 4 + [vec] * 4,
+        ),
+        out_shape=shapes,
+        compiler_params=params(60),
         cost_estimate=cost(20 * size, 28 * size),
-    )(*state, grad, *extra)
+    )(group, *mats, *downs, *vecs, small, *grads)
 
 
 def local(groups, replicas, *args):
@@ -996,15 +1107,15 @@
         cost_estimate=cost(2 * total * 4 * d * d * 4, 20 * total * d),
     )(counts, keep3, vectors, mats, down, tokens, cot)
     quarter = d // 4
-    er, ea, block_output, sums_feed, part_sum, z_mine, z_got, u_mine, u_got, h2_got, em_got = pl.pallas_call(
+    sums_feed, er, ea, block_output, part_sum, z_mine, z_got, u_mine, u_got, h2_got, em_got = pl.pallas_call(
         functools.partial(feed_kernel, seqs, buf),
-        in_specs=[SMEM_SPEC] + [VMEM_SPEC] * 5 + [ANY_SPEC] * 5,
-        out_specs=[VMEM_SPEC] * 4 + [ANY_SPEC] * 7,
+        in_specs=[SMEM_SPEC] + [VMEM_SPEC] * 4 + [ANY_SPEC] * 6,
+        out_specs=[VMEM_SPEC] + [ANY_SPEC] * 10,
         out_shape=[
+            sds((16, d), f32),
             sds((total, d), f32),
             sds((total, d), bf16),
             sds((seqs, length, d), bf16),
-            sds((16, d), f32),
             sds((quarter, d), bf16),
             sds((total, d), bf16),
             sds((total, d), bf16),
@@ -1014,6 +1125,10 @@
             sds((total, d), bf16),
         ],
         scratch_shapes=[
+            pltpu.VMEM((total, d), f32),
+            pltpu.VMEM((total, d), f32),
+            pltpu.VMEM((total, d), bf16),
+            pltpu.VMEM((seqs, length, d), bf16),
             pltpu.VMEM((2, d, 2 * d), bf16),
             pltpu.VMEM((2, 2, d, d), bf16),
             pltpu.VMEM((total, d), f32),
@@ -1025,6 +1140,8 @@
             pltpu.VMEM((2, quarter, d), bf16),
             pltpu.VMEM((quarter, d), bf16),
             pltpu.SemaphoreType.DMA((5,)),
+            pltpu.SemaphoreType.DMA((8, 2)),
+            pltpu.SemaphoreType.DMA((seqs, 3)),
             pltpu.SemaphoreType.DMA((2,)),
             pltpu.SemaphoreType.DMA((2,)),
             pltpu.SemaphoreType.DMA((10,)),
@@ -1037,7 +1154,7 @@
         ],
         compiler_params=params(61, collective_id=1, has_side_effects=True),
         cost_estimate=cost(2 * total * 16 * d * d, 60 * total * d),
-    )(counts, keep3, h2, em, r, vec, h2, em, w_up, w_down, own_down)
+    )(counts, keep3, h2, em, vec, h2, em, r, w_up, w_down, own_down)
 
     bits = []
     while (4 << len(bits)) < replicas:
@@ -1046,13 +1163,17 @@
     chunks, steps = len(sizes), 7 + len(bits)
     found = pl.pallas_call(
         functools.partial(tail_kernel, seqs, buf, tuple(bits), sizes),
-        in_specs=[SMEM_SPEC] + [VMEM_SPEC] * 7 + [ANY_SPEC] * 13,
+        in_specs=[SMEM_SPEC] + [VMEM_SPEC] * 4 + [ANY_SPEC] * 16,
         out_specs=[VMEM_SPEC, ANY_SPEC] + [ANY_SPEC] * (chunks + 4),
         out_shape=[sds((16, d), f32), sds((seqs, length, d), f32)]
         + [sds((2, quarter, wide), bf16) for wide in sizes]
         + [sds((total, d), bf16)] * 3
         + [sds((total, 3 * half), bf16)],
         scratch_shapes=[
+            pltpu.VMEM((total, 3 * d), bf16),
+            pltpu.VMEM((total, d), bf16),
+            pltpu.VMEM((total, d), f32),
+            pltpu.SemaphoreType.DMA((3,)),
             pltpu.VMEM((2, d, 3 * half), bf16),
             pltpu.VMEM((total, d), bf16),
             pltpu.VMEM((2, total, 3 * half), bf16),
@@ -1081,65 +1202,20 @@
         ],
         compiler_params=params(61, collective_id=2, has_side_effects=True),
         cost_estimate=cost(2 * total * 16 * d * d, 100 * total * d),
-    )(counts, keep3, qkv, x, er, vec, stats, sums_feed, part_sum, z_mine, z_got, em, em_got, h2, h2_got, u_mine, u_got, o, ea, h1, w_attn)
+    )(counts, keep3, vec, stats, sums_feed, qkv, x, er, part_sum, z_mine, z_got, em, em_got, h2, h2_got, u_mine, u_got, o, ea, h1, w_attn)
     small, input_grad = found[:2]
     grads = found[2 : 2 + chunks]
     branch_rms = jnp.sqrt(small[12, 0:3] / (small[12, 3] * d))
-    part = vectors.shape[1]
-    grad_vectors = lax.dynamic_slice(small, (0, group * part), (12, part))
-
-    new_down = None
-    for k in range(2):
-        new_down = adam_call(
-            (down, f_down, s_down),
-            grads[k],
-            (2, 2),
-            (quarter, half),
-            lambda h, j, k=k: (2 * h + k, j),
-            lambda h, j: (h, 0, j),
-            new_down,
-        )
-    new_mats = None
-    for t in range(2):
-        new_mats = adam_call(
-            (mats, f_mats, s_mats),
-            grads[2 + t],
-            (2, 4),
-            (quarter, quarter),
-            lambda h, j, t=t: (0, 16 + 4 * j + 2 * h + t),
-            lambda h, j: (h, 0, j),
-            new_mats,
-        )
-    for k, first_strip in ((4, 3), (5, 0), (6, 2)):
-        new_mats = adam_call(
-            (mats, f_mats, s_mats),
-            grads[k],
-            (2, sizes[k] // half),
-            (quarter, half),
-            lambda h, j, at=first_strip: (0, 2 * (at + j) + h),
-            lambda h, j: (h, 0, j),
-            new_mats,
-        )
-    new_vectors, first_vectors, second_vectors = adam_math(
-        vectors, f_vectors, s_vectors, grad_vectors, rate_vector, 0.0
+    new = adam_call(
+        group.astype(jnp.int32).reshape(1),
+        (mats, f_mats, s_mats),
+        (down, f_down, s_down),
+        (vectors, f_vectors, s_vectors),
+        small,
+        grads,
     )
-    return (
-        block_output,
-        input_grad,
-        new_mats[0],
-        new_down[0],
-        new_vectors,
-        new_mats[1],
-        new_down[1],
-        first_vectors,
-        new_mats[2],
-        new_down[2],
-        second_vectors,
-        new_mats[3],
-        new_down[3],
-        new_vectors.astype(bf16),
-        branch_rms,
-    )
+    by_kind = [new[4 * part + kind] for kind in range(4) for part in range(3)]
+    return (block_output, input_grad, *by_kind, branch_rms)
 
 
 def solution(mesh):

time: 356 us -> 328 us (0.921)
  Pallas kernels: 331 us -> 314 us
  local copies, waits for them, and re-layouts: 17.5 us -> 8.33 us
    unnamed x32 -> x6, local copies, waits for them, and re-layouts: 14.9 us -> 5.79 us
    pallas_call x1, Pallas kernels: 61.9 us -> 52.9 us  [local(): pl.pallas_call(functools.partial(feed_kernel, seqs, buf), in_specs=[SMEM_...]
    pallas_call x1, Pallas kernels: 87.9 us -> 83.8 us  [local(): pl.pallas_call(functools.partial(attend_kernel, seqs, buf), in_specs=[SME...]
    pallas_call x7 -> x1, Pallas kernels: 37.3 us -> 34 us  [adam_call(): pl.pallas_call(functools.partial(adam_kernel, columns), grid_spec=pltpu.P...]
where the time goes in v5:
time: 328 us; the launch traced here: 326 us
  Pallas kernels  314 us (96%)
  local copies, waits for them, and re-layouts  8.33 us (3%)
    pallas_call x1, Pallas kernels, local(): pl.pallas_call(functools.partial(tail_kernel, seqs, buf, tuple(bits), siz...  143 us
    pallas_call x1, Pallas kernels, local(): pl.pallas_call(functools.partial(attend_kernel, seqs, buf), in_specs=[SME...  83.8 us
    pallas_call x1, Pallas kernels, local(): pl.pallas_call(functools.partial(feed_kernel, seqs, buf), in_specs=[SMEM_...  52.9 us
    pallas_call x1, Pallas kernels, adam_call(): pl.pallas_call(functools.partial(adam_kernel, columns), grid_spec=pltpu.P...  34 us

profile of v5, /device:TPU:0, one launch (start us, length us, event | category | flops | bytes accessed | tf_op | source)
XLA Modules:
  0.0 325.9 jit_solution(10076056682647031322)
XLA Ops:
  0.6 0.8 reduce_sum.9
  1.5 0.5 broadcast_add_fusion.refs_0_
  2.0 1.3 reshape.41.refs_1_
  3.2 83.8 %shard_map.235 = (bf16[2,1024,2048]{2,1,0:T(8,128)(2,1)}, bf16[2,1024,2048]{2,1,0:T(8,128)(2,1)}, bf16[2,1024,1024]{2,1,0:T(8,128)(2,1)}, bf16[256,1024]{1,0:T(8...) custom-call(s32[4]{0:T(128)} %broadcast_add_fusion.refs_0_, ...), custom_call_target="tpu_custom_call" | custom-call | flops 19327352832 | bytes 11796480 | tf_op jit(solution)/shard_map/pallas_call | solution.py:1063
  87.0 52.9 %shard_map.236 = (f32[16,1024]{1,0:T(8,128)}, f32[576,1024]{1,0:T(8,128)}, bf16[576,1024]{1,0:T(8,128)(2,1)}, bf16[4,320,1024]{2,1,0:T(8,128)(2,1)}, bf16[256,10...) custom-call(s32[4]{0:T(128)} %broadcast_add_fusion.refs_0_, ...), custom_call_target="tpu_custom_call" | custom-call | flops 19327352832 | bytes 35389440 | tf_op jit(solution)/shard_map/pallas_call | solution.py:1110
  139.9 143.1 %shard_map.237 = (f32[16,1024]{1,0:T(8,128)}, f32[4,320,1024]{2,1,0:T(8,128)}, bf16[2,256,1024]{2,1,0:T(8,128)(2,1)}, bf16[2,256,1024]{2,1,0:T(8,128)(2,1)}, bf1...) custom-call(s32[4]{0:T(128)} %broadcast_add_fusion.refs_0_, ...), custom_call_target="tpu_custom_call" | custom-call | flops 19327352832 | bytes 58982400 | tf_op jit(solution)/shard_map/pallas_call | solution.py:1164
  283.0 0.0 copy-start.1
  283.0 34.0 %shard_map.238 = (f32[256,8192]{1,0:T(8,128)}, f32[256,8192]{1,0:T(8,128)}, f32[256,8192]{1,0:T(8,128)}, bf16[256,8192]{1,0:T(8,128)(2,1)}, f32[1024,1024]{1,0:T...) custom-call(s32[1]{0:T(128)} %bitcast.info, ...), custom_call_target="tpu_custom_call" | custom-call | flops 62914560 | bytes 88080384 | tf_op jit(solution)/shard_map/pallas_call | solution.py:1035
  317.0 1.3 slice.7
  318.9 1.2 sqrt_bitcast_fusion
  320.1 0.0 copy-done.1
  320.1 0.0 copy-start
  320.1 1.5 copy.29
  321.6 1.9 copy-done
  323.6 2.4 copy.30
Async XLA Ops:
  283.0 37.1 %copy-start.1 = (bf16[4,320,1024]{2,1,0:T(8,128)(2,1)S(1)}, bf16[4,320,1024]{2,1,0:T(8,128)(2,1)}, u32[]{:S(2)}) copy-start(bf16[4,320,1024]{2,1,0:T(8,128)(2,1)} %get-tuple-element.120) | copy-start | bytes 7864324
  320.1 3.4 %copy-start = (f32[4,320,1024]{2,1,0:T(8,128)S(1)}, f32[4,320,1024]{2,1,0:T(8,128)}, u32[]{:S(2)}) copy-start(f32[4,320,1024]{2,1,0:T(8,128)} %get-tuple-element.121) | copy-start | bytes 15728644

commit v6 on v5

--- a/solution.py
+++ b/solution.py
@@ -26,32 +26,26 @@
 f32 = jnp.float32
 BOTH = ("group", "dp")
 VMEM_SPEC = pl.BlockSpec(memory_space=pltpu.VMEM)
-SMEM_SPEC = pl.BlockSpec(memory_space=pltpu.SMEM)
 ANY_SPEC = pl.BlockSpec(memory_space=pl.ANY)
 MIB = 1 << 20
 GATHER = dict(attn=3.0, up=18.0, up_gap=10.0, down=38.0, two=2.0, third=4.0, near=4.5, four=6.0, five=8.0, loop=23.5, gap=0.9)
 FEED = (4, 6, 7, 9, 10, 15)
 TAIL = {
     0: ((0, 2), (1, -1), (1, 0)),
-    2: ((2, -1), (0, 3)),
-    6: ((1, 1), (2, 0)),
-    7: ((3, -1),),
-    8: ((1, 2),),
-    10: ((0, 4),),
-    13: ((4, -1), (2, 1)),
-    14: ((1, 3),),
-    15: ((3, 0),),
-    18: ((0, 5),),
-    20: ((2, 2),),
-    26: ((3, 1), (2, 3)),
-    32: ((4, 0), (1, 4)),
-    34: ((3, 2), (5, -1), (4, 1), (5, 0), (2, 4)),
-    36: ((4, 2),),
-    37: ((3, 3), (5, 1), (6, -1), (1, 5)),
-    38: ((4, 3),),
-    40: ((5, 2),),
-    41: ((3, 4),),
-    42: ((1, 6), (6, 0), (5, 3), (6, 1), (9, 10), (3, 5), (9, 11), (0, 6), (9, 12), (6, 2), (9, 13), (4, 4), (6, 3), (9, 14), (5, 4), (2, 5), (9, 15), (6, 4), (5, 5), (4, 5), (3, 6), (6, 5), (9, 16), (5, 6), (2, 6), (4, 6), (6, 6)),
+    2: ((2, -1),),
+    3: ((1, 1), (3, -1)),
+    4: ((3, 0),),
+    6: ((4, -1),),
+    7: ((2, 0),),
+    11: ((0, 3), (1, 2)),
+    21: ((3, 1),),
+    26: ((1, 3), (0, 4)),
+    30: ((2, 1),),
+    34: ((5, -1), (5, 0)),
+    35: ((3, 2),),
+    40: ((2, 2),),
+    41: ((3, 3), (5, 1), (1, 4)),
+    42: ((4, 0), (6, -1), (5, 2), (2, 3), (9, 10), (3, 4), (6, 0), (4, 1), (5, 3), (6, 1), (2, 4), (9, 11), (0, 5), (6, 2), (5, 4), (1, 5), (6, 3), (4, 2), (3, 5), (9, 12), (4, 3), (9, 13), (2, 5), (6, 4), (9, 14), (5, 5), (2, 6), (9, 15), (4, 4), (9, 16), (0, 6), (5, 6), (6, 5), (4, 5), (4, 6), (1, 6), (3, 6), (6, 6)),
 }
 
 
@@ -117,6 +111,7 @@
     def __init__(self):
         self.group, self.replica = lax.axis_index("group"), lax.axis_index("dp")
         self.core, self.level = self.replica % 2, (self.replica // 2) % 2
+        self.inner = (self.level + self.replica // 4) % 2
         one, two = flip(self.group, 1), flip(self.group, 2)
         self.first = (1 - self.core) * one + self.core * two
         self.second = (1 - self.core) * two + self.core * one
@@ -125,6 +120,10 @@
         self.to_second = (self.second, self.replica)
         self.to_third = (self.third, self.replica)
         self.to_core = (self.group, flip(self.replica, 1))
+
+    @property
+    def to_middle(self):
+        return (self.group, flip(flip(self.replica, 2), 4))
 
     def to_bit(self, bit):
         return (self.group, flip(self.replica, bit))
@@ -264,18 +263,18 @@
     return jnp.where(first, both[:rows], both[rows:])
 
 
-def pair_probs(q_pair, k_pair, count):
+def pair_probs(q_pair, k_pair, counts, n):
     raw = mm_nt(q_pair, k_pair) * (1.0 / math.sqrt(HEAD))
     col = lax.broadcasted_iota(jnp.int32, raw.shape, 1)
-    raw = jnp.where(col < count, raw, -1e30)
+    raw = jnp.where(col < counts[pl.ds(n, 1), :][:, 0 : raw.shape[1]], raw, -1e30)
     top = jnp.max(raw, axis=-1, keepdims=True)
     exponent = jnp.exp(raw - top)
     return exponent / jnp.sum(exponent, axis=-1, keepdims=True)
 
 
 def attend_kernel(seqs, buf, *refs):
-    counts, keep, vectors, mats, down, tokens, cot = refs[:7]
-    w_attn, w_up, w_down, own_down, x_out, em_out, h1_out, qkv_out, o_out, r_out, h2_out, vec, stats = refs[7:20]
+    keep, vectors, mats, down, tokens, cot = refs[:6]
+    w_attn, w_up, w_down, own_down, x_out, em_out, h1_out, qkv_out, o_out, r_out, h2_out, vec, stats, counts = refs[6:20]
     x, em, h1, qkv, o, r, h2, outs, wbuf, wide, tall, low_up, low_down, rows_in, parts, send, recv, vec_send, vec_recv, loads, stores, reads = refs[20:]
     rows = h1.shape[0] // seqs
     d = h1.shape[1]
@@ -349,6 +348,10 @@
         one.start()
         keeps.append(one)
 
+    kept = jnp.sum(keep[...], axis=1, keepdims=True) + buf
+    counts[0:seqs, :] = jnp.broadcast_to(kept, keep.shape)
+    counts[2 * seqs : 3 * seqs, :] = keep[...]
+
     for one in reads_in:
         one.wait()
     due_pack = line.during(seqs, 4.0, 1.0)
@@ -357,7 +360,7 @@
     def _(n):
         due_pack(n)
         at = pl.multiple_of(n * rows, 16)
-        pick = picker(keep[n], rows - buf)
+        pick = picker(counts[pl.ds(2 * seqs + n, 1), :], rows - buf)
         for k, dst in ((0, x), (1, em)):
             dst[pl.ds(at, buf), :] = rows_in[k, n, 0:buf, :]
             dst[pl.ds(pl.multiple_of(at + buf, 16), rows - buf), :] = mm(pick, rows_in[k, n, buf:, :]).astype(bf16)
@@ -410,7 +413,7 @@
         at = pl.ds(pl.multiple_of(n * rows, 16), rows)
         lanes = [pl.ds(pl.multiple_of(j * 2 * HEAD + m * d, 2 * HEAD), 2 * HEAD) for m in range(3)]
         q_pair = two_heads(qkv[at, lanes[0]], low, high)
-        probs = pair_probs(q_pair, qkv[at, lanes[1]], counts[n]).astype(bf16)
+        probs = pair_probs(q_pair, qkv[at, lanes[1]], counts, n).astype(bf16)
         o[at, lanes[0]] = pick_heads(mm(probs, qkv[at, lanes[2]]), first).astype(bf16)
 
     keep_attn = pltpu.make_async_copy(wbuf, w_attn, stores.at[4])
@@ -433,7 +436,7 @@
     def _(n):
         due_last(n)
         at = pl.ds(pl.multiple_of(n * rows, 16), rows)
-        valid = lax.broadcasted_iota(jnp.int32, (rows, 1), 0) < counts[n]
+        valid = lax.broadcasted_iota(jnp.int32, (rows, 1), 0) < counts[pl.ds(n, 1), :][:, 0:1]
         valid = jnp.where(valid, 1.0, 0.0)
         inputs = x[at, :].astype(f32)
         branch = r[at, :]
@@ -453,29 +456,25 @@
 
 
 class Reduce:
-    def __init__(self, place, bits, g, r1, r2, r3, r4, total, send, recv):
+    def __init__(self, place, bits, g, r1, r2, r3, r4, far, total, send, recv, home=None):
         self.place, self.bits, self.g, self.r1, self.r2, self.r3, self.r4 = place, bits, g, r1, r2, r3, r4
-        self.total, self.send, self.recv = total, send, recv
-        self.half = g.shape[1] // 2
-        self.hold = r2.at[pl.ds(0, self.half)]
-        self.slots = [r1.at[n // 2 % 2, pl.ds(n % 2 * self.half, self.half)] for n in range(len(bits))]
+        self.far, self.total, self.send, self.recv = far, total, send, recv
+        self.home = place.group if home is None else home
 
     def copy(self, k):
         p = self.place
-        half = self.half
-        mine, other = p.level * half, (1 - p.level) * half
-        at = lambda start: pl.ds(pl.multiple_of(start, 16), half)
         plans = [
             lambda: (self.g.at[p.third], self.r1.at[1], p.to_first),
             lambda: (self.g.at[p.first], self.r1.at[0], p.to_first),
             lambda: (self.g.at[p.second], self.r2, p.to_second),
-            lambda: (self.g.at[p.group, at(other)], self.r3, p.to_bit(2)),
-            lambda: (self.hold, self.total.at[p.core, at(mine)], p.to_bit(2)),
-            lambda: (self.hold, self.total.at[p.core, at(mine)], p.to_core),
-            lambda: (self.total.at[p.core, at(other)], self.total.at[p.core, at(other)], p.to_core),
+            lambda: (self.g.at[self.home], self.r3, p.to_bit(2)),
+            lambda: (self.r2, self.total.at[p.core], p.to_bit(2)),
+            lambda: (self.r2, self.total.at[p.core], p.to_core),
+            lambda: (self.total.at[p.core], self.total.at[p.core], p.to_core),
+            lambda: (self.r1.at[0], self.r4, p.to_middle),
         ]
         for n, bit in enumerate(self.bits):
-            plans.append(lambda n=n, bit=bit: (self.slots[n], self.r4.at[n], p.to_bit(bit)))
+            plans.append(lambda n=n, bit=bit: (self.far.at[n, 0], self.far.at[n, 1], p.to_bit(bit)))
         src, dst, device = plans[k]()
         return pltpu.make_async_remote_copy(
             src_ref=src, dst_ref=dst, send_sem=self.send.at[k], recv_sem=self.recv.at[k],
@@ -502,42 +501,55 @@
         at = self.place.group
         self.g[at] = (self.g[at].astype(f32) + self.r1[0].astype(f32) + self.r2[...].astype(f32)).astype(bf16)
 
-    def pass_replica(self):
-        self.settle()
-        self.copy(3).start()
-
-    def pass_bit(self, n):
-        p = self.place
-        if n == 0:
+    def pass_in(self):
+        pl.when(self.place.inner == 0)(self.copy(3).start)
+
+    def pass_middle(self):
+        @pl.when(self.place.inner == 1)
+        def _():
             self.copy(3).wait_recv()
-            at = pl.ds(pl.multiple_of(p.level * self.half, 16), self.half)
-            value = self.g[p.group, at].astype(f32) + self.r3[...].astype(f32)
-        else:
-            self.copy(6 + n).wait_recv()
-            value = self.slots[n - 1][...].astype(f32) + self.r4[n - 1].astype(f32)
-        if n < len(self.bits):
-            self.slots[n][...] = value.astype(bf16)
-            self.copy(7 + n).start()
-        else:
-            self.hold[...] = value.astype(bf16)
+            value = self.g[self.home].astype(f32) + self.r3[...].astype(f32)
+            self.r1[0] = value.astype(bf16)
+            self.copy(7).start()
+
+    def pass_out(self):
+        @pl.when(self.place.inner == 1)
+        def _():
+            self.copy(7).wait_recv()
+            self.r2[...] = (self.r1[0].astype(f32) + self.r4[...].astype(f32)).astype(bf16)
+            for n in range(len(self.bits)):
+                pltpu.sync_copy(self.r2, self.far.at[n, 0])
+                self.copy(8 + n).start()
+                self.copy(8 + n).wait()
+                pltpu.sync_copy(self.far.at[n, 1], self.r3)
+                self.r2[...] = (self.r2[...].astype(f32) + self.r3[...].astype(f32)).astype(bf16)
             self.copy(4).start()
             self.copy(5).start()
             self.stay().start()
 
     def stay(self):
-        p = self.place
-        at = pl.ds(pl.multiple_of(p.level * self.half, 16), self.half)
-        return pltpu.make_async_copy(self.hold, self.total.at[p.core, at], self.send.at[7 + len(self.bits)])
+        return pltpu.make_async_copy(self.r2, self.total.at[self.place.core], self.send.at[8 + len(self.bits)])
 
     def pass_core(self):
-        self.copy(4).wait_recv()
-        self.copy(6).start()
-
-    def finish(self, start=0):
-        self.copy(5).wait_recv()
-        self.copy(6).wait_recv()
-        self.sent(*range(start, 7 + len(self.bits)))
-        self.stay().wait()
+        @pl.when(self.place.inner == 0)
+        def _():
+            self.copy(4).wait_recv()
+            self.copy(6).start()
+
+    def finish(self, whole=True):
+        if whole:
+            self.sent(0, 1, 2)
+
+        @pl.when(self.place.inner == 1)
+        def _():
+            self.copy(5).wait_recv()
+            self.sent(4, 5, 7)
+            self.stay().wait()
+
+        @pl.when(self.place.inner == 0)
+        def _():
+            self.copy(6).wait_recv()
+            self.sent(3, 6)
 
 
 def block_grads(place, sides, wide, g):
@@ -562,10 +574,10 @@
 
 
 def feed_kernel(seqs, buf, *refs):
-    counts, keep, h2, em, vec, h2_hbm, em_hbm, r_hbm, ups, downs, own_down = refs[:11]
-    sums, er_hbm, ea_hbm, out_hbm, part_sum, z_mine, z_got, u_mine, u_got, h2_got, em_got = refs[11:22]
-    r, er, ea, out, wup, wdown, m_acc, t_acc, z_all, u_all, sides, g, r1, r2 = refs[22:36]
-    sems, w_sems, o_sems, send, recv, g_send, g_recv, k_sems, t_send, t_recv, r_send, r_recv = refs[36:]
+    counts, h2, em, vec, h2_hbm, em_hbm, r_hbm, ups, downs, own_down = refs[:10]
+    sums, er_hbm, ea_hbm, out_hbm, part_sum, z_mine, z_got, u_mine, u_got, h2_got, em_got = refs[10:21]
+    r, er, ea, out, wup, wdown, m_acc, t_acc, z_all, u_all, sides, g, r1, r2 = refs[21:35]
+    sems, w_sems, o_sems, send, recv, g_send, g_recv, k_sems, t_send, t_recv, r_send, r_recv = refs[35:]
     total, d = h2.shape
     rows = total // seqs
     strip = wup.shape[2] // 4
@@ -604,7 +616,7 @@
         swap_start(place, em_hbm, em_got, send, recv, 0),
         swap_start(place, h2_hbm, h2_got, send, recv, 1),
     ]
-    reduce = Reduce(place, (), g, r1, r2, None, None, None, r_send, r_recv)
+    reduce = Reduce(place, (), g, r1, r2, None, None, None, None, r_send, r_recv)
     sides[1, 0:total, :] = em[...]
     take_em = pltpu.make_async_copy(em_got, sides.at[1, pl.ds(total, total)], sems.at[4])
     sums[...] = jnp.zeros_like(sums)
@@ -695,13 +707,13 @@
     @pl.loop(0, seqs)
     def _(n):
         at = pl.ds(pl.multiple_of(n * rows, 16), rows)
-        valid = lax.broadcasted_iota(jnp.int32, (rows, 1), 0) < counts[n]
+        valid = lax.broadcasted_iota(jnp.int32, (rows, 1), 0) < counts[pl.ds(n, 1), :][:, 0:1]
         valid = jnp.where(valid, 1.0, 0.0)
         resid = r[at, :]
         m = m_acc[at, :] + vec[7:8, :]
         packed = ((resid + m) * valid).astype(bf16)
         out[n, 0:buf, :] = packed[0:buf]
-        pick = picker(keep[n], rows - buf)
+        pick = picker(counts[pl.ds(2 * seqs + n, 1), :], rows - buf)
         out[n, buf:, :] = mm_tn(pick, packed[buf:]).astype(bf16)
         normal, inverse = layer_stats(resid)
         t = t_acc[at, :]
@@ -733,15 +745,17 @@
 
 
 def tail_kernel(seqs, buf, bits, sizes, *refs):
-    counts, keep, vec, stats, sums_feed, qkv_hbm, x_hbm, er_hbm = refs[:8]
-    part_sum, z_mine, z_got, em, em_got, h2, h2_got, u_mine, u_got, o, ea, h1, w_attn = refs[8:21]
+    counts, vec, stats, sums_feed, qkv_hbm, x_hbm, er_hbm = refs[:7]
+    part_sum, z_mine, z_got, em, em_got, h2, h2_got, u_mine, u_got, o, ea, h1, w_attn = refs[7:20]
     chunks = len(sizes)
-    small, out = refs[21:23]
-    totals = refs[23 : 23 + chunks]
-    o_got, ea_got, h1_got, e_got = refs[23 + chunks : 27 + chunks]
-    scratch = refs[27 + chunks :]
-    qkv, x, er, in_sems = scratch[:4]
-    scratch = scratch[4:]
+    small, out = refs[20:22]
+    totals = refs[22 : 22 + chunks]
+    o_got, ea_got, h1_got, e_got = refs[22 + chunks : 26 + chunks]
+    outs = 26 + chunks + (chunks if bits else 0)
+    far = refs[26 + chunks : outs] or [None] * chunks
+    scratch = refs[outs:]
+    qkv, er, in_sems = scratch[:3]
+    scratch = scratch[3:]
     wbuf, eo, e, t_acc, stage, sides, small_in = scratch[:7]
     buffers = [scratch[7 + k * chunks : 7 + (k + 1) * chunks] for k in range(5)]
     send, recv, w_sem, ea_sem, first_sem, side_sems, stage_sem, swap_send, swap_recv, small_send, small_recv = scratch[7 + 5 * chunks :]
@@ -783,11 +797,12 @@
     load_sides(2)
     inputs = [
         pltpu.make_async_copy(src, dst, in_sems.at[k])
-        for k, (src, dst) in enumerate(((qkv_hbm, qkv), (x_hbm, x), (er_hbm, er)))
+        for k, (src, dst) in enumerate(((qkv_hbm, qkv), (er_hbm, er)))
     ]
     for one in inputs:
         one.start()
-    partners = [place.to_first, place.to_second, place.to_core, place.to_bit(2)] + [place.to_bit(b) for b in bits]
+    partners = [place.to_first, place.to_second, place.to_core, place.to_bit(2), place.to_bit(4), place.to_middle]
+    partners += [place.to_bit(b) for b in bits]
     place.meet(partners)
     swaps = [
         swap_start(place, o, o_got, swap_send, swap_recv, 0),
@@ -799,10 +814,10 @@
         device_id=place.to_core, device_id_type=MESH,
     )
     reduces = [
-        Reduce(place, bits, *(buffers[b][k] for b in range(5)), totals[k], send.at[k], recv.at[k]) for k in range(chunks)
+        Reduce(place, bits, *(buffers[b][k] for b in range(5)), far[k], totals[k], send.at[k], recv.at[k], None if k else 0) for k in range(chunks)
     ]
 
-    first_sum = pltpu.make_async_copy(part_sum, buffers[0][0].at[place.group], first_sem)
+    first_sum = pltpu.make_async_copy(part_sum, buffers[0][0].at[0], first_sem)
     first_sum.start()
 
     def gradient(k):
@@ -829,20 +844,20 @@
             one.begin()
         elif step == 1:
             one.pass_second()
-        elif step == 2 and k == 0:
-            first_sum.wait()
-            one.copy(3).start()
         elif step == 2:
-            one.pass_replica()
+            if k == 0:
+                first_sum.wait()
+            else:
+                one.settle()
+            one.pass_in()
         elif step == 3:
-            one.pass_bit(0)
+            one.pass_middle()
         elif step == 4:
-            for n in range(1, len(bits) + 1):
-                one.pass_bit(n)
+            one.pass_out()
         elif step == 5:
             one.pass_core()
         else:
-            one.finish(0 if k else 3)
+            one.finish(k > 0)
 
     def due(slot, turn=None, count=1):
         for n in range(count):
@@ -890,7 +905,7 @@
         lanes = [pl.ds(pl.multiple_of(far + m * d, 2 * HEAD), 2 * HEAD) for m in range(3)]
         k_pair = qkv[at, lanes[1]]
         q_both = two_heads(qkv[at, lanes[0]], low, high)
-        probs = pair_probs(q_both, k_pair, counts[n])
+        probs = pair_probs(q_both, k_pair, counts, n)
         eo_both = two_heads(eo[at, lanes[0]], low, high)
         ep = mm_nt(eo_both, qkv[at, lanes[2]])
         inner = jnp.sum(probs * ep, axis=-1, keepdims=True)
@@ -904,11 +919,15 @@
         small[3:4, lanes[0]] += jnp.sum(ev.astype(f32), axis=0, keepdims=True)
 
     due(1 + planned)
+    take_x = pltpu.make_async_copy(x_hbm, eo, in_sems.at[2])
+    take_x.start()
+    x = eo
     sent_e.wait()
     swaps[2].wait()
     load_sides(5)
     load_sides(6)
     in_weight.wait()
+    take_x.wait()
     @pl.loop(0, 4)
     def _(s):
         due(2 + planned, s, 4)
@@ -931,7 +950,7 @@
             write.wait()
 
         stage[0:buf, :] = grad[0:buf]
-        pick = picker(keep[n], rows - buf)
+        pick = picker(counts[pl.ds(2 * seqs + n, 1), :], rows - buf)
         rest = grad[buf:]
         top = rest.astype(bf16)
         rest = rest - top.astype(f32)
@@ -943,15 +962,13 @@
     pltpu.make_async_copy(stage, out.at[0], stage_sem).wait()
 
     small[4:12, :] = sums_feed[4:12, :]
-    kept = counts[0]
-    for n in range(1, seqs):
-        kept = kept + counts[n]
+    kept = jnp.sum(counts[0:seqs, 0:1], axis=0, keepdims=True)
     lane = lax.broadcasted_iota(jnp.int32, (1, d), 1)
     tally = jnp.where(lane == 3, kept.astype(f32), 0.0)
     for k, row in enumerate((stats[0:1, :], stats[1:2, :], sums_feed[12:13, :])):
         tally = tally + jnp.where(lane == k, jnp.sum(row, axis=1, keepdims=True), 0.0)
     small[12:13, :] = tally
-    hops = [place.to_first, place.to_second] + [place.to_bit(b) for b in (1, 2, *bits)]
+    hops = [place.to_first, place.to_second] + [place.to_bit(b) for b in (1, 2, 4, *bits)]
     small_in[0, 0] = small[...]
 
     def hop(k):
@@ -1056,14 +1073,12 @@
     total = seqs * rows
     half = d // 2
     group = lax.axis_index("group")
-    counts = (buf + jnp.sum(keep, axis=1)).astype(jnp.int32)
-
-    keep3 = keep.reshape(seqs, 1, image)
+
     deep = mats.shape[0]
-    w_attn, w_up, w_down, own_down, x, em, h1, qkv, o, r, h2, vec, stats = pl.pallas_call(
+    w_attn, w_up, w_down, own_down, x, em, h1, qkv, o, r, h2, vec, stats, counts = pl.pallas_call(
         functools.partial(attend_kernel, seqs, buf),
-        in_specs=[SMEM_SPEC] + [VMEM_SPEC] * 2 + [ANY_SPEC] * 4,
-        out_specs=[ANY_SPEC] * 11 + [VMEM_SPEC] * 2,
+        in_specs=[VMEM_SPEC] * 2 + [ANY_SPEC] * 4,
+        out_specs=[ANY_SPEC] * 11 + [VMEM_SPEC] * 3,
         out_shape=[
             sds((2, d, 2 * d), bf16),
             sds((2, d, 2 * d), bf16),
@@ -1078,6 +1093,7 @@
             sds((total, d), bf16),
             sds((16, d), f32),
             sds((8, d), f32),
+            sds((4 * seqs, image), jnp.int32),
         ],
         scratch_shapes=[
             pltpu.VMEM((total, d), bf16),
@@ -1105,11 +1121,11 @@
         ],
         compiler_params=params(60, collective_id=0, has_side_effects=True),
         cost_estimate=cost(2 * total * 4 * d * d * 4, 20 * total * d),
-    )(counts, keep3, vectors, mats, down, tokens, cot)
+    )(keep, vectors, mats, down, tokens, cot)
     quarter = d // 4
     sums_feed, er, ea, block_output, part_sum, z_mine, z_got, u_mine, u_got, h2_got, em_got = pl.pallas_call(
         functools.partial(feed_kernel, seqs, buf),
-        in_specs=[SMEM_SPEC] + [VMEM_SPEC] * 4 + [ANY_SPEC] * 6,
+        in_specs=[VMEM_SPEC] * 4 + [ANY_SPEC] * 6,
         out_specs=[VMEM_SPEC] + [ANY_SPEC] * 10,
         out_shape=[
             sds((16, d), f32),
@@ -1154,24 +1170,24 @@
         ],
         compiler_params=params(61, collective_id=1, has_side_effects=True),
         cost_estimate=cost(2 * total * 16 * d * d, 60 * total * d),
-    )(counts, keep3, h2, em, vec, h2, em, r, w_up, w_down, own_down)
+    )(counts, h2, em, vec, h2, em, r, w_up, w_down, own_down)
 
     bits = []
-    while (4 << len(bits)) < replicas:
-        bits.append(4 << len(bits))
+    while (8 << len(bits)) < replicas:
+        bits.append(8 << len(bits))
     sizes = (d, d, d, d, half, d, half)
-    chunks, steps = len(sizes), 7 + len(bits)
+    chunks, steps = len(sizes), 8 + len(bits)
     found = pl.pallas_call(
         functools.partial(tail_kernel, seqs, buf, tuple(bits), sizes),
-        in_specs=[SMEM_SPEC] + [VMEM_SPEC] * 4 + [ANY_SPEC] * 16,
-        out_specs=[VMEM_SPEC, ANY_SPEC] + [ANY_SPEC] * (chunks + 4),
+        in_specs=[VMEM_SPEC] * 4 + [ANY_SPEC] * 16,
+        out_specs=[VMEM_SPEC, ANY_SPEC] + [ANY_SPEC] * (chunks + 4 + (chunks if bits else 0)),
         out_shape=[sds((16, d), f32), sds((seqs, length, d), f32)]
         + [sds((2, quarter, wide), bf16) for wide in sizes]
         + [sds((total, d), bf16)] * 3
-        + [sds((total, 3 * half), bf16)],
+        + [sds((total, 3 * half), bf16)]
+        + [sds((len(bits), 2, quarter, wide), bf16) for wide in sizes if bits],
         scratch_shapes=[
             pltpu.VMEM((total, 3 * d), bf16),
-            pltpu.VMEM((total, d), bf16),
             pltpu.VMEM((total, d), f32),
             pltpu.SemaphoreType.DMA((3,)),
             pltpu.VMEM((2, d, 3 * half), bf16),
@@ -1180,13 +1196,12 @@
             pltpu.VMEM((total, d), f32),
             pltpu.VMEM((length, d), f32),
             pltpu.VMEM((2, 2, 2 * total, d), bf16),
-            pltpu.VMEM((4 + len(bits), 2, 16, d), f32),
+            pltpu.VMEM((5 + len(bits), 2, 16, d), f32),
         ]
-        + [pltpu.VMEM((4, quarter, wide), bf16) for wide in sizes]
-        + [pltpu.VMEM((2, quarter, wide), bf16) for wide in sizes]
+        + [pltpu.VMEM((4 if k else 1, quarter, wide), bf16) for k, wide in enumerate(sizes)]
+        + [pltpu.VMEM((2 if k else 1, quarter, wide), bf16) for k, wide in enumerate(sizes)]
         + [pltpu.VMEM((quarter, wide), bf16) for wide in sizes]
-        + [pltpu.VMEM((quarter // 2, wide), bf16) for wide in sizes]
-        + [pltpu.VMEM((len(bits), quarter // 2, wide), bf16) for wide in sizes]
+        + [pltpu.VMEM((quarter, wide), bf16) for wide in sizes] * 2
         + [
             pltpu.SemaphoreType.DMA((chunks, steps + 1)),
             pltpu.SemaphoreType.DMA((chunks, steps)),
@@ -1197,12 +1212,12 @@
             pltpu.SemaphoreType.DMA(()),
             pltpu.SemaphoreType.DMA((4,)),
             pltpu.SemaphoreType.DMA((4,)),
-            pltpu.SemaphoreType.DMA((4 + len(bits),)),
-            pltpu.SemaphoreType.DMA((4 + len(bits),)),
+            pltpu.SemaphoreType.DMA((5 + len(bits),)),
+            pltpu.SemaphoreType.DMA((5 + len(bits),)),
         ],
         compiler_params=params(61, collective_id=2, has_side_effects=True),
         cost_estimate=cost(2 * total * 16 * d * d, 100 * total * d),
-    )(counts, keep3, vec, stats, sums_feed, qkv, x, er, part_sum, z_mine, z_got, em, em_got, h2, h2_got, u_mine, u_got, o, ea, h1, w_attn)
+    )(counts, vec, stats, sums_feed, qkv, x, er, part_sum, z_mine, z_got, em, em_got, h2, h2_got, u_mine, u_got, o, ea, h1, w_attn)
     small, input_grad = found[:2]
     grads = found[2 : 2 + chunks]
     branch_rms = jnp.sqrt(small[12, 0:3] / (small[12, 3] * d))

time: 328 us -> 318 us (0.970)
  Pallas kernels: 314 us -> 308 us
    pallas_call x1, Pallas kernels: 143 us -> 137 us  [local(): pl.pallas_call(functools.partial(tail_kernel, seqs, buf, tuple(bits), siz...]
where the time goes in v6:
time: 318 us
  Pallas kernels  308 us (97%)
  local copies, waits for them, and re-layouts  7.06 us (2%)
    pallas_call x1, Pallas kernels, local(): pl.pallas_call(functools.partial(tail_kernel, seqs, buf, tuple(bits), siz...  137 us
    pallas_call x1, Pallas kernels, local(): pl.pallas_call(functools.partial(attend_kernel, seqs, buf), in_specs=[VME...  83.8 us
    pallas_call x1, Pallas kernels, local(): pl.pallas_call(functools.partial(feed_kernel, seqs, buf), in_specs=[VMEM_...  52.7 us
    pallas_call x1, Pallas kernels, adam_call(): pl.pallas_call(functools.partial(adam_kernel, columns), grid_spec=pltpu.P...  34 us

profile of v6, /device:TPU:0, one launch (start us, length us, event | category | flops | bytes accessed | tf_op | source)
XLA Modules:
  0.0 317.6 jit_solution(2685903475370645531)
XLA Ops:
  0.6 83.8 %shard_map.235 = (bf16[2,1024,2048]{2,1,0:T(8,128)(2,1)}, bf16[2,1024,2048]{2,1,0:T(8,128)(2,1)}, bf16[2,1024,1024]{2,1,0:T(8,128)(2,1)}, bf16[256,1024]{1,0:T(8...) custom-call(s32[4,256]{1,0:T(4,128)} %refs_0_.2, ...), custom_call_target="tpu_custom_call" | custom-call | flops 19327352832 | bytes 11796480 | tf_op jit(solution)/shard_map/pallas_call | solution.py:1078
  84.5 52.7 %shard_map.236 = (f32[16,1024]{1,0:T(8,128)}, f32[576,1024]{1,0:T(8,128)}, bf16[576,1024]{1,0:T(8,128)(2,1)}, bf16[4,320,1024]{2,1,0:T(8,128)(2,1)}, bf16[256,10...) custom-call(s32[16,256]{1,0:T(8,128)} %get-tuple-element.61.refs_0_,, ...), custom_call_target="tpu_custom_call" | custom-call | flops 19327352832 | bytes 35389440 | tf_op jit(solution)/shard_map/pallas_call | solution.py:1126
  137.2 137.5 %shard_map.237 = (f32[16,1024]{1,0:T(8,128)}, f32[4,320,1024]{2,1,0:T(8,128)}, bf16[2,256,1024]{2,1,0:T(8,128)(2,1)}, bf16[2,256,1024]{2,1,0:T(8,128)(2,1)}, bf1...) custom-call(s32[16,256]{1,0:T(8,128)} %get-tuple-element.61.refs_0_,, ...), custom_call_target="tpu_custom_call" | custom-call | flops 19327352832 | bytes 58982400 | tf_op jit(solution)/shard_map/pallas_call | solution.py:1180
  274.7 0.0 copy-start.1
  274.7 34.0 %shard_map.238 = (f32[256,8192]{1,0:T(8,128)}, f32[256,8192]{1,0:T(8,128)}, f32[256,8192]{1,0:T(8,128)}, bf16[256,8192]{1,0:T(8,128)(2,1)}, f32[1024,1024]{1,0:T...) custom-call(s32[1]{0:T(128)} %bitcast.info, ...), custom_call_target="tpu_custom_call" | custom-call | flops 62914560 | bytes 88080384 | tf_op jit(solution)/shard_map/pallas_call | solution.py:1052
  308.7 1.3 slice.7
  310.6 1.2 sqrt_bitcast_fusion
  311.8 0.0 copy-done.1
  311.8 0.0 copy-start
  311.8 1.5 copy.29
  313.3 1.9 copy-done
  315.2 2.4 copy.30
Async XLA Ops:
  274.7 37.1 %copy-start.1 = (bf16[4,320,1024]{2,1,0:T(8,128)(2,1)S(1)}, bf16[4,320,1024]{2,1,0:T(8,128)(2,1)}, u32[]{:S(2)}) copy-start(bf16[4,320,1024]{2,1,0:T(8,128)(2,1)} %get-tuple-element.122) | copy-start | bytes 7864324
  311.8 3.4 %copy-start = (f32[4,320,1024]{2,1,0:T(8,128)S(1)}, f32[4,320,1024]{2,1,0:T(8,128)}, u32[]{:S(2)}) copy-start(f32[4,320,1024]{2,1,0:T(8,128)} %get-tuple-element.123) | copy-start | bytes 15728644

commit v7 on v6

--- a/solution.py
+++ b/solution.py
@@ -29,7 +29,7 @@
 ANY_SPEC = pl.BlockSpec(memory_space=pl.ANY)
 MIB = 1 << 20
 GATHER = dict(attn=3.0, up=18.0, up_gap=10.0, down=38.0, two=2.0, third=4.0, near=4.5, four=6.0, five=8.0, loop=23.5, gap=0.9)
-FEED = (4, 6, 7, 9, 10, 15)
+FEED = (6, 8, 9, 10, 11, 15)
 TAIL = {
     0: ((0, 2), (1, -1), (1, 0)),
     2: ((2, -1),),
@@ -657,42 +657,42 @@
 
     due = [(2, swaps[0].wait), (7, late_own), (8, begin)]
     due += zip(FEED, (late.step_two, late.step_third, late.step_near, late.step_four, late_last, reduce.pass_second))
-    orders = [[(when - 8 * t, step) for when, step in due if when // 8 == t] for t in range(2)]
+    orders = [[(when // 2 - 4 * t, step) for when, step in due if when // 8 == t] for t in range(2)]
 
     for t in range(2):
 
-        @pl.loop(0, 8)
-        def _(i):
+        @pl.loop(0, 4)
+        def _(turn):
             for when, step in orders[t]:
-                pl.when(i == when)(step)
+                pl.when(turn == when)(step)
             if t == 0:
-                pl.when(i == 2)(take_em.start)
-                for one in takes(i):
-                    one.wait()
-            turn, away = i // 2, i % 2
-            h = (1 - core) * away + core * (1 - away)
+                pl.when(turn == 1)(take_em.start)
+                for away in range(2):
+                    for one in takes(2 * turn + away):
+                        one.wait()
             s = owner_at(turn)
             cols = pl.ds(pl.multiple_of(s * strip + t * tile, tile), tile)
-            far = (pl.ds(8 + s, 1), pl.ds(pl.multiple_of(h * strip + t * tile, tile), tile))
             near = pl.ds(pl.multiple_of(s * tile, tile), tile)
-            w_up = wup[h, :, cols]
-            w_down = wdown[t, h, near, :]
-            u = mm(h2[...], w_up) + vec[far]
-            phi = 0.5 * (1.0 + lax.erf(u * root_half))
-            z = (u * phi).astype(bf16)
-            z_all[h, t, :, near] = z
-            slope = phi + u * jnp.exp(-0.5 * u * u) * inverse_root_two_pi
-            eu = (mm_nt(em[...], w_down) * slope).astype(bf16)
-            u_all[h, t, :, near] = eu
-            m_acc[...] += mm(z, w_down)
-            t_acc[...] += mm_nt(eu, w_up)
-            sums[far] = jnp.sum(eu.astype(f32), axis=0, keepdims=True)
-            for side in range(2):
-
-                @pl.when(away == side)
-                def _():
-                    for one in tile_copies(4 * t + turn, s, t, side == 1):
-                        one.start()
+            parts = []
+            for away in range(2):
+                h = (1 - core) * away + core * (1 - away)
+                far = (pl.ds(8 + s, 1), pl.ds(pl.multiple_of(h * strip + t * tile, tile), tile))
+                w_up = wup[h, :, cols]
+                w_down = wdown[t, h, near, :]
+                u = mm(h2[...], w_up) + vec[far]
+                phi = 0.5 * (1.0 + lax.erf(u * root_half))
+                z = (u * phi).astype(bf16)
+                z_all[h, t, :, near] = z
+                slope = phi + u * jnp.exp(-0.5 * u * u) * inverse_root_two_pi
+                eu = (mm_nt(em[...], w_down) * slope).astype(bf16)
+                u_all[h, t, :, near] = eu
+                sums[far] = jnp.sum(eu.astype(f32), axis=0, keepdims=True)
+                for one in tile_copies(4 * t + turn, s, t, away == 1):
+                    one.start()
+                parts.append((z, eu, w_up, w_down))
+            z_pair, u_pair = (jnp.concatenate([part[k] for part in parts], axis=1) for k in range(2))
+            m_acc[...] += mm(z_pair, jnp.concatenate([part[3] for part in parts], axis=0))
+            t_acc[...] += mm_nt(u_pair, jnp.concatenate([part[2] for part in parts], axis=1))
 
     take_r.wait()
 

time: 318 us -> 311 us (0.978)
  Pallas kernels: 308 us -> 301 us
    pallas_call x1, Pallas kernels: 52.7 us -> 46.5 us  [local(): pl.pallas_call(functools.partial(feed_kernel, seqs, buf), in_specs=[VMEM_...]
where the time goes in v7:
time: 311 us; the launch traced here: 310 us
  Pallas kernels  301 us (97%)
  local copies, waits for them, and re-layouts  7.06 us (2%)
    pallas_call x1, Pallas kernels, local(): pl.pallas_call(functools.partial(tail_kernel, seqs, buf, tuple(bits), siz...  137 us
    pallas_call x1, Pallas kernels, local(): pl.pallas_call(functools.partial(attend_kernel, seqs, buf), in_specs=[VME...  83.8 us
    pallas_call x1, Pallas kernels, local(): pl.pallas_call(functools.partial(feed_kernel, seqs, buf), in_specs=[VMEM_...  46.5 us
    pallas_call x1, Pallas kernels, adam_call(): pl.pallas_call(functools.partial(adam_kernel, columns), grid_spec=pltpu.P...  34 us

profile of v7, /device:TPU:0, one launch (start us, length us, event | category | flops | bytes accessed | tf_op | source)
XLA Modules:
  0.0 310.5 jit_solution(7474353959599014093)
XLA Ops:
  0.6 83.8 %shard_map.235 = (bf16[2,1024,2048]{2,1,0:T(8,128)(2,1)}, bf16[2,1024,2048]{2,1,0:T(8,128)(2,1)}, bf16[2,1024,1024]{2,1,0:T(8,128)(2,1)}, bf16[256,1024]{1,0:T(8...) custom-call(s32[4,256]{1,0:T(4,128)} %refs_0_.2, ...), custom_call_target="tpu_custom_call" | custom-call | flops 19327352832 | bytes 11796480 | tf_op jit(solution)/shard_map/pallas_call | solution.py:1078
  84.5 46.5 %shard_map.236 = (f32[16,1024]{1,0:T(8,128)}, f32[576,1024]{1,0:T(8,128)}, bf16[576,1024]{1,0:T(8,128)(2,1)}, bf16[4,320,1024]{2,1,0:T(8,128)(2,1)}, bf16[256,10...) custom-call(s32[16,256]{1,0:T(8,128)} %get-tuple-element.61.refs_0_,, ...), custom_call_target="tpu_custom_call" | custom-call | flops 19327352832 | bytes 35389440 | tf_op jit(solution)/shard_map/pallas_call | solution.py:1126
  130.9 136.7 %shard_map.237 = (f32[16,1024]{1,0:T(8,128)}, f32[4,320,1024]{2,1,0:T(8,128)}, bf16[2,256,1024]{2,1,0:T(8,128)(2,1)}, bf16[2,256,1024]{2,1,0:T(8,128)(2,1)}, bf1...) custom-call(s32[16,256]{1,0:T(8,128)} %get-tuple-element.61.refs_0_,, ...), custom_call_target="tpu_custom_call" | custom-call | flops 19327352832 | bytes 58982400 | tf_op jit(solution)/shard_map/pallas_call | solution.py:1180
  267.6 0.0 copy-start.1
  267.6 34.0 %shard_map.238 = (f32[256,8192]{1,0:T(8,128)}, f32[256,8192]{1,0:T(8,128)}, f32[256,8192]{1,0:T(8,128)}, bf16[256,8192]{1,0:T(8,128)(2,1)}, f32[1024,1024]{1,0:T...) custom-call(s32[1]{0:T(128)} %bitcast.info, ...), custom_call_target="tpu_custom_call" | custom-call | flops 62914560 | bytes 88080384 | tf_op jit(solution)/shard_map/pallas_call | solution.py:1052
  301.6 1.3 slice.7
  303.5 1.2 sqrt_bitcast_fusion
  304.7 0.0 copy-done.1
  304.7 0.0 copy-start
  304.7 1.5 copy.29
  306.2 1.9 copy-done
  308.1 2.4 copy.30
Async XLA Ops:
  267.6 37.1 %copy-start.1 = (bf16[4,320,1024]{2,1,0:T(8,128)(2,1)S(1)}, bf16[4,320,1024]{2,1,0:T(8,128)(2,1)}, u32[]{:S(2)}) copy-start(bf16[4,320,1024]{2,1,0:T(8,128)(2,1)} %get-tuple-element.122) | copy-start | bytes 7864324
  304.7 3.4 %copy-start = (f32[4,320,1024]{2,1,0:T(8,128)S(1)}, f32[4,320,1024]{2,1,0:T(8,128)}, u32[]{:S(2)}) copy-start(f32[4,320,1024]{2,1,0:T(8,128)} %get-tuple-element.123) | copy-start | bytes 15728644
